TPU v7x, 32 devices: a whole 2x2x4 slice. The times are simulated.
32 devices in a mesh: groups: 2 (over y), seq: 8 (over z, x), vocab: 2 (over core).
Axes of the slice: x: 2, y: 2, z: 4, core: 2. Of those that a mesh axis runs over, the one named last changes fastest.
Arguments:
- ssm_input: bfloat16 [128, 2560], P(('groups', 'seq'), 'vocab'), parts along dimension 0, may hold values from -6 to 6
- gate_input: bfloat16 [128, 2560], P(('groups', 'seq'), 'vocab'), parts along dimension 0, may hold values from -6 to 6
- b_proj: bfloat16 [128, 128], P(('groups', 'seq')), parts along dimension 0, may hold values from -1.796875 to 1.796875
- readout_matrix: bfloat16 [128, 128], P(('groups', 'seq')), parts along dimension 0, may hold values from -1.796875 to 1.796875
- step_raw: float32 [128, 40], P(('groups', 'seq'), 'vocab'), parts along dimension 0, may hold values from -3 to 7
- step_bias: float32 [40], P('vocab'), may hold values from -1 to 1
- decay_log: float32 [40], P('vocab'), may hold values from -9 to -2
- head_skip_gain: float32 [40], P('vocab'), may hold values from 0.5 to 1.5
- norm_gain: float32 [2560], P('vocab'), may hold values from 0.1 to 1.9
- out_weight: bfloat16 [2560, 2560], P('vocab', 'seq'), may hold values from -0.125 to 0.125
- residual: bfloat16 [128, 2560], P('groups', 'seq'), parts along dimension 0, may hold values from -6 to 6
- final_gain: float32 [2560], replicated, may hold values from 0.1 to 1.9
- head_weight: bfloat16 [2560, 3136], P(None, ('seq', 'vocab')), may hold values from -12.253826 to 12.253826
- mask_table: int32 [96, 3136], P(None, ('seq', 'vocab')), may hold values 0 or 1
- state_ids: int32 [128], P(('groups', 'seq')), parts along dimension 0, may hold values from 0 to 95
- targets: int32 [128], P(('groups', 'seq')), parts along dimension 0, may hold values from 0 to 3135
Outputs:
- token_nll_loss: float32 [128], P(('groups', 'seq', 'vocab')), parts along dimension 0
There are 2 independent parts, one for each index of `groups`. A program takes and returns all parts, laid end to end along the dimension named above; an argument that names none is the same for every part. Nothing has to cross between parts.
All inputs are finite; a program needn't handle non-finite values. No bound on the sum of `mask_table` on one device may be relied on, other than what follows from the above.
Results may differ from a plain program's by a relative error of at most 0.0022.
Values may be sent and summed in bfloat16 or wider, within the bound.
No kernel may reach another device: no remote copies, remote signals or barrier semaphores. Data moves between devices by JAX's collectives and lax.ppermute only.
A program may use at most 192 MiB of HBM per device.

v0:
```python
import jax
import jax.numpy as jnp
from jax import lax
from jax.sharding import PartitionSpec as P


def carried_in(value, axis, join, neutral):
    count, mine = (lax.axis_size(axis), lax.axis_index(axis))
    pieces = jax.tree.map(lambda part: lax.all_gather(part, axis), value)
    total = jax.tree.map(
        lambda part, zero: jnp.full_like(part, 0) + jnp.asarray(zero, part.dtype), value, neutral
    )

    def lap(position, total):
        longer = join(total, jax.tree.map(lambda part: part[position], pieces))
        return jax.tree.map(lambda new, old: jnp.where(position < mine, new, old), longer, total)

    return lax.fori_loop(0, count - 1, lap, total)


def joined(part, axis, combine):
    gathered = jax.tree.map(lambda a: lax.all_gather(a, axis), part)

    def take(source):
        return jax.tree.map(lambda a: lax.dynamic_index_in_dim(a, source, 0, False), gathered)

    return lax.fori_loop(
        1, lax.axis_size(axis), lambda source, state: combine(state, take(source)), take(0)
    )


def carry_join(preceding, later):
    return (preceding[0] * later[0], preceding[1] * later[0][:, None, None] + later[1])


def total_join(first, second):
    top = jnp.maximum(first[0], second[0])
    total = first[1] * jnp.exp(first[0] - top) + second[1] * jnp.exp(second[0] - top)
    return (top, total, first[2] + second[2])


def shards(
    ssm_input,
    gate_input,
    b_proj,
    readout_matrix,
    step_raw,
    step_bias,
    decay_log,
    head_skip_gain,
    norm_gain,
    out_weight,
    residual,
    final_gain,
    head_weight,
    mask_table,
    state_ids,
    targets,
):
    highest = lax.Precision.HIGHEST
    rows = ssm_input.shape[0]
    heads = step_raw.shape[1]
    channels = ssm_input.shape[1]
    head_size = channels // heads
    state_size = b_proj.shape[1]
    step = jax.nn.softplus(step_raw + step_bias[None, :])
    log_rate = step * -jnp.exp(decay_log)[None, :]
    log_cum = jnp.cumsum(log_rate, axis=0)
    values = ssm_input.astype(jnp.float32).reshape(rows, heads, head_size)
    scaled = values * step[:, :, None]
    in_rows = b_proj.astype(jnp.float32)
    out_rows = readout_matrix.astype(jnp.float32)
    correlations = jnp.dot(out_rows, in_rows.T, precision=highest)
    causal = jnp.arange(rows)[:, None] >= jnp.arange(rows)[None, :]
    spread = log_cum[:, None, :] - log_cum[None, :, :]
    weights = jnp.exp(jnp.where(causal[:, :, None], spread, -1e30))
    within = jnp.einsum("tsh,ts,shp->thp", weights, correlations, scaled, precision=highest)
    last_log = log_cum[rows - 1]
    tails = jnp.exp(last_log[None, :] - log_cum)
    local_state = jnp.einsum("sh,shp,sn->hpn", tails, scaled, in_rows, precision=highest)
    identity = (
        jnp.ones((heads,), jnp.float32),
        jnp.zeros((heads, head_size, state_size), jnp.float32),
    )
    _, incoming = carried_in((jnp.exp(last_log), local_state), "seq", carry_join, identity)
    carried = jnp.einsum("th,hpn,tn->thp", jnp.exp(log_cum), incoming, out_rows, precision=highest)
    mixed = within + carried + head_skip_gain[None, :, None] * values
    gated = (mixed.reshape(rows, channels) * jax.nn.silu(gate_input.astype(jnp.float32))).astype(
        jnp.bfloat16
    )
    every_rows, all_states, all_targets = (
        lax.all_gather(gated, "seq", axis=0, tiled=True),
        lax.all_gather(state_ids, "seq", axis=0, tiled=True),
        lax.all_gather(targets, "seq", axis=0, tiled=True),
    )
    every_f = every_rows.astype(jnp.float32)
    squares = lax.psum(jnp.sum(every_f * every_f, axis=-1), "vocab")
    pair_count = lax.axis_size("vocab")
    scale = lax.rsqrt(squares / (channels * pair_count) + 1e-05)
    normed = (every_f * scale[:, None] * norm_gain[None, :]).astype(jnp.bfloat16)
    partial_sum = jnp.dot(normed, out_weight, preferred_element_type=jnp.float32)
    summed = lax.psum(partial_sum, "vocab")
    hidden = (residual.astype(jnp.float32) + summed).astype(jnp.bfloat16)
    full = lax.all_gather(hidden, "seq", axis=1, tiled=True)
    full_f = full.astype(jnp.float32)
    scale_two = lax.rsqrt(jnp.mean(full_f * full_f, axis=-1) + 1e-05)
    final = (full_f * scale_two[:, None] * final_gain[None, :]).astype(jnp.bfloat16)
    vocab_logits = jnp.dot(final, head_weight, preferred_element_type=jnp.float32)
    entries = head_weight.shape[1]
    block_index = lax.axis_index("seq") * pair_count + lax.axis_index("vocab")
    vocab_ids = block_index * entries + jnp.arange(entries, dtype=jnp.int32)
    state_count = mask_table.shape[0]
    one_hot = (all_states[:, None] == jnp.arange(state_count, dtype=jnp.int32)[None, :]).astype(
        jnp.float32
    )
    table_rows = jnp.dot(one_hot, mask_table.astype(jnp.float32))
    is_target = vocab_ids[None, :] == all_targets[:, None]
    allowed = (table_rows > 0.5) | is_target
    local_top = jnp.max(jnp.where(allowed, vocab_logits, -1e30), axis=-1)
    local_total = jnp.sum(
        jnp.where(allowed, jnp.exp(vocab_logits - local_top[:, None]), 0.0), axis=-1
    )
    local_pick = jnp.sum(jnp.where(is_target, vocab_logits, 0.0), axis=-1)
    positions = vocab_logits.shape[0]
    seq_count = lax.axis_size("seq")
    own_rows = positions // (seq_count * pair_count)
    top, total, picked = joined((local_top, local_total, local_pick), ("seq", "vocab"), total_join)
    losses = jnp.log(total) + top - picked
    return lax.dynamic_slice_in_dim(losses, block_index * own_rows, own_rows, 0)


def solution(mesh):
    placed = (
        P(("groups", "seq"), "vocab"),
        P(("groups", "seq"), "vocab"),
        P(("groups", "seq"), None),
        P(("groups", "seq"), None),
        P(("groups", "seq"), "vocab"),
        P("vocab"),
        P("vocab"),
        P("vocab"),
        P("vocab"),
        P("vocab", "seq"),
        P("groups", "seq"),
        P(),
        P(None, ("seq", "vocab")),
        P(None, ("seq", "vocab")),
        P(("groups", "seq")),
        P(("groups", "seq")),
    )
    return jax.shard_map(
        shards, mesh=mesh, in_specs=placed, out_specs=P(("groups", "seq", "vocab")), check_vma=False
    )
```

profile of v0, /device:TPU:0, one launch (start us, length us, event | category | flops | bytes accessed | tf_op | source)
XLA Modules:
  0.0 261.6 jit_solution(14560804017254880365)
XLA Ops:
  6.5 0.7 exponential_negate_fusion
  7.3 0.7 broadcast_multiply_fusion.2
  8.0 0.8 reshape.48
  9.0 2.3 fusion.23
  11.5 1.2 dynamic-slice
  12.8 1.3 dynamic-slice.2
  14.7 0.9 dynamic-update-slice.1
  15.5 0.8 dynamic-update-slice
  17.1 13.3 %all-reduce.5 = (s32[64]{0:T(128)S(1)}, s32[64]{0:T(128)S(1)}) all-reduce(s32[64]{0:T(128)S(1)} %dynamic-update-slice.1, s32[64]{0:T(128)S(1)} %dynamic-update-slice), channel_id=1, replica_groups=mesh['groups'=2,'seq'=8,'vocab'=2] {'seq'}, use_global_device_ids=true, to_apply=%add.1 | all-reduce | flops 128 | bytes 1024
  30.3 18.0 %all-gather.4 = f32[8,1,20]{2,1,0:T(1,128)S(1)} all-gather(f32[1,1,20]{2,1,0:T(1,128)S(1)} %get-tuple-element.339), channel_id=1, replica_groups=mesh['groups'=2,'seq'=8,'vocab'=2] {'seq'}, dimensions={0}, use_global_device_ids=true | all-gather | bytes 720 | tf_op jit(solution)/shard_map/all_gather | solution.py:9
  48.3 0.8 fusion.48
  49.2 0.4 convolution_bitcast_fusion.1
  49.5 51.0 %all-gather.8.cloned.1.call-done = f32[160,64,128]{2,1,0:T(8,128)} async-done(((f32[20,64,128]{2,1,0:T(8,128)}), f32[160,64,128]{2,1,0:T(8,128)}) %all-gather.8.cloned.1.call-update) | async-done | bytes 5242896 | tf_op jit(solution)/shard_map/all_gather | solution.py:9
  100.6 9.0 %while.34 = (s32[]{:T(128)}, f32[20,64,128]{2,1,0:T(8,128)S(1)}, s32[]{:T(128)}, f32[8,20]{1,0:T(8,128)S(1)}, f32[8,20,64,128]{3,2,1,0:T(8,128)}, /*index=5*/s32[]{:T(128)}, s32[]{:T(128)}) while((s32[]{:T(128)}, f32[20,64,128]{2,1,0:T(8,128)S(1)}, s32[]{:T(128)}, f32[8,20]{1,0:T(8,128)S(1)}, f32[8,20,64,128]{3,2,1,0:T(8,128)}, ...), condition=%wide.region_2.3_spmd.clone, body=%wide.region_1.2_spmd.clone.sunk | while | flops 655364 | bytes 1966433 | solution.py:18
  100.6 1.3 fusion.57
  101.9 1.2 fusion.57
  103.2 1.2 fusion.57
  104.5 1.2 fusion.57
  105.8 1.2 fusion.57
  107.0 1.2 fusion.57
  108.3 1.2 fusion.57
  109.6 0.9 fusion.10
  110.6 30.6 %all_gather.45 = bf16[64,1280]{1,0:T(8,128)(2,1)S(1)} all-gather(bf16[8,1280]{1,0:T(8,128)(2,1)S(1)} %fusion.40), channel_id=1, replica_groups=mesh['groups'=2,'seq'=8,'vocab'=2] {'seq'}, dimensions={0}, use_global_device_ids=true | all-gather | bytes 184320 | tf_op jit(solution)/shard_map/all_gather | solution.py:92
  141.4 2.5 psum.14
  143.8 1.0 fusion.18
  144.9 16.1 %all-reduce.9.cloned.1.call-done = f32[64,320]{1,0:T(8,128)} async-done(((f32[64,320]{1,0:T(8,128)}), f32[64,320]{1,0:T(8,128)}) %all-reduce.9.cloned.1.call-update) | async-done | bytes 81936 | tf_op jit(solution)/shard_map/psum | solution.py:102
  161.0 0.9 fusion.31
  161.9 31.4 %all-gather.5 = bf16[8,320,64]{1,2,0:T(8,128)(2,1)S(1)} all-gather(bf16[1,320,64]{1,2,0:T(8,128)(2,1)S(1)} %fusion.31), channel_id=1, replica_groups=mesh['groups'=2,'seq'=8,'vocab'=2] {'seq'}, dimensions={0}, use_global_device_ids=true | all-gather | bytes 368640 | tf_op jit(solution)/shard_map/all_gather | solution.py:104
  194.0 0.5 fusion.15
  195.6 57.6 %all-reduce.6 = (f32[1024]{0:T(1024)S(1)}, f32[1024]{0:T(1024)S(1)}, f32[1024]{0:T(1024)S(1)}) all-reduce(f32[1024]{0:T(1024)S(1)} %dynamic-update-slice.2, f32[1024]{0:T(1024)S(1)} %dynamic-update-slice.3, f32[1024]{0:T(1024)S(1)} %dynamic-update-slice.4), channel_id=3, replica_groups=mesh['groups'=2,'seq'=8,'vocab'=2] {'seq','vocab'}, use_global_device_ids=true, to_apply=%add.2 | all-reduce | flops 3072 | bytes 24576
  253.5 0.7 while.33
  254.2 0.6 dynamic_slice.60
  (79 shorter events, 3.2 us)
Async XLA Ops:
  6.5 187.4 %copy-start = (bf16[2560,196]{0,1:T(8,128)(2,1)S(1)}, bf16[2560,196]{0,1:T(8,128)(2,1)}, u32[]{:S(2)}) copy-start(bf16[2560,196]{0,1:T(8,128)(2,1)} %param.32) | copy-start | bytes 3010564
  6.5 94.0 %all-gather.8.cloned.1.call-start = ((), (), s32[]{:S(2)}) async-start(), calls=%async_computation.1 | async-start | bytes 5898240 | tf_op jit(solution)/shard_map/all_gather | solution.py:9
  11.3 98.3 %copy-start.6 = (bf16[8,128]{1,0:T(8,128)(2,1)S(1)}, bf16[8,128]{1,0:T(8,128)(2,1)}, u32[]{:S(2)}) copy-start(bf16[8,128]{1,0:T(8,128)(2,1)} %param.23) | copy-start | bytes 6148
  11.3 98.3 %copy-start.7 = (f32[20]{0:T(128)S(1)}, f32[20]{0:T(128)}, u32[]{:S(2)}) copy-start(f32[20]{0:T(128)} %param.27) | copy-start | bytes 244
  11.3 149.7 %all-reduce.9.cloned.1.call-start = ((), (), s32[]{:S(2)}) async-start(), calls=%async_computation | async-start | bytes 196608 | tf_op jit(solution)/shard_map/psum | solution.py:102
  100.6 10.0 %copy-start.3 = (bf16[8,1280]{1,0:T(8,128)(2,1)S(1)}, bf16[8,1280]{1,0:T(8,128)(2,1)}, u32[]{:S(2)}) copy-start(bf16[8,1280]{1,0:T(8,128)(2,1)} %param.21) | copy-start | bytes 61444
  100.6 43.3 %copy-start.1 = (bf16[1280,320]{0,1:T(8,128)(2,1)S(1)}, bf16[1280,320]{0,1:T(8,128)(2,1)}, u32[]{:S(2)}) copy-start(bf16[1280,320]{0,1:T(8,128)(2,1)} %param.29) | copy-start | bytes 2457604
  100.6 43.3 %copy-start.5 = (f32[1280]{0:T(1024)S(1)}, f32[1280]{0:T(1024)}, u32[]{:S(2)}) copy-start(f32[1280]{0:T(1024)} %param.28) | copy-start | bytes 15364
  100.6 60.5 %copy-start.2 = (bf16[64,320]{1,0:T(8,128)(2,1)S(1)}, bf16[64,320]{1,0:T(8,128)(2,1)}, u32[]{:S(2)}) copy-start(bf16[64,320]{1,0:T(8,128)(2,1)} %param.30) | copy-start | bytes 122884
  109.6 84.4 %copy-start.4 = (f32[2560]{0:T(1024)S(1)}, f32[2560]{0:T(1024)}, u32[]{:S(2)}) copy-start(f32[2560]{0:T(1024)} %param.31) | copy-start | bytes 30724
  109.6 84.9 %copy-start.8 = (s32[96,196]{1,0:T(8,128)S(1)}, s32[96,196]{1,0:T(8,128)}, u32[]{:S(2)}) copy-start(s32[96,196]{1,0:T(8,128)} %param.33) | copy-start | bytes 225796
Sparse Core Ops, SparseCore 0:
  11.4 89.1 all-gather.7
  145.0 15.9 all-reduce.8
where the time goes:
time: 262 us
  blocking collectives  153 us (58%)
  waiting for transfers between devices  67.2 us (26%)
  between operations  14.9 us (6%)
  other arithmetic  12.2 us (5%)
  local copies, waits for them, and re-layouts  7.35 us (3%)
  matrix products  6.07 us (2%)
    unnamed x2, blocking collectives  70.9 us
    all_gather x1, waiting for transfers between devices, carried_in(): pieces = jax.tree.map(lambda part: lax.all_gather(part, axis), value)  51 us
    all_gather x1, blocking collectives, shards(): full = lax.all_gather(hidden, 'seq', axis=1, tiled=True)  31.4 us
    all_gather x1, blocking collectives, shards(): lax.all_gather(gated, 'seq', axis=0, tiled=True)  30.6 us
    all_gather x1, blocking collectives, carried_in(): pieces = jax.tree.map(lambda part: lax.all_gather(part, axis), value)  18 us
    psum x1, waiting for transfers between devices, shards(): summed = lax.psum(partial_sum, 'vocab')  16.1 us
    select_n x7, other arithmetic, lap(): jnp.where(position < mine, new, old)  8.7 us
  transfers between devices with their start and end apart: 2, of which 2 were waited for; matrix products, arithmetic and copies ran while one was open for 2% of the time, Pallas kernels for 0%

commit v1 on v0

v1 whole, which is shorter than its diff:
```python
import jax
import jax.numpy as jnp
from jax import lax
from jax.experimental import pallas as pl
from jax.experimental.pallas import tpu as pltpu
from jax.sharding import PartitionSpec as P

F32 = jnp.float32
BF16 = jnp.bfloat16
HIGHEST = lax.Precision.HIGHEST
EPS = 1e-05
LANES = 128
NEG = -1e30
IDS = 64
VMEM = pltpu.VMEM


def dims(shape):
    return (((len(shape) - 1,), (0,)), ((), ()))


def pack_kernel(ssm_ref, gate_ref, b_ref, c_ref, raw_ref, ids_ref, targets_ref, out_ref):
    count, rows, _ = out_ref.shape
    channels = ssm_ref.shape[1]
    state = b_ref.shape[1]
    heads = raw_ref.shape[1]
    raw = raw_ref[...]
    high = raw.astype(BF16)
    rest = raw - high.astype(F32)
    middle = rest.astype(BF16)
    low = (rest - middle.astype(F32)).astype(BF16)
    ids = ids_ref[...].astype(F32)
    targets = targets_ref[...]
    upper = lax.shift_right_logical(targets, 8)
    under = (targets - upper * 256).astype(F32)
    parts = [high.astype(F32), middle.astype(F32), low.astype(F32)]
    parts.append(jnp.zeros((rows, IDS - 3 * heads), F32))
    for part in (ids, upper.astype(F32), under):
        parts.append(jnp.broadcast_to(part, (rows, rows)))
    parts.append(jnp.zeros((rows, LANES - IDS - 3 * rows), F32))
    misc = jnp.concatenate(parts, axis=1).astype(BF16)
    edge = 2 * channels
    for k in range(count):
        out_ref[k, :, 0:channels] = ssm_ref[...]
        out_ref[k, :, channels:edge] = gate_ref[...]
        out_ref[k, :, edge : edge + state] = b_ref[...]
        out_ref[k, :, edge + state : edge + 2 * state] = c_ref[...]
        out_ref[k, :, edge + 2 * state :] = misc


def pack(count, ssm, gate, b, c, raw, ids, targets):
    rows, channels = ssm.shape
    width = 2 * channels + 2 * b.shape[1] + LANES
    return pl.pallas_call(
        pack_kernel,
        out_shape=jax.ShapeDtypeStruct((count, rows, width), BF16),
        name="pack",
    )(ssm, gate, b, c, raw, ids.reshape(1, rows), targets.reshape(1, rows))


def mixer_kernel(
    seq_rows, x_ref, bias_ref, decay_ref, skip_ref, gain_ref, weight_ref, residual_ref,
    mine_ref, theirs_ref, kept_ref, unit_ref,
):
    core = lax.axis_index("vocab")
    rows = x_ref.shape[0]
    heads = bias_ref.shape[1]
    channels = gain_ref.shape[1]
    state = (x_ref.shape[1] - LANES - 2 * channels) // 2
    edge = 2 * channels
    half = rows // 2
    size = channels // heads
    misc = x_ref[:, edge + 2 * state :].astype(F32)
    raw = misc[:, 0:heads] + misc[:, heads : 2 * heads] + misc[:, 2 * heads : 3 * heads]
    step = jax.nn.softplus(raw + bias_ref[...])
    rate = step * -jnp.exp(decay_ref[...])
    r64 = lax.broadcasted_iota(jnp.int32, (rows, rows), 0)
    c64 = lax.broadcasted_iota(jnp.int32, (rows, rows), 1)
    tri = (c64 <= r64).astype(F32)
    log_cum = jnp.dot(tri, rate, precision=HIGHEST, preferred_element_type=F32)
    fill = jnp.zeros((rows, LANES - heads), F32)
    wide_cum = jnp.concatenate([log_cum, fill], axis=1)
    wide_step = jnp.concatenate([step, fill], axis=1)
    cum_rows = jnp.concatenate([wide_cum, wide_cum], axis=0).T
    step_rows = jnp.concatenate([wide_step, wide_step], axis=0).T
    b = x_ref[:, edge : edge + state]
    c = x_ref[:, edge + state : edge + 2 * state]
    twice = jnp.concatenate([b, b], axis=0)
    corr = lax.dot_general(c, twice, (((1,), (1,)), ((), ())), preferred_element_type=F32)
    lane = lax.broadcasted_iota(jnp.int32, (rows, LANES), 1)
    row = lax.broadcasted_iota(jnp.int32, (rows, LANES), 0)
    first = lane < size
    causal = jnp.where(first, lane, lane - size) <= row
    first_row = lax.broadcasted_iota(jnp.int32, (1, LANES), 1) < size

    own = seq_rows // 2
    side = r64 // half
    place = r64 - side * half
    which = jnp.where(side == 0, core, 1 - core)
    source = (place // own) * seq_rows + which * own + place % own
    order = (c64 == source).astype(BF16)

    squares = jnp.zeros((rows, LANES), F32)
    for j in range(heads // 2):
        left, right = 2 * j, 2 * j + 1
        span = slice(j * LANES, (j + 1) * LANES)
        at = jnp.where(first, log_cum[:, left : left + 1], log_cum[:, right : right + 1])
        back = jnp.where(first_row, cum_rows[left : left + 1], cum_rows[right : right + 1])
        sizes = jnp.where(first_row, step_rows[left : left + 1], step_rows[right : right + 1])
        weights = jnp.exp(jnp.where(causal, at - back, NEG)) * (corr * sizes)
        high = weights.astype(BF16)
        low = (weights - high.astype(F32)).astype(BF16)
        v = x_ref[:, span]
        none = jnp.zeros_like(v)
        stacked = jnp.concatenate([jnp.where(first, v, none), jnp.where(first, none, v)], axis=0)
        y = jnp.dot(high, stacked, preferred_element_type=F32)
        y = y + jnp.dot(low, stacked, preferred_element_type=F32)
        skip = jnp.where(first_row, skip_ref[0, left], skip_ref[0, right])
        mixed = y + skip * v.astype(F32)
        gate = x_ref[:, channels + j * LANES : channels + (j + 1) * LANES].astype(F32)
        gated = (mixed * (gate / (1.0 + jnp.exp(-gate)))).astype(BF16)
        moved = jnp.dot(order, gated, preferred_element_type=F32)
        squares = squares + moved * moved
        unit_ref[:, span] = (moved * gain_ref[:, span]).astype(BF16)
    partial = jnp.dot(unit_ref[...], weight_ref[...], preferred_element_type=F32)
    kept_ref[...] = jnp.dot(order[0:half], residual_ref[...], preferred_element_type=F32)

    at_row = row % seq_rows
    info = jnp.zeros((rows, LANES), F32)
    for k in range(3):
        column = jnp.sum(
            jnp.where(lane == IDS + k * seq_rows + at_row, misc, 0.0), axis=1, keepdims=True
        )
        info = jnp.where(lane == k + 1, column, info)
    info = jnp.dot(order, info.astype(BF16), preferred_element_type=F32)
    total = jnp.sum(squares, axis=1, keepdims=True)
    info = jnp.where(lane == 0, total, info)
    width = partial.shape[1]
    start = mine_ref.shape[1] - LANES
    mine_ref[:, 0:width] = partial[0:half]
    mine_ref[:, start:] = info[0:half]
    theirs_ref[:, 0:width] = partial[half:]
    theirs_ref[:, start:] = info[half:]


def mixer(x, seq_rows, bias, decay, skip, gain, weight, residual):
    rows = x.shape[0]
    heads = bias.shape[0]
    channels = gain.shape[0]
    width = weight.shape[1]
    total = (width + LANES - 1) // LANES * LANES + LANES
    half = rows // 2
    sums = jax.ShapeDtypeStruct((half, total), F32)
    whole = pl.BlockSpec(memory_space=VMEM)

    def kernel(*refs):
        mixer_kernel(seq_rows, *refs)

    return pl.pallas_call(
        kernel,
        out_shape=(sums, sums, jax.ShapeDtypeStruct((half, width), F32)),
        in_specs=[whole, whole, whole, pl.BlockSpec(memory_space=pltpu.SMEM), whole, whole, whole],
        scratch_shapes=[VMEM((rows, channels), BF16)],
        name="mixer",
    )(
        x, bias.reshape(1, heads), decay.reshape(1, heads), skip.reshape(1, heads),
        gain.reshape(1, channels), weight, residual,
    )


def hidden_kernel(features, mine_ref, theirs_ref, kept_ref, out_ref):
    count, _, width = out_ref.shape
    start = mine_ref.shape[1] - LANES
    squares = mine_ref[:, start : start + 1] + theirs_ref[:, start : start + 1]
    scale = lax.rsqrt(squares / features + EPS)
    sums = mine_ref[:, 0:width] + theirs_ref[:, 0:width]
    hidden = (kept_ref[...] + sums * scale).astype(BF16)
    for k in range(count):
        out_ref[k] = hidden


def hidden_rows(count, features, mine, theirs, kept):
    def kernel(*refs):
        hidden_kernel(features, *refs)

    return pl.pallas_call(
        kernel,
        out_shape=jax.ShapeDtypeStruct((count,) + kept.shape, BF16),
        name="hidden",
    )(mine, theirs, kept)


def head_kernel(
    h_ref, gain_ref, own_ref, other_ref, own_mask_ref, other_mask_ref, info_ref, out_ref
):
    core = lax.axis_index("vocab")
    block = lax.axis_index("seq") * 2
    count, rows, width = h_ref.shape
    features = count * width
    squares = jnp.zeros((rows, width), F32)
    for k in range(count):
        part = h_ref[k].astype(F32)
        squares = squares + part * part
    scale = lax.rsqrt(jnp.sum(squares, axis=1, keepdims=True) / features + EPS)
    entries = own_ref.shape[1]
    logits = [jnp.zeros((rows, entries), F32), jnp.zeros((rows, entries), F32)]
    for k in range(count):
        final = (h_ref[k].astype(F32) * scale * gain_ref[k : k + 1, :]).astype(BF16)
        span = slice(k * width, (k + 1) * width)
        for i, ref in enumerate((own_ref, other_ref)):
            logits[i] = logits[i] + jnp.dot(final, ref[span, :], preferred_element_type=F32)
    states = own_mask_ref.shape[0]
    start = info_ref.shape[1] - LANES
    ids = info_ref[:, start + 1 : start + 2].astype(jnp.int32)
    upper = info_ref[:, start + 2 : start + 3].astype(jnp.int32)
    target = upper * 256 + info_ref[:, start + 3 : start + 4].astype(jnp.int32)
    pick_row = (lax.broadcasted_iota(jnp.int32, (rows, states), 1) == ids).astype(BF16)
    column = lax.broadcasted_iota(jnp.int32, (rows, entries), 1)
    allowed, wanted = [], []
    for ref, which in ((own_mask_ref, core), (other_mask_ref, 1 - core)):
        table = (ref[...] == 1).astype(F32).astype(BF16)
        chosen = jnp.dot(pick_row, table, preferred_element_type=F32)
        is_target = column + (block + which) * entries == target
        wanted.append(is_target)
        allowed.append((chosen > 0.5) | is_target)
    tops = [
        jnp.max(jnp.where(a, x, NEG), axis=1, keepdims=True) for a, x in zip(allowed, logits)
    ]
    top = jnp.maximum(tops[0], tops[1])
    total = jnp.zeros((rows, 1), F32)
    picked = jnp.zeros((rows, 1), F32)
    for a, w, x in zip(allowed, wanted, logits):
        total = total + jnp.sum(jnp.where(a, jnp.exp(x - top), 0.0), axis=1, keepdims=True)
        picked = picked + jnp.sum(jnp.where(w, x, 0.0), axis=1, keepdims=True)
    lane = lax.broadcasted_iota(jnp.int32, (rows, LANES), 1)
    stats = jnp.where(lane == 0, top, jnp.where(lane == 1, total, picked))
    own = out_ref.shape[1]
    for k in range(count):
        out_ref[k] = stats[k * own : (k + 1) * own]


def head(h, gain, own, other, own_mask, other_mask, info):
    count, rows, width = h.shape
    whole = pl.BlockSpec(memory_space=VMEM)
    return pl.pallas_call(
        head_kernel,
        out_shape=jax.ShapeDtypeStruct((count, rows // count, LANES), F32),
        in_specs=[whole] * 7,
        name="head",
    )(h, gain.reshape(count, width), own, other, own_mask, other_mask, info)


def combine_kernel(stats_ref, out_ref):
    count = stats_ref.shape[0]
    top = stats_ref[0, :, 0:1]
    for k in range(1, count):
        top = jnp.maximum(top, stats_ref[k, :, 0:1])
    total = jnp.zeros_like(top)
    picked = jnp.zeros_like(top)
    for k in range(count):
        total = total + stats_ref[k, :, 1:2] * jnp.exp(stats_ref[k, :, 0:1] - top)
        picked = picked + stats_ref[k, :, 2:3]
    out_ref[...] = jnp.log(total) + top - picked


def combine(stats):
    own = stats.shape[1]
    out = pl.pallas_call(
        combine_kernel, out_shape=jax.ShapeDtypeStruct((own, 1), F32), name="combine"
    )(stats)
    return out.reshape(own)


def wide_pack(count, ssm, gate, b, c, raw, ids, targets):
    rows = ssm.shape[0]
    heads = raw.shape[1]
    high = lax.reduce_precision(raw, 8, 7)
    middle = lax.reduce_precision(raw - high, 8, 7)
    low = raw - high - middle
    parts = [high, middle, low, jnp.zeros((rows, IDS - 3 * heads), F32)]
    parts += [a.astype(F32)[:, None] for a in (ids, targets // 256, targets % 256)]
    parts.append(jnp.zeros((rows, LANES - IDS - 3), F32))
    misc = jnp.concatenate(parts, axis=1).astype(BF16)
    row = jnp.concatenate([ssm, gate, b, c, misc], axis=1)
    return jnp.broadcast_to(row[None], (count,) + row.shape)


def wide_mixer(x, seq_rows, bias, decay, skip, gain, weight, residual):
    rows = x.shape[0]
    heads, channels = bias.shape[0], gain.shape[0]
    state = (x.shape[1] - LANES - 2 * channels) // 2
    edge = 2 * channels
    core = lax.axis_index("vocab")
    misc = x[:, edge + 2 * state :].astype(F32)
    raw = misc[:, 0:heads] + misc[:, heads : 2 * heads] + misc[:, 2 * heads : 3 * heads]
    step = jax.nn.softplus(raw + bias[None, :])
    log_cum = jnp.cumsum(step * -jnp.exp(decay)[None, :], axis=0)
    corr = jnp.dot(
        x[:, edge + state : edge + 2 * state],
        x[:, edge : edge + state].T,
        preferred_element_type=F32,
    )
    values = x[:, 0:channels].astype(F32).reshape(rows, heads, -1).transpose(1, 0, 2)
    causal = jnp.arange(rows)[:, None] >= jnp.arange(rows)[None, :]

    def one(inputs):
        cum, size, v = inputs
        weights = jnp.exp(jnp.where(causal, cum[:, None] - cum[None, :], NEG))
        return jnp.dot(weights * corr * size[None, :], v, precision=HIGHEST)

    y = lax.map(one, (log_cum.T, step.T, values))
    mixed = (y + skip[:, None, None] * values).transpose(1, 0, 2).reshape(rows, channels)
    gated = (mixed * jax.nn.silu(x[:, channels:edge].astype(F32))).astype(BF16)
    wide = gated.astype(F32)
    squares = jnp.sum(wide * wide, axis=1, keepdims=True)
    unit = (wide * gain[None, :]).astype(BF16)
    partial = jnp.dot(unit, weight, preferred_element_type=F32)
    width = weight.shape[1]
    start = (width + LANES - 1) // LANES * LANES
    info = jnp.concatenate([squares, misc[:, IDS : IDS + 3]], axis=1)
    sums = jnp.concatenate(
        [
            partial,
            jnp.zeros((rows, start - width), F32),
            info,
            jnp.zeros((rows, LANES - info.shape[1]), F32),
        ],
        axis=1,
    )

    def side(a, which):
        split = a.reshape(rows // seq_rows, 2, seq_rows // 2, -1)
        return lax.dynamic_index_in_dim(split, which, 1, False).reshape(rows // 2, -1)

    return side(sums, core), side(sums, 1 - core), side(residual.astype(F32), core)


def shards(
    ssm_input,
    gate_input,
    b_proj,
    readout_matrix,
    step_raw,
    step_bias,
    decay_log,
    head_skip_gain,
    norm_gain,
    out_weight,
    residual,
    final_gain,
    head_weight,
    mask_table,
    state_ids,
    targets,
):
    count = lax.axis_size("seq")
    rows, channels = ssm_input.shape
    features = 2 * channels
    small = count * rows <= LANES // 2
    swap = [(0, 1), (1, 0)]
    other_weight = lax.ppermute(head_weight, "vocab", swap)
    other_mask = lax.ppermute(mask_table, "vocab", swap)
    packed = (pack if small else wide_pack)(
        count, ssm_input, gate_input, b_proj, readout_matrix, step_raw, state_ids, targets
    )
    gathered = lax.all_to_all(packed, "seq", 0, 0, tiled=True)
    x = gathered.reshape(count * rows, packed.shape[2])
    mine, theirs, kept = (mixer if small else wide_mixer)(
        x, rows, step_bias, decay_log, head_skip_gain, norm_gain, out_weight, residual
    )
    arrived = lax.ppermute(theirs, "vocab", swap)
    if small:
        spread = hidden_rows(count, features, mine, arrived, kept)
    else:
        width = kept.shape[1]
        start = mine.shape[1] - LANES
        sums = mine + arrived
        scale = lax.rsqrt(sums[:, start : start + 1] / features + EPS)
        hidden = (kept + sums[:, 0:width] * scale).astype(BF16)
        spread = jnp.broadcast_to(hidden[None], (count,) + hidden.shape)
    full = lax.all_to_all(spread, "seq", 0, 0, tiled=True)
    if small:
        stats = head(full, final_gain, head_weight, other_weight, mask_table, other_mask, mine)
    else:
        stats = wide_head(
            full, final_gain, head_weight, other_weight, mask_table, other_mask, mine
        )
    placed = lax.all_to_all(stats, "seq", 0, 0, tiled=True)
    return combine(placed) if small else wide_combine(placed)


def wide_head(full, gain, own, other, own_mask, other_mask, info):
    count, rows, width = full.shape
    core = lax.axis_index("vocab")
    block = lax.axis_index("seq") * 2
    wide = full.transpose(1, 0, 2).reshape(rows, count * width).astype(F32)
    scale = lax.rsqrt(jnp.mean(wide * wide, axis=1, keepdims=True) + EPS)
    final = (wide * scale * gain[None, :]).astype(BF16)
    start = info.shape[1] - LANES
    ids, upper, under = (info[:, start + k].astype(jnp.int32) for k in (1, 2, 3))
    target = upper * 256 + under
    entries = own.shape[1]
    logits, allowed, wanted = [], [], []
    for weight, table, which in ((own, own_mask, core), (other, other_mask, 1 - core)):
        logits.append(jnp.dot(final, weight, preferred_element_type=F32))
        column = (block + which) * entries + jnp.arange(entries, dtype=jnp.int32)
        wanted.append(column[None, :] == target[:, None])
        one_hot = (ids[:, None] == jnp.arange(table.shape[0])[None, :]).astype(BF16)
        chosen = jnp.dot(one_hot, (table == 1).astype(BF16), preferred_element_type=F32)
        allowed.append((chosen > 0.5) | wanted[-1])
    x, a, w = (jnp.concatenate(p, axis=1) for p in (logits, allowed, wanted))
    top = jnp.max(jnp.where(a, x, NEG), axis=1)
    total = jnp.sum(jnp.where(a, jnp.exp(x - top[:, None]), 0.0), axis=1)
    picked = jnp.sum(jnp.where(w, x, 0.0), axis=1)
    return jnp.stack([top, total, picked], axis=1).reshape(count, rows // count, 3)


def wide_combine(stats):
    top = jnp.max(stats[:, :, 0], axis=0)
    total = jnp.sum(stats[:, :, 1] * jnp.exp(stats[:, :, 0] - top[None, :]), axis=0)
    return jnp.log(total) + top - jnp.sum(stats[:, :, 2], axis=0)


def solution(mesh):
    placed = (
        P(("groups", "seq"), "vocab"),
        P(("groups", "seq"), "vocab"),
        P(("groups", "seq"), None),
        P(("groups", "seq"), None),
        P(("groups", "seq"), "vocab"),
        P("vocab"),
        P("vocab"),
        P("vocab"),
        P("vocab"),
        P("vocab", "seq"),
        P("groups", "seq"),
        P(),
        P(None, ("seq", "vocab")),
        P(None, ("seq", "vocab")),
        P(("groups", "seq")),
        P(("groups", "seq")),
    )
    return jax.shard_map(
        shards, mesh=mesh, in_specs=placed, out_specs=P(("groups", "seq", "vocab")), check_vma=False
    )
```

time: 262 us -> 58.9 us (0.22)
  blocking collectives: 153 us -> 10.5 us
  waiting for transfers between devices: 67.2 us -> 14.9 us
  between operations: 14.9 us -> 0.05 us
  Pallas kernels: 0 us -> 12.4 us
  starting transfers between devices: 0.04 us -> 11.1 us
  other arithmetic: 12.2 us -> 1.29 us
  matrix products: 6.07 us -> 0 us
    all_gather x3 -> x0, blocking collectives: 80 us -> none  [the longest x1 31.4 us: shards(): full = lax.all_gather(hidden, 'seq', axis=1, tiled=True)]
    unnamed x2 -> x0, blocking collectives: 70.9 us -> none
    all_gather x1 -> x0, waiting for transfers between devices: 51 us -> none  [carried_in(): pieces = jax.tree.map(lambda part: lax.all_gather(part, axis), value)]
    psum x1 -> x0, waiting for transfers between devices: 16.1 us -> none  [shards(): summed = lax.psum(partial_sum, 'vocab')]
    all_to_all x0 -> x2, waiting for transfers between devices: none -> 13.4 us  [the longest x1 8.76 us: shards(): gathered = lax.all_to_all(packed, 'seq', 0, 0, tiled=True)]
    pallas_call x0 -> x5, Pallas kernels: none -> 12.4 us  [the longest x1 4.31 us: mixer(): pl.pallas_call(kernel, out_shape=(sums, sums, jax.ShapeDtypeStruct((half,...]
    all_to_all x0 -> x2, starting transfers between devices: none -> 11 us  [the longest x1 7.25 us: shards(): gathered = lax.all_to_all(packed, 'seq', 0, 0, tiled=True)]
    all_to_all x0 -> x1, blocking collectives: none -> 10.5 us  [shards(): placed = lax.all_to_all(stats, 'seq', 0, 0, tiled=True)]
  transfers between devices with their start and end apart: 2 -> 5, of which waited for: 2 -> 3; matrix products, arithmetic and copies ran while one was open for 2% -> 10% of each run, Pallas kernels for 0% -> 10%
where the time goes in v1:
time: 58.9 us; the launch traced here: 58.3 us
  waiting for transfers between devices  14.9 us (25%)
  Pallas kernels  12.4 us (21%)
  starting transfers between devices  11.1 us (19%)
  blocking collectives  10.5 us (18%)
  local copies, waits for them, and re-layouts  8.19 us (14%)
  other arithmetic  1.29 us (2%)
    all_to_all x1, blocking collectives, shards(): placed = lax.all_to_all(stats, 'seq', 0, 0, tiled=True)  10.5 us
    all_to_all x1, waiting for transfers between devices, shards(): gathered = lax.all_to_all(packed, 'seq', 0, 0, tiled=True)  8.76 us
    all_to_all x1, starting transfers between devices, shards(): gathered = lax.all_to_all(packed, 'seq', 0, 0, tiled=True)  7.25 us
    unnamed x18, local copies, waits for them, and re-layouts  4.79 us
    all_to_all x1, waiting for transfers between devices, shards(): full = lax.all_to_all(spread, 'seq', 0, 0, tiled=True)  4.63 us
    pallas_call x1, Pallas kernels, mixer(): pl.pallas_call(kernel, out_shape=(sums, sums, jax.ShapeDtypeStruct((half,...  4.31 us
    all_to_all x1, starting transfers between devices, shards(): full = lax.all_to_all(spread, 'seq', 0, 0, tiled=True)  3.75 us
    pallas_call x1, Pallas kernels, head(): pl.pallas_call(head_kernel, out_shape=jax.ShapeDtypeStruct((count, rows /...  3.24 us
  transfers between devices with their start and end apart: 5, of which 3 were waited for; matrix products, arithmetic and copies ran while one was open for 10% of the time, Pallas kernels for 10%

profile of v1, /device:TPU:0, one launch (start us, length us, event | category | flops | bytes accessed | tf_op | source)
XLA Modules:
  0.0 58.3 jit_solution(13196932378984269972)
XLA Ops:
  0.0 0.0 copy-start.2
  0.0 1.7 %pack.1 = bf16[8,8,2944]{2,1,0:T(8,128)(2,1)} custom-call(bf16[8,1280]{1,0:T(8,128)(2,1)} %ssm_ref.1, bf16[8,1280]{1,0:T(8,128)(2,1)} %gate_ref.1, bf16[8,128]{1,0:T(8,128)(2,1)} %b_ref.1, bf16[8,128]{1,0:T(8,128)(2,1)} %c_ref.1, f32[8,20]{1,0:T(8,128)} %raw_ref.1, s32[1,8]{1,0:T(1,128)} %bitcast.10, s32[1,8]{1,0:T(1,128)} %bitcast.11), custom_call_target="tpu_custom_call" | custom-call | tf_op jit(solution)/shard_map/pack/pallas_call | solution.py:54
  1.7 7.3 %all-to-all-start = ((bf16[8,8,2944]{2,1,0:T(8,128)(2,1)}), bf16[8,8,2944]{2,1,0:T(8,128)(2,1)S(1)}, u32[]{:S(2)}, u32[]{:S(2)}) async-start(bf16[8,8,2944]{2,1,0:T(8,128)(2,1)} %pack.1), calls=%async_computation | async-start | bytes 753664 | tf_op jit(solution)/shard_map/all_to_all | solution.py:366
  9.0 0.0 collective-permute-start.1
  9.0 1.3 %reshape.33.refs_4_ = f32[1,1280]{1,0:T(1,128)} reshape(f32[1280]{0:T(1024)} %param.24) | data formatting | bytes 10240 | tf_op jit(solution)/shard_map/reshape | solution.py:167
  10.3 0.0 copy-done.2
  10.3 1.3 %copy.23.refs_5_ = bf16[1280,320]{1,0:T(8,128)(2,1)} copy(bf16[1280,320]{0,1:T(8,128)(2,1)S(1)} %copy-done.2) | data formatting | bytes 1638400 | tf_op args[9]
  11.5 0.0 copy-start.1
  11.5 8.8 %all-to-all-done = bf16[8,8,2944]{2,1,0:T(8,128)(2,1)S(1)} async-done(((bf16[8,8,2944]{2,1,0:T(8,128)(2,1)}), bf16[8,8,2944]{2,1,0:T(8,128)(2,1)S(1)}, u32[]{:S(2)}, u32[]{:S(2)}) %all-to-all-start) | async-done | bytes 376864 | tf_op jit(solution)/shard_map/all_to_all | solution.py:366
  20.3 0.8 %copy-done = bf16[8,8,2944]{2,1,0:T(8,128)(2,1)} copy-done((bf16[8,8,2944]{2,1,0:T(8,128)(2,1)}, bf16[8,8,2944]{2,1,0:T(8,128)(2,1)S(1)}, u32[]{:S(2)}) %copy-start) | copy-done | bytes 376856
  21.1 4.3 %mixer.1 = (f32[32,512]{1,0:T(8,128)}, f32[32,512]{1,0:T(8,128)}, f32[32,320]{1,0:T(8,128)}) custom-call(bf16[64,2944]{1,0:T(8,128)(2,1)} %bitcast.6, f32[1,20]{1,0:T(1,128)} %bitcast.7, f32[1,20]{1,0:T(1,128)} %bitcast.8, f32[1,20]{1,0:T(1,128)} %bitcast.9, f32[1,1280]{1,0:T(1,128)} %reshape.33.refs_4_, bf16[1280,320]{1,0:T(8,128)(2,1)} %copy.23.refs_5_, ...), custom_call_target="tpu_custom_call" | custom-call | tf_op jit(solution)/shard_map/mixer/pallas_call | solution.py:159
  25.4 0.0 collective-permute-start
  25.4 1.5 %collective-permute-done.refs_1_ = f32[32,512]{1,0:T(8,128)S(1)} collective-permute-done((f32[32,512]{1,0:T(8,128)}, f32[32,512]{1,0:T(8,128)S(1)}, u32[]{:S(2)}, u32[]{:S(2)}) %collective-permute-start) | collective-permute-done | bytes 65568 | tf_op jit(solution)/shard_map/ppermute | solution.py:371
  26.9 0.6 %copy-done.6 = f32[32,512]{1,0:T(8,128)} copy-done((f32[32,512]{1,0:T(8,128)}, f32[32,512]{1,0:T(8,128)S(1)}, u32[]{:S(2)}) %copy-start.6) | copy-done | bytes 65560
  27.5 1.6 %hidden.1 = bf16[8,32,320]{2,1,0:T(8,128)(2,1)} custom-call(f32[32,512]{1,0:T(8,128)} %get-tuple-element.8.refs_0_.info_ref, f32[32,512]{1,0:T(8,128)} %copy-done.6, f32[32,320]{1,0:T(8,128)} %get-tuple-element.10.refs_2_), custom_call_target="tpu_custom_call" | custom-call | tf_op jit(solution)/shard_map/hidden/pallas_call | solution.py:186
  29.1 3.7 %all-to-all-start.1 = ((bf16[8,32,320]{2,1,0:T(8,128)(2,1)}), bf16[8,32,320]{2,1,0:T(8,128)(2,1)S(1)}, u32[]{:S(2)}, u32[]{:S(2)}) async-start(bf16[8,32,320]{2,1,0:T(8,128)(2,1)} %hidden.1), calls=%async_computation.1 | async-start | bytes 393216 | tf_op jit(solution)/shard_map/all_to_all | solution.py:381
  32.9 0.0 copy-done.4
  32.9 0.1 collective-permute-start.2
  32.9 0.0 copy-done.1
  33.0 1.4 %copy.24.own_ref = bf16[2560,196]{1,0:T(8,128)(2,1)} copy(bf16[2560,196]{0,1:T(8,128)(2,1)S(1)} %copy-done.1) | data formatting | bytes 2007040 | tf_op args[12]
  34.4 0.0 copy-done.7
  34.4 0.7 %reshape.34.gain_ref = f32[8,320]{1,0:T(8,128)} reshape(f32[2560]{0:T(1024)S(1)} %copy-done.7) | data formatting | bytes 20480 | tf_op jit(solution)/shard_map/reshape | solution.py:250
  35.1 0.0 collective-permute-done.1
  35.1 1.4 %copy.25.other_ref = bf16[2560,196]{1,0:T(8,128)(2,1)} copy(bf16[2560,196]{0,1:T(8,128)(2,1)S(1)} %collective-permute-done.1) | data formatting | bytes 2007040 | tf_op jit(solution)/shard_map/ppermute | solution.py:361
  36.5 0.0 collective-permute-done.2.other_mask_ref
  36.5 4.6 %all-to-all-done.1.h_ref = bf16[8,32,320]{2,1,0:T(8,128)(2,1)S(1)} async-done(((bf16[8,32,320]{2,1,0:T(8,128)(2,1)}), bf16[8,32,320]{2,1,0:T(8,128)(2,1)S(1)}, u32[]{:S(2)}, u32[]{:S(2)}) %all-to-all-start.1) | async-done | bytes 163872 | tf_op jit(solution)/shard_map/all_to_all | solution.py:381
  41.1 0.0 copy-done.5
  41.1 0.7 %copy-done.3 = bf16[8,32,320]{2,1,0:T(8,128)(2,1)} copy-done((bf16[8,32,320]{2,1,0:T(8,128)(2,1)}, bf16[8,32,320]{2,1,0:T(8,128)(2,1)S(1)}, u32[]{:S(2)}) %copy-start.3) | copy-done | bytes 163864
  41.8 3.2 %head.1 = f32[8,4,128]{2,1,0:T(4,128)} custom-call(bf16[8,32,320]{2,1,0:T(8,128)(2,1)} %copy-done.3, f32[8,320]{1,0:T(8,128)} %reshape.34.gain_ref, bf16[2560,196]{1,0:T(8,128)(2,1)} %copy.24.own_ref, bf16[2560,196]{1,0:T(8,128)(2,1)} %copy.25.other_ref, s32[96,196]{1,0:T(8,128)} %own_mask_ref.1, s32[96,196]{1,0:T(8,128)} %copy-done.5, ...), custom_call_target="tpu_custom_call" | custom-call | tf_op jit(solution)/shard_map/head/pallas_call | solution.py:245
  45.1 10.5 %all_to_all.15.stats_ref = f32[8,4,128]{2,1,0:T(4,128)} all-to-all(f32[8,4,128]{2,1,0:T(4,128)} %head.1), channel_id=1, replica_groups=mesh['groups'=2,'seq'=8,'vocab'=2] {'seq'}, dimensions={0} | all-to-all | bytes 32768 | tf_op jit(solution)/shard_map/all_to_all | solution.py:388
  55.5 1.5 %combine.1 = f32[4,1]{1,0:T(4,128)} custom-call(f32[8,4,128]{2,1,0:T(4,128)} %all_to_all.15.stats_ref), custom_call_target="tpu_custom_call" | custom-call | tf_op jit(solution)/shard_map/combine/pallas_call | solution.py:268
  57.0 1.3 %reduce = f32[4]{0:T(128)} reduce(f32[4,1]{1,0:T(4,128)} %combine.1, f32[]{:T(128)} %constant.9), dimensions={1}, to_apply=%pallas_call.25.reduce_sub_computation | reduce | bytes 36 | tf_op jit(solution)/shard_map/combine/pallas_call | solution.py:268
  (6 shorter events, 0.0 us)
Async XLA Ops:
  0.0 10.3 %copy-start.2 = (bf16[1280,320]{0,1:T(8,128)(2,1)S(1)}, bf16[1280,320]{0,1:T(8,128)(2,1)}, u32[]{:S(2)}) copy-start(bf16[1280,320]{0,1:T(8,128)(2,1)} %param.25) | copy-start | bytes 2457604
  1.7 18.6 %all-to-all-start = ((bf16[8,8,2944]{2,1,0:T(8,128)(2,1)}), bf16[8,8,2944]{2,1,0:T(8,128)(2,1)S(1)}, u32[]{:S(2)}, u32[]{:S(2)}) async-start(bf16[8,8,2944]{2,1,0:T(8,128)(2,1)} %pack.1), calls=%async_computation | async-start | bytes 753664 | tf_op jit(solution)/shard_map/all_to_all | solution.py:366
  9.0 26.1 %collective-permute-start.1 = (bf16[2560,196]{0,1:T(8,128)(2,1)}, bf16[2560,196]{0,1:T(8,128)(2,1)S(1)}, u32[]{:S(2)}, u32[]{:S(2)}) collective-permute-start(bf16[2560,196]{0,1:T(8,128)(2,1)} %param.28), channel_id=1, source_target_pairs={{0,1},{1,0},{2,3},{3,2},{4,5},{5,4},{6,7},{7,6},{8,9},{9,8},{10,11... | collective-permute-start | bytes 3010568 | tf_op jit(solution)/shard_map/ppermute | solution.py:361
  11.5 21.3 %copy-start.4 = (s32[96,196]{1,0:T(8,128)S(1)}, s32[96,196]{1,0:T(8,128)}, u32[]{:S(2)}) copy-start(s32[96,196]{1,0:T(8,128)} %own_mask_ref.1) | copy-start | bytes 225796
  11.5 21.4 %copy-start.1 = (bf16[2560,196]{0,1:T(8,128)(2,1)S(1)}, bf16[2560,196]{0,1:T(8,128)(2,1)}, u32[]{:S(2)}) copy-start(bf16[2560,196]{0,1:T(8,128)(2,1)} %param.28) | copy-start | bytes 3010564
  20.3 0.8 %copy-start = (bf16[8,8,2944]{2,1,0:T(8,128)(2,1)}, bf16[8,8,2944]{2,1,0:T(8,128)(2,1)S(1)}, u32[]{:S(2)}) copy-start(bf16[8,8,2944]{2,1,0:T(8,128)(2,1)S(1)} %all-to-all-done) | copy-start | bytes 1130500
  25.4 1.5 %collective-permute-start = (f32[32,512]{1,0:T(8,128)}, f32[32,512]{1,0:T(8,128)S(1)}, u32[]{:S(2)}, u32[]{:S(2)}) collective-permute-start(f32[32,512]{1,0:T(8,128)} %get-tuple-element.9), channel_id=1, source_target_pairs={{0,1},{1,0},{2,3},{3,2},{4,5},{5,4},{6,7},{7,6},{8,9},{9,8},{10,11... | collective-permute-start | bytes 196616 | tf_op jit(solution)/shard_map/ppermute | solution.py:371
  26.9 0.6 %copy-start.6 = (f32[32,512]{1,0:T(8,128)}, f32[32,512]{1,0:T(8,128)S(1)}, u32[]{:S(2)}) copy-start(f32[32,512]{1,0:T(8,128)S(1)} %collective-permute-done.refs_1_) | copy-start | bytes 196612
  29.1 5.3 %copy-start.7 = (f32[2560]{0:T(1024)S(1)}, f32[2560]{0:T(1024)}, u32[]{:S(2)}) copy-start(f32[2560]{0:T(1024)} %param.27) | copy-start | bytes 30724
  29.1 12.0 %all-to-all-start.1 = ((bf16[8,32,320]{2,1,0:T(8,128)(2,1)}), bf16[8,32,320]{2,1,0:T(8,128)(2,1)S(1)}, u32[]{:S(2)}, u32[]{:S(2)}) async-start(bf16[8,32,320]{2,1,0:T(8,128)(2,1)} %hidden.1), calls=%async_computation.1 | async-start | bytes 393216 | tf_op jit(solution)/shard_map/all_to_all | solution.py:381
  32.9 3.6 %collective-permute-start.2 = (s32[96,196]{1,0:T(8,128)S(1)}, s32[96,196]{1,0:T(8,128)S(1)}, u32[]{:S(2)}, u32[]{:S(2)}) collective-permute-start(s32[96,196]{1,0:T(8,128)S(1)} %copy-done.4), channel_id=1, source_target_pairs={{0,1},{1,0},{2,3},{3,2},{4,5},{5,4},{6,7},{7,6},{8,9},{9,8},{10,11... | collective-permute-start | bytes 225800 | tf_op jit(solution)/shard_map/ppermute | solution.py:362
  36.5 4.6 %copy-start.5 = (s32[96,196]{1,0:T(8,128)}, s32[96,196]{1,0:T(8,128)S(1)}, u32[]{:S(2)}) copy-start(s32[96,196]{1,0:T(8,128)S(1)} %collective-permute-done.2.other_mask_ref) | copy-start | bytes 225796
  41.1 0.7 %copy-start.3 = (bf16[8,32,320]{2,1,0:T(8,128)(2,1)}, bf16[8,32,320]{2,1,0:T(8,128)(2,1)S(1)}, u32[]{:S(2)}) copy-start(bf16[8,32,320]{2,1,0:T(8,128)(2,1)S(1)} %all-to-all-done.1.h_ref) | copy-start | bytes 491524

commit v2 on v1

--- a/solution.py
+++ b/solution.py
@@ -13,6 +13,10 @@
 NEG = -1e30
 IDS = 64
 VMEM = pltpu.VMEM
+
+
+def grant(mebibytes):
+    return pltpu.CompilerParams(vmem_limit_bytes=mebibytes << 20)
 
 
 def dims(shape):
@@ -161,6 +165,7 @@
         out_shape=(sums, sums, jax.ShapeDtypeStruct((half, width), F32)),
         in_specs=[whole, whole, whole, pl.BlockSpec(memory_space=pltpu.SMEM), whole, whole, whole],
         scratch_shapes=[VMEM((rows, channels), BF16)],
+        compiler_params=grant(8),
         name="mixer",
     )(
         x, bias.reshape(1, heads), decay.reshape(1, heads), skip.reshape(1, heads),
@@ -186,6 +191,7 @@
     return pl.pallas_call(
         kernel,
         out_shape=jax.ShapeDtypeStruct((count,) + kept.shape, BF16),
+        compiler_params=grant(4),
         name="hidden",
     )(mine, theirs, kept)
 
@@ -246,6 +252,7 @@
         head_kernel,
         out_shape=jax.ShapeDtypeStruct((count, rows // count, LANES), F32),
         in_specs=[whole] * 7,
+        compiler_params=grant(12),
         name="head",
     )(h, gain.reshape(count, width), own, other, own_mask, other_mask, info)
 
@@ -260,13 +267,20 @@
     for k in range(count):
         total = total + stats_ref[k, :, 1:2] * jnp.exp(stats_ref[k, :, 0:1] - top)
         picked = picked + stats_ref[k, :, 2:3]
-    out_ref[...] = jnp.log(total) + top - picked
+    losses = jnp.broadcast_to(jnp.log(total) + top - picked, (top.shape[0], LANES))
+    row = lax.broadcasted_iota(jnp.int32, losses.shape, 0)
+    lane = lax.broadcasted_iota(jnp.int32, losses.shape, 1)
+    flat = jnp.sum(jnp.where(row == lane, losses, 0.0), axis=0, keepdims=True)
+    out_ref[...] = flat[:, 0 : out_ref.shape[1]]
 
 
 def combine(stats):
     own = stats.shape[1]
     out = pl.pallas_call(
-        combine_kernel, out_shape=jax.ShapeDtypeStruct((own, 1), F32), name="combine"
+        combine_kernel,
+        out_shape=jax.ShapeDtypeStruct((1, own), F32),
+        compiler_params=grant(2),
+        name="combine",
     )(stats)
     return out.reshape(own)
 

time: 58.9 us -> 49 us (0.83)
  Pallas kernels: 12.4 us -> 6.84 us
  local copies, waits for them, and re-layouts: 8.19 us -> 3.57 us
  waiting for transfers between devices: 14.9 us -> 17.2 us
  other arithmetic: 1.29 us -> 0 us
  blocking collectives: 10.5 us -> 9.52 us
    unnamed x18, local copies, waits for them, and re-layouts: 4.79 us -> 1.25 us
    pallas_call x1, Pallas kernels: 3.24 us -> 0.83 us  [head(): pl.pallas_call(head_kernel, out_shape=jax.ShapeDtypeStruct((count, rows /...]
    pallas_call x1, Pallas kernels: 4.31 us -> 2.83 us  [mixer(): pl.pallas_call(kernel, out_shape=(sums, sums, jax.ShapeDtypeStruct((half,...]
    all_to_all x1, waiting for transfers between devices: 4.63 us -> 5.93 us  [shards(): full = lax.all_to_all(spread, 'seq', 0, 0, tiled=True)]
    pallas_call x1 -> x0, other arithmetic: 1.29 us -> none  [combine(): pl.pallas_call(combine_kernel, out_shape=jax.ShapeDtypeStruct((own, 1), F...]
    all_to_all x1, waiting for transfers between devices: 8.76 us -> 9.97 us  [shards(): gathered = lax.all_to_all(packed, 'seq', 0, 0, tiled=True)]
    all_to_all x1, blocking collectives: 10.5 us -> 9.52 us  [shards(): placed = lax.all_to_all(stats, 'seq', 0, 0, tiled=True)]
    pallas_call x1, Pallas kernels: 1.64 us -> 0.78 us  [hidden_rows(): pl.pallas_call(kernel, out_shape=jax.ShapeDtypeStruct((count,) + kept.sha...]
  transfers between devices with their start and end apart: 5 -> 5, of which waited for: 3 -> 3; matrix products, arithmetic and copies ran while one was open for 10% -> 7% of each run, Pallas kernels for 10% -> 7%
where the time goes in v2:
time: 49 us; the launch traced here: 48.5 us
  waiting for transfers between devices  17.2 us (35%)
  starting transfers between devices  11.3 us (23%)
  blocking collectives  9.52 us (19%)
  Pallas kernels  6.84 us (14%)
  local copies, waits for them, and re-layouts  3.57 us (7%)
    all_to_all x1, waiting for transfers between devices, shards(): gathered = lax.all_to_all(packed, 'seq', 0, 0, tiled=True)  9.97 us
    all_to_all x1, blocking collectives, shards(): placed = lax.all_to_all(stats, 'seq', 0, 0, tiled=True)  9.52 us
    all_to_all x1, starting transfers between devices, shards(): gathered = lax.all_to_all(packed, 'seq', 0, 0, tiled=True)  7.4 us
    all_to_all x1, waiting for transfers between devices, shards(): full = lax.all_to_all(spread, 'seq', 0, 0, tiled=True)  5.93 us
    all_to_all x1, starting transfers between devices, shards(): full = lax.all_to_all(spread, 'seq', 0, 0, tiled=True)  3.75 us
    pallas_call x1, Pallas kernels, mixer(): pl.pallas_call(kernel, out_shape=(sums, sums, jax.ShapeDtypeStruct((half,...  2.83 us
    pallas_call x1, Pallas kernels, pack(): pl.pallas_call(pack_kernel, out_shape=jax.ShapeDtypeStruct((count, rows,...  1.7 us
    ppermute x1, local copies, waits for them, and re-layouts, shards(): other_weight = lax.ppermute(head_weight, 'vocab', swap)  1.54 us
  transfers between devices with their start and end apart: 5, of which 3 were waited for; matrix products, arithmetic and copies ran while one was open for 7% of the time, Pallas kernels for 7%

profile of v2, /device:TPU:0, one launch (start us, length us, event | category | flops | bytes accessed | tf_op | source)
XLA Modules:
  0.0 48.5 jit_solution(703147730008500502)
XLA Ops:
  0.0 1.7 %pack.1 = bf16[8,8,2944]{2,1,0:T(8,128)(2,1)} custom-call(bf16[8,1280]{1,0:T(8,128)(2,1)} %ssm_ref.1, bf16[8,1280]{1,0:T(8,128)(2,1)} %gate_ref.1, bf16[8,128]{1,0:T(8,128)(2,1)} %b_ref.1, bf16[8,128]{1,0:T(8,128)(2,1)} %c_ref.1, f32[8,20]{1,0:T(8,128)} %raw_ref.1, s32[1,8]{1,0:T(1,128)} %bitcast.11, s32[1,8]{1,0:T(1,128)} %bitcast.12), custom_call_target="tpu_custom_call" | custom-call | tf_op jit(solution)/shard_map/pack/pallas_call | solution.py:58
  1.7 0.0 copy-start.4
  1.7 7.4 %all-to-all-start = ((bf16[8,8,2944]{2,1,0:T(8,128)(2,1)}), bf16[8,8,2944]{2,1,0:T(8,128)(2,1)S(1)}, u32[]{:S(2)}, u32[]{:S(2)}) async-start(bf16[8,8,2944]{2,1,0:T(8,128)(2,1)} %pack.1), calls=%async_computation | async-start | bytes 753664 | tf_op jit(solution)/shard_map/all_to_all | solution.py:380
  9.1 0.0 collective-permute-start.1
  9.1 0.7 %reshape.33.refs_4_ = f32[1,1280]{1,0:T(1,128)S(1)} reshape(f32[1280]{0:T(1024)} %param.24) | data formatting | bytes 10240 | tf_op jit(solution)/shard_map/reshape | solution.py:172
  9.8 0.0 copy-done.6
  9.8 0.6 %copy.20.refs_5_ = bf16[1280,320]{1,0:T(8,128)(2,1)S(1)} copy(bf16[1280,320]{0,1:T(8,128)(2,1)S(1)} %copy-done.6) | data formatting | bytes 1638400 | tf_op args[9]
  10.5 0.0 copy-start
  10.5 0.0 copy-start.5
  10.5 10.0 %all-to-all-done = bf16[8,8,2944]{2,1,0:T(8,128)(2,1)S(1)} async-done(((bf16[8,8,2944]{2,1,0:T(8,128)(2,1)}), bf16[8,8,2944]{2,1,0:T(8,128)(2,1)S(1)}, u32[]{:S(2)}, u32[]{:S(2)}) %all-to-all-start) | async-done | bytes 376864 | tf_op jit(solution)/shard_map/all_to_all | solution.py:380
  20.5 0.0 copy-done.1
  20.5 0.0 copy-done.2
  20.5 0.0 copy-done.3
  20.5 0.0 copy-done.4
  20.5 2.8 %mixer.1 = (f32[32,512]{1,0:T(8,128)S(1)}, f32[32,512]{1,0:T(8,128)S(1)}, f32[32,320]{1,0:T(8,128)S(1)}) custom-call(bf16[64,2944]{1,0:T(8,128)(2,1)S(1)} %bitcast.7, f32[1,20]{1,0:T(1,128)S(1)} %bitcast.8, f32[1,20]{1,0:T(1,128)S(1)} %bitcast.9, f32[1,20]{1,0:T(1,128)S(1)} %bitcast.10, f32[1,1280]{1,0:T(1,128)S(1)} %reshape.33.refs_4_, ...), custom_call_target="tpu_custom_call" | custom-call | tf_op jit(solution)/shard_map/mixer/pallas_call | solution.py:163
  23.3 0.1 collective-permute-start
  23.4 1.2 %collective-permute-done.refs_1_ = f32[32,512]{1,0:T(8,128)S(1)} collective-permute-done((f32[32,512]{1,0:T(8,128)S(1)}, f32[32,512]{1,0:T(8,128)S(1)}, u32[]{:S(2)}, u32[]{:S(2)}) %collective-permute-start) | collective-permute-done | bytes 65568 | tf_op jit(solution)/shard_map/ppermute | solution.py:385
  24.6 0.8 %hidden.1 = bf16[8,32,320]{2,1,0:T(8,128)(2,1)} custom-call(f32[32,512]{1,0:T(8,128)S(1)} %get-tuple-element.8.refs_0_.info_ref, f32[32,512]{1,0:T(8,128)S(1)} %collective-permute-done.refs_1_, f32[32,320]{1,0:T(8,128)S(1)} %get-tuple-element.10.refs_2_), custom_call_target="tpu_custom_call" | custom-call | tf_op jit(solution)/shard_map/hidden/pallas_call | solution.py:191
  25.4 3.7 %all-to-all-start.1 = ((bf16[8,32,320]{2,1,0:T(8,128)(2,1)}), bf16[8,32,320]{2,1,0:T(8,128)(2,1)S(1)}, u32[]{:S(2)}, u32[]{:S(2)}) async-start(bf16[8,32,320]{2,1,0:T(8,128)(2,1)} %hidden.1), calls=%async_computation.1 | async-start | bytes 393216 | tf_op jit(solution)/shard_map/all_to_all | solution.py:395
  29.2 0.0 copy-done
  29.2 0.1 collective-permute-start.2
  29.3 0.0 copy-done.5
  29.3 0.6 %copy.21.own_ref = bf16[2560,196]{1,0:T(8,128)(2,1)S(1)} copy(bf16[2560,196]{0,1:T(8,128)(2,1)S(1)} %copy-done.5) | data formatting | bytes 2007040 | tf_op args[12]
  29.9 0.0 copy-done.7
  29.9 0.1 reshape.34.gain_ref
  30.0 0.0 collective-permute-done.1
  30.0 1.5 %copy.22.other_ref = bf16[2560,196]{1,0:T(8,128)(2,1)S(1)} copy(bf16[2560,196]{0,1:T(8,128)(2,1)} %collective-permute-done.1) | data formatting | bytes 2007040 | tf_op jit(solution)/shard_map/ppermute | solution.py:375
  31.5 0.0 collective-permute-done.2.other_mask_ref
  31.5 5.9 %all-to-all-done.1.h_ref = bf16[8,32,320]{2,1,0:T(8,128)(2,1)S(1)} async-done(((bf16[8,32,320]{2,1,0:T(8,128)(2,1)}), bf16[8,32,320]{2,1,0:T(8,128)(2,1)S(1)}, u32[]{:S(2)}, u32[]{:S(2)}) %all-to-all-start.1) | async-done | bytes 163872 | tf_op jit(solution)/shard_map/all_to_all | solution.py:395
  37.5 0.8 %head.1 = f32[8,4,128]{2,1,0:T(4,128)S(1)} custom-call(bf16[8,32,320]{2,1,0:T(8,128)(2,1)S(1)} %all-to-all-done.1.h_ref, f32[8,320]{1,0:T(8,128)S(1)} %reshape.34.gain_ref, bf16[2560,196]{1,0:T(8,128)(2,1)S(1)} %copy.21.own_ref, bf16[2560,196]{1,0:T(8,128)(2,1)S(1)} %copy.22.other_ref, s32[96,196]{1,0:T(8,128)S(1)} %copy-done, ...), custom_call_target="tpu_custom_call" | custom-call | tf_op jit(solution)/shard_map/head/pallas_call | solution.py:251
  38.3 9.5 %all_to_all.15.stats_ref = f32[8,4,128]{2,1,0:T(4,128)S(1)} all-to-all(f32[8,4,128]{2,1,0:T(4,128)S(1)} %head.1), channel_id=1, replica_groups=mesh['groups'=2,'seq'=8,'vocab'=2] {'seq'}, dimensions={0} | all-to-all | bytes 32768 | tf_op jit(solution)/shard_map/all_to_all | solution.py:402
  47.8 0.7 %combine.1 = f32[1,4]{1,0:T(1,128)} custom-call(f32[8,4,128]{2,1,0:T(4,128)S(1)} %all_to_all.15.stats_ref), custom_call_target="tpu_custom_call" | custom-call | tf_op jit(solution)/shard_map/combine/pallas_call | solution.py:279
  (5 shorter events, 0.0 us)
Async XLA Ops:
  0.0 9.8 %copy-start.6 = (bf16[1280,320]{0,1:T(8,128)(2,1)S(1)}, bf16[1280,320]{0,1:T(8,128)(2,1)}, u32[]{:S(2)}) copy-start(bf16[1280,320]{0,1:T(8,128)(2,1)} %param.25) | copy-start | bytes 2457604
  1.7 18.8 %copy-start.1 = (bf16[64,320]{1,0:T(8,128)(2,1)S(1)}, bf16[64,320]{1,0:T(8,128)(2,1)}, u32[]{:S(2)}) copy-start(bf16[64,320]{1,0:T(8,128)(2,1)} %refs_6_.1) | copy-start | bytes 122884
  1.7 18.8 %copy-start.2 = (f32[20]{0:T(128)S(1)}, f32[20]{0:T(128)}, u32[]{:S(2)}) copy-start(f32[20]{0:T(128)} %param.21) | copy-start | bytes 244
  1.7 18.8 %copy-start.3 = (f32[20]{0:T(128)S(1)}, f32[20]{0:T(128)}, u32[]{:S(2)}) copy-start(f32[20]{0:T(128)} %param.22) | copy-start | bytes 244
  1.7 18.8 %copy-start.4 = (f32[20]{0:T(128)S(1)}, f32[20]{0:T(128)}, u32[]{:S(2)}) copy-start(f32[20]{0:T(128)} %param.23) | copy-start | bytes 244
  1.7 18.7 %all-to-all-start = ((bf16[8,8,2944]{2,1,0:T(8,128)(2,1)}), bf16[8,8,2944]{2,1,0:T(8,128)(2,1)S(1)}, u32[]{:S(2)}, u32[]{:S(2)}) async-start(bf16[8,8,2944]{2,1,0:T(8,128)(2,1)} %pack.1), calls=%async_computation | async-start | bytes 753664 | tf_op jit(solution)/shard_map/all_to_all | solution.py:380
  9.1 20.8 %collective-permute-start.1 = (bf16[2560,196]{0,1:T(8,128)(2,1)}, bf16[2560,196]{0,1:T(8,128)(2,1)}, u32[]{:S(2)}, u32[]{:S(2)}) collective-permute-start(bf16[2560,196]{0,1:T(8,128)(2,1)} %param.28), channel_id=1, source_target_pairs={{0,1},{1,0},{2,3},{3,2},{4,5},{5,4},{6,7},{7,6},{8,9},{9,8},{10,11... | collective-permute-start | bytes 3010568 | tf_op jit(solution)/shard_map/ppermute | solution.py:375
  10.5 18.7 %copy-start = (s32[96,196]{1,0:T(8,128)S(1)}, s32[96,196]{1,0:T(8,128)}, u32[]{:S(2)}) copy-start(s32[96,196]{1,0:T(8,128)} %own_mask_ref.1) | copy-start | bytes 225796
  10.5 18.8 %copy-start.5 = (bf16[2560,196]{0,1:T(8,128)(2,1)S(1)}, bf16[2560,196]{0,1:T(8,128)(2,1)}, u32[]{:S(2)}) copy-start(bf16[2560,196]{0,1:T(8,128)(2,1)} %param.28) | copy-start | bytes 3010564
  23.3 1.3 %collective-permute-start = (f32[32,512]{1,0:T(8,128)S(1)}, f32[32,512]{1,0:T(8,128)S(1)}, u32[]{:S(2)}, u32[]{:S(2)}) collective-permute-start(f32[32,512]{1,0:T(8,128)S(1)} %get-tuple-element.9), channel_id=1, source_target_pairs={{0,1},{1,0},{2,3},{3,2},{4,5},{5,4},{6,7},{7,6},{8,9},{9,8},{10,11... | collective-permute-start | bytes 196616 | tf_op jit(solution)/shard_map/ppermute | solution.py:385
  25.4 4.4 %copy-start.7 = (f32[2560]{0:T(1024)S(1)}, f32[2560]{0:T(1024)}, u32[]{:S(2)}) copy-start(f32[2560]{0:T(1024)} %param.27) | copy-start | bytes 30724
  25.4 12.0 %all-to-all-start.1 = ((bf16[8,32,320]{2,1,0:T(8,128)(2,1)}), bf16[8,32,320]{2,1,0:T(8,128)(2,1)S(1)}, u32[]{:S(2)}, u32[]{:S(2)}) async-start(bf16[8,32,320]{2,1,0:T(8,128)(2,1)} %hidden.1), calls=%async_computation.1 | async-start | bytes 393216 | tf_op jit(solution)/shard_map/all_to_all | solution.py:395
  29.2 2.3 %collective-permute-start.2 = (s32[96,196]{1,0:T(8,128)S(1)}, s32[96,196]{1,0:T(8,128)S(1)}, u32[]{:S(2)}, u32[]{:S(2)}) collective-permute-start(s32[96,196]{1,0:T(8,128)S(1)} %copy-done), channel_id=1, source_target_pairs={{0,1},{1,0},{2,3},{3,2},{4,5},{5,4},{6,7},{7,6},{8,9},{9,8},{10,11... | collective-permute-start | bytes 225800 | tf_op jit(solution)/shard_map/ppermute | solution.py:376

commit v3 on v2

--- a/solution.py
+++ b/solution.py
@@ -19,8 +19,12 @@
     return pltpu.CompilerParams(vmem_limit_bytes=mebibytes << 20)
 
 
-def dims(shape):
-    return (((len(shape) - 1,), (0,)), ((), ()))
+def turn(seq):
+    return (seq // 2) % 2
+
+
+def circles(count):
+    return [[2 * s + (w + turn(s)) % 2 for s in range(count)] for w in range(2)]
 
 
 def pack_kernel(ssm_ref, gate_ref, b_ref, c_ref, raw_ref, ids_ref, targets_ref, out_ref):
@@ -66,7 +70,7 @@
     seq_rows, x_ref, bias_ref, decay_ref, skip_ref, gain_ref, weight_ref, residual_ref,
     mine_ref, theirs_ref, kept_ref, unit_ref,
 ):
-    core = lax.axis_index("vocab")
+    mine = lax.axis_index("vocab") + turn(lax.axis_index("seq"))
     rows = x_ref.shape[0]
     heads = bias_ref.shape[1]
     channels = gain_ref.shape[1]
@@ -100,7 +104,7 @@
     own = seq_rows // 2
     side = r64 // half
     place = r64 - side * half
-    which = jnp.where(side == 0, core, 1 - core)
+    which = (mine + side + turn(place // own)) % 2
     source = (place // own) * seq_rows + which * own + place % own
     order = (c64 == source).astype(BF16)
 
@@ -174,14 +178,16 @@
 
 
 def hidden_kernel(features, mine_ref, theirs_ref, kept_ref, out_ref):
-    count, _, width = out_ref.shape
+    count, half, _ = out_ref.shape
+    width = kept_ref.shape[1]
     start = mine_ref.shape[1] - LANES
     squares = mine_ref[:, start : start + 1] + theirs_ref[:, start : start + 1]
     scale = lax.rsqrt(squares / features + EPS)
     sums = mine_ref[:, 0:width] + theirs_ref[:, 0:width]
-    hidden = (kept_ref[...] + sums * scale).astype(BF16)
-    for k in range(count):
-        out_ref[k] = hidden
+    hidden = (kept_ref[...] + sums * scale).astype(BF16).astype(F32)
+    paired = jnp.concatenate([hidden[0:half], hidden[half:]], axis=1).astype(BF16)
+    for k in range(count):
+        out_ref[k] = paired
 
 
 def hidden_rows(count, features, mine, theirs, kept):
@@ -190,7 +196,7 @@
 
     return pl.pallas_call(
         kernel,
-        out_shape=jax.ShapeDtypeStruct((count,) + kept.shape, BF16),
+        out_shape=jax.ShapeDtypeStruct((count, kept.shape[0] // 2, 2 * kept.shape[1]), BF16),
         compiler_params=grant(4),
         name="hidden",
     )(mine, theirs, kept)
@@ -201,17 +207,21 @@
 ):
     core = lax.axis_index("vocab")
     block = lax.axis_index("seq") * 2
-    count, rows, width = h_ref.shape
+    count, half, width = h_ref.shape
+    rows, width = 2 * half, width // 2
     features = count * width
     squares = jnp.zeros((rows, width), F32)
-    for k in range(count):
-        part = h_ref[k].astype(F32)
+    parts = []
+    for k in range(count):
+        pair = h_ref[k].astype(F32)
+        part = jnp.concatenate([pair[:, 0:width], pair[:, width:]], axis=0)
+        parts.append(part)
         squares = squares + part * part
     scale = lax.rsqrt(jnp.sum(squares, axis=1, keepdims=True) / features + EPS)
     entries = own_ref.shape[1]
     logits = [jnp.zeros((rows, entries), F32), jnp.zeros((rows, entries), F32)]
     for k in range(count):
-        final = (h_ref[k].astype(F32) * scale * gain_ref[k : k + 1, :]).astype(BF16)
+        final = (parts[k] * scale * gain_ref[k : k + 1, :]).astype(BF16)
         span = slice(k * width, (k + 1) * width)
         for i, ref in enumerate((own_ref, other_ref)):
             logits[i] = logits[i] + jnp.dot(final, ref[span, :], preferred_element_type=F32)
@@ -246,15 +256,15 @@
 
 
 def head(h, gain, own, other, own_mask, other_mask, info):
-    count, rows, width = h.shape
+    count, half, width = h.shape
     whole = pl.BlockSpec(memory_space=VMEM)
     return pl.pallas_call(
         head_kernel,
-        out_shape=jax.ShapeDtypeStruct((count, rows // count, LANES), F32),
+        out_shape=jax.ShapeDtypeStruct((count, 2 * half // count, LANES), F32),
         in_specs=[whole] * 7,
         compiler_params=grant(12),
         name="head",
-    )(h, gain.reshape(count, width), own, other, own_mask, other_mask, info)
+    )(h, gain.reshape(count, width // 2), own, other, own_mask, other_mask, info)
 
 
 def combine_kernel(stats_ref, out_ref):
@@ -372,6 +382,14 @@
     features = 2 * channels
     small = count * rows <= LANES // 2
     swap = [(0, 1), (1, 0)]
+    both = ("seq", "vocab")
+
+    def exchange(a):
+        if small:
+            groups = circles(count)
+            return lax.all_to_all(a, both, 0, 0, tiled=True, axis_index_groups=groups)
+        return lax.all_to_all(a, "seq", 0, 0, tiled=True)
+
     other_weight = lax.ppermute(head_weight, "vocab", swap)
     other_mask = lax.ppermute(mask_table, "vocab", swap)
     packed = (pack if small else wide_pack)(
@@ -392,14 +410,14 @@
         scale = lax.rsqrt(sums[:, start : start + 1] / features + EPS)
         hidden = (kept + sums[:, 0:width] * scale).astype(BF16)
         spread = jnp.broadcast_to(hidden[None], (count,) + hidden.shape)
-    full = lax.all_to_all(spread, "seq", 0, 0, tiled=True)
+    full = exchange(spread)
     if small:
         stats = head(full, final_gain, head_weight, other_weight, mask_table, other_mask, mine)
     else:
         stats = wide_head(
             full, final_gain, head_weight, other_weight, mask_table, other_mask, mine
         )
-    placed = lax.all_to_all(stats, "seq", 0, 0, tiled=True)
+    placed = exchange(stats)
     return combine(placed) if small else wide_combine(placed)
 
 

time: 49 us -> 47.7 us (0.973)
  waiting for transfers between devices: 17.2 us -> 16.2 us
  blocking collectives: 9.52 us -> 8.96 us
    all_to_all x1, waiting for transfers between devices: 5.93 us -> 4.95 us  [exchange(): return lax.all_to_all(a, both, 0, 0, tiled=True, axis_index_groups=groups)]
    all_to_all x1, blocking collectives: 9.52 us -> 8.96 us  [exchange(): return lax.all_to_all(a, both, 0, 0, tiled=True, axis_index_groups=groups)]
  transfers between devices with their start and end apart: 5 -> 5, of which waited for: 3 -> 3; matrix products, arithmetic and copies ran while one was open for 7% -> 7% of each run, Pallas kernels for 7% -> 8%
where the time goes in v3:
time: 47.7 us; the launch traced here: 47.2 us
  waiting for transfers between devices  16.2 us (34%)
  starting transfers between devices  11.4 us (24%)
  blocking collectives  8.96 us (19%)
  Pallas kernels  6.95 us (15%)
  local copies, waits for them, and re-layouts  3.56 us (7%)
    all_to_all x1, waiting for transfers between devices, shards(): gathered = lax.all_to_all(packed, 'seq', 0, 0, tiled=True)  9.97 us
    all_to_all x1, blocking collectives, exchange(): return lax.all_to_all(a, both, 0, 0, tiled=True, axis_index_groups=groups)  8.96 us
    all_to_all x1, starting transfers between devices, shards(): gathered = lax.all_to_all(packed, 'seq', 0, 0, tiled=True)  7.4 us
    all_to_all x1, waiting for transfers between devices, exchange(): return lax.all_to_all(a, both, 0, 0, tiled=True, axis_index_groups=groups)  4.95 us
    all_to_all x1, starting transfers between devices, exchange(): return lax.all_to_all(a, both, 0, 0, tiled=True, axis_index_groups=groups)  3.51 us
    pallas_call x1, Pallas kernels, mixer(): pl.pallas_call(kernel, out_shape=(sums, sums, jax.ShapeDtypeStruct((half,...  2.84 us
    pallas_call x1, Pallas kernels, pack(): pl.pallas_call(pack_kernel, out_shape=jax.ShapeDtypeStruct((count, rows,...  1.7 us
    ppermute x1, local copies, waits for them, and re-layouts, shards(): other_weight = lax.ppermute(head_weight, 'vocab', swap)  1.54 us
  transfers between devices with their start and end apart: 5, of which 3 were waited for; matrix products, arithmetic and copies ran while one was open for 7% of the time, Pallas kernels for 8%

profile of v3, /device:TPU:0, one launch (start us, length us, event | category | flops | bytes accessed | tf_op | source)
XLA Modules:
  0.0 47.2 jit_solution(17184226204479783504)
XLA Ops:
  0.0 1.7 %pack.1 = bf16[8,8,2944]{2,1,0:T(8,128)(2,1)} custom-call(bf16[8,1280]{1,0:T(8,128)(2,1)} %ssm_ref.1, bf16[8,1280]{1,0:T(8,128)(2,1)} %gate_ref.1, bf16[8,128]{1,0:T(8,128)(2,1)} %b_ref.1, bf16[8,128]{1,0:T(8,128)(2,1)} %c_ref.1, f32[8,20]{1,0:T(8,128)} %raw_ref.1, s32[1,8]{1,0:T(1,128)} %bitcast.11, s32[1,8]{1,0:T(1,128)} %bitcast.12), custom_call_target="tpu_custom_call" | custom-call | tf_op jit(solution)/shard_map/pack/pallas_call | solution.py:62
  1.7 0.0 copy-start.4
  1.7 7.4 %all-to-all-start = ((bf16[8,8,2944]{2,1,0:T(8,128)(2,1)}), bf16[8,8,2944]{2,1,0:T(8,128)(2,1)S(1)}, u32[]{:S(2)}, u32[]{:S(2)}) async-start(bf16[8,8,2944]{2,1,0:T(8,128)(2,1)} %pack.1), calls=%async_computation | async-start | bytes 753664 | tf_op jit(solution)/shard_map/all_to_all | solution.py:398
  9.1 0.0 collective-permute-start.1
  9.1 0.7 %reshape.33.refs_4_ = f32[1,1280]{1,0:T(1,128)S(1)} reshape(f32[1280]{0:T(1024)} %param.24) | data formatting | bytes 10240 | tf_op jit(solution)/shard_map/reshape | solution.py:176
  9.8 0.0 copy-done.6
  9.8 0.6 %copy.20.refs_5_ = bf16[1280,320]{1,0:T(8,128)(2,1)S(1)} copy(bf16[1280,320]{0,1:T(8,128)(2,1)S(1)} %copy-done.6) | data formatting | bytes 1638400 | tf_op args[9]
  10.5 0.0 copy-start
  10.5 0.0 copy-start.5
  10.5 10.0 %all-to-all-done = bf16[8,8,2944]{2,1,0:T(8,128)(2,1)S(1)} async-done(((bf16[8,8,2944]{2,1,0:T(8,128)(2,1)}), bf16[8,8,2944]{2,1,0:T(8,128)(2,1)S(1)}, u32[]{:S(2)}, u32[]{:S(2)}) %all-to-all-start) | async-done | bytes 376864 | tf_op jit(solution)/shard_map/all_to_all | solution.py:398
  20.5 0.0 copy-done.1
  20.5 0.0 copy-done.2
  20.5 0.0 copy-done.3
  20.5 0.0 copy-done.4
  20.5 2.8 %mixer.1 = (f32[32,512]{1,0:T(8,128)S(1)}, f32[32,512]{1,0:T(8,128)S(1)}, f32[32,320]{1,0:T(8,128)S(1)}) custom-call(bf16[64,2944]{1,0:T(8,128)(2,1)S(1)} %bitcast.7, f32[1,20]{1,0:T(1,128)S(1)} %bitcast.8, f32[1,20]{1,0:T(1,128)S(1)} %bitcast.9, f32[1,20]{1,0:T(1,128)S(1)} %bitcast.10, f32[1,1280]{1,0:T(1,128)S(1)} %reshape.33.refs_4_, ...), custom_call_target="tpu_custom_call" | custom-call | tf_op jit(solution)/shard_map/mixer/pallas_call | solution.py:167
  23.3 0.1 collective-permute-start
  23.4 1.2 %collective-permute-done.refs_1_ = f32[32,512]{1,0:T(8,128)S(1)} collective-permute-done((f32[32,512]{1,0:T(8,128)S(1)}, f32[32,512]{1,0:T(8,128)S(1)}, u32[]{:S(2)}, u32[]{:S(2)}) %collective-permute-start) | collective-permute-done | bytes 65568 | tf_op jit(solution)/shard_map/ppermute | solution.py:403
  24.6 0.8 %hidden.1 = bf16[8,16,640]{2,1,0:T(8,128)(2,1)} custom-call(f32[32,512]{1,0:T(8,128)S(1)} %get-tuple-element.8.refs_0_.info_ref, f32[32,512]{1,0:T(8,128)S(1)} %collective-permute-done.refs_1_, f32[32,320]{1,0:T(8,128)S(1)} %get-tuple-element.10.refs_2_), custom_call_target="tpu_custom_call" | custom-call | tf_op jit(solution)/shard_map/hidden/pallas_call | solution.py:197
  25.5 3.5 %all-to-all-start.1 = ((bf16[8,16,640]{2,1,0:T(8,128)(2,1)}), bf16[8,16,640]{2,1,0:T(8,128)(2,1)S(1)}, u32[]{:S(2)}, u32[]{:S(2)}) async-start(bf16[8,16,640]{2,1,0:T(8,128)(2,1)} %hidden.1), calls=%async_computation.1 | async-start | bytes 327680 | tf_op jit(solution)/shard_map/all_to_all | solution.py:390
  29.0 0.0 copy-done
  29.0 0.4 collective-permute-start.2
  29.4 0.0 copy-done.5
  29.4 0.6 %copy.21.own_ref = bf16[2560,196]{1,0:T(8,128)(2,1)S(1)} copy(bf16[2560,196]{0,1:T(8,128)(2,1)S(1)} %copy-done.5) | data formatting | bytes 2007040 | tf_op args[12]
  30.0 0.0 copy-done.7
  30.0 0.1 reshape.34.gain_ref
  30.1 0.0 collective-permute-done.1
  30.1 1.5 %copy.22.other_ref = bf16[2560,196]{1,0:T(8,128)(2,1)S(1)} copy(bf16[2560,196]{0,1:T(8,128)(2,1)} %collective-permute-done.1) | data formatting | bytes 2007040 | tf_op jit(solution)/shard_map/ppermute | solution.py:393
  31.6 0.0 collective-permute-done.2.other_mask_ref
  31.7 4.9 %all-to-all-done.1.h_ref = bf16[8,16,640]{2,1,0:T(8,128)(2,1)S(1)} async-done(((bf16[8,16,640]{2,1,0:T(8,128)(2,1)}), bf16[8,16,640]{2,1,0:T(8,128)(2,1)S(1)}, u32[]{:S(2)}, u32[]{:S(2)}) %all-to-all-start.1) | async-done | bytes 163872 | tf_op jit(solution)/shard_map/all_to_all | solution.py:390
  36.6 0.9 %head.1 = f32[8,4,128]{2,1,0:T(4,128)S(1)} custom-call(bf16[8,16,640]{2,1,0:T(8,128)(2,1)S(1)} %all-to-all-done.1.h_ref, f32[8,320]{1,0:T(8,128)S(1)} %reshape.34.gain_ref, bf16[2560,196]{1,0:T(8,128)(2,1)S(1)} %copy.21.own_ref, bf16[2560,196]{1,0:T(8,128)(2,1)S(1)} %copy.22.other_ref, s32[96,196]{1,0:T(8,128)S(1)} %copy-done, ...), custom_call_target="tpu_custom_call" | custom-call | tf_op jit(solution)/shard_map/head/pallas_call | solution.py:261
  37.5 9.0 %all_to_all.15.stats_ref = f32[8,4,128]{2,1,0:T(4,128)S(1)} all-to-all(f32[8,4,128]{2,1,0:T(4,128)S(1)} %head.1), channel_id=1, replica_groups={{0,2,5,7,8,10,13,15},{1,3,4,6,9,11,12,14},{16,18,21,23,24,26,29,31},{17..., dimensions={0} | all-to-all | bytes 32768 | tf_op jit(solution)/shard_map/all_to_all | solution.py:390
  46.5 0.7 %combine.1 = f32[1,4]{1,0:T(1,128)} custom-call(f32[8,4,128]{2,1,0:T(4,128)S(1)} %all_to_all.15.stats_ref), custom_call_target="tpu_custom_call" | custom-call | tf_op jit(solution)/shard_map/combine/pallas_call | solution.py:289
  (5 shorter events, 0.0 us)
Async XLA Ops:
  0.0 9.8 %copy-start.6 = (bf16[1280,320]{0,1:T(8,128)(2,1)S(1)}, bf16[1280,320]{0,1:T(8,128)(2,1)}, u32[]{:S(2)}) copy-start(bf16[1280,320]{0,1:T(8,128)(2,1)} %param.25) | copy-start | bytes 2457604
  1.7 18.8 %copy-start.1 = (bf16[64,320]{1,0:T(8,128)(2,1)S(1)}, bf16[64,320]{1,0:T(8,128)(2,1)}, u32[]{:S(2)}) copy-start(bf16[64,320]{1,0:T(8,128)(2,1)} %refs_6_.1) | copy-start | bytes 122884
  1.7 18.8 %copy-start.2 = (f32[20]{0:T(128)S(1)}, f32[20]{0:T(128)}, u32[]{:S(2)}) copy-start(f32[20]{0:T(128)} %param.21) | copy-start | bytes 244
  1.7 18.8 %copy-start.3 = (f32[20]{0:T(128)S(1)}, f32[20]{0:T(128)}, u32[]{:S(2)}) copy-start(f32[20]{0:T(128)} %param.22) | copy-start | bytes 244
  1.7 18.8 %copy-start.4 = (f32[20]{0:T(128)S(1)}, f32[20]{0:T(128)}, u32[]{:S(2)}) copy-start(f32[20]{0:T(128)} %param.23) | copy-start | bytes 244
  1.7 18.7 %all-to-all-start = ((bf16[8,8,2944]{2,1,0:T(8,128)(2,1)}), bf16[8,8,2944]{2,1,0:T(8,128)(2,1)S(1)}, u32[]{:S(2)}, u32[]{:S(2)}) async-start(bf16[8,8,2944]{2,1,0:T(8,128)(2,1)} %pack.1), calls=%async_computation | async-start | bytes 753664 | tf_op jit(solution)/shard_map/all_to_all | solution.py:398
  9.1 21.0 %collective-permute-start.1 = (bf16[2560,196]{0,1:T(8,128)(2,1)}, bf16[2560,196]{0,1:T(8,128)(2,1)}, u32[]{:S(2)}, u32[]{:S(2)}) collective-permute-start(bf16[2560,196]{0,1:T(8,128)(2,1)} %param.28), channel_id=1, source_target_pairs={{0,1},{1,0},{2,3},{3,2},{4,5},{5,4},{6,7},{7,6},{8,9},{9,8},{10,11... | collective-permute-start | bytes 3010568 | tf_op jit(solution)/shard_map/ppermute | solution.py:393
  10.5 18.5 %copy-start = (s32[96,196]{1,0:T(8,128)S(1)}, s32[96,196]{1,0:T(8,128)}, u32[]{:S(2)}) copy-start(s32[96,196]{1,0:T(8,128)} %own_mask_ref.1) | copy-start | bytes 225796
  10.5 18.9 %copy-start.5 = (bf16[2560,196]{0,1:T(8,128)(2,1)S(1)}, bf16[2560,196]{0,1:T(8,128)(2,1)}, u32[]{:S(2)}) copy-start(bf16[2560,196]{0,1:T(8,128)(2,1)} %param.28) | copy-start | bytes 3010564
  23.3 1.3 %collective-permute-start = (f32[32,512]{1,0:T(8,128)S(1)}, f32[32,512]{1,0:T(8,128)S(1)}, u32[]{:S(2)}, u32[]{:S(2)}) collective-permute-start(f32[32,512]{1,0:T(8,128)S(1)} %get-tuple-element.9), channel_id=1, source_target_pairs={{0,1},{1,0},{2,3},{3,2},{4,5},{5,4},{6,7},{7,6},{8,9},{9,8},{10,11... | collective-permute-start | bytes 196616 | tf_op jit(solution)/shard_map/ppermute | solution.py:403
  25.5 4.5 %copy-start.7 = (f32[2560]{0:T(1024)S(1)}, f32[2560]{0:T(1024)}, u32[]{:S(2)}) copy-start(f32[2560]{0:T(1024)} %param.27) | copy-start | bytes 30724
  25.5 11.1 %all-to-all-start.1 = ((bf16[8,16,640]{2,1,0:T(8,128)(2,1)}), bf16[8,16,640]{2,1,0:T(8,128)(2,1)S(1)}, u32[]{:S(2)}, u32[]{:S(2)}) async-start(bf16[8,16,640]{2,1,0:T(8,128)(2,1)} %hidden.1), calls=%async_computation.1 | async-start | bytes 327680 | tf_op jit(solution)/shard_map/all_to_all | solution.py:390
  29.0 2.6 %collective-permute-start.2 = (s32[96,196]{1,0:T(8,128)S(1)}, s32[96,196]{1,0:T(8,128)S(1)}, u32[]{:S(2)}, u32[]{:S(2)}) collective-permute-start(s32[96,196]{1,0:T(8,128)S(1)} %copy-done), channel_id=1, source_target_pairs={{0,1},{1,0},{2,3},{3,2},{4,5},{5,4},{6,7},{7,6},{8,9},{9,8},{10,11... | collective-permute-start | bytes 225800 | tf_op jit(solution)/shard_map/ppermute | solution.py:394

commit v4 on v3

--- a/solution.py
+++ b/solution.py
@@ -11,8 +11,13 @@
 EPS = 1e-05
 LANES = 128
 NEG = -1e30
-IDS = 64
+INFO = 60
+PARAMS = 64
 VMEM = pltpu.VMEM
+
+
+def times_transposed(a, b):
+    return lax.dot_general(a, b, (((1,), (1,)), ((), ())), preferred_element_type=F32)
 
 
 def grant(mebibytes):
@@ -27,27 +32,40 @@
     return [[2 * s + (w + turn(s)) % 2 for s in range(count)] for w in range(2)]
 
 
-def pack_kernel(ssm_ref, gate_ref, b_ref, c_ref, raw_ref, ids_ref, targets_ref, out_ref):
+def thirds(a):
+    high = a.astype(BF16).astype(F32)
+    middle = (a - high).astype(BF16).astype(F32)
+    return high, middle, a - high - middle
+
+
+def pack_kernel(
+    ssm_ref, gate_ref, b_ref, c_ref, raw_ref, bias_ref, decay_ref, skip_ref, ids_ref, targets_ref,
+    out_ref,
+):
     count, rows, _ = out_ref.shape
     channels = ssm_ref.shape[1]
     state = b_ref.shape[1]
     heads = raw_ref.shape[1]
-    raw = raw_ref[...]
-    high = raw.astype(BF16)
-    rest = raw - high.astype(F32)
-    middle = rest.astype(BF16)
-    low = (rest - middle.astype(F32)).astype(BF16)
-    ids = ids_ref[...].astype(F32)
-    targets = targets_ref[...]
-    upper = lax.shift_right_logical(targets, 8)
-    under = (targets - upper * 256).astype(F32)
-    parts = [high.astype(F32), middle.astype(F32), low.astype(F32)]
-    parts.append(jnp.zeros((rows, IDS - 3 * heads), F32))
-    for part in (ids, upper.astype(F32), under):
-        parts.append(jnp.broadcast_to(part, (rows, rows)))
-    parts.append(jnp.zeros((rows, LANES - IDS - 3 * rows), F32))
+    edge = 2 * channels
+    parts = list(thirds(jax.nn.softplus(raw_ref[...] + bias_ref[...])))
+    row = lax.broadcasted_iota(jnp.int32, (rows, rows), 0)
+    diagonal = row == lax.broadcasted_iota(jnp.int32, (rows, rows), 1)
+
+    def upright(a):
+        wide = jnp.broadcast_to(a.astype(F32), (rows, rows))
+        return jnp.sum(jnp.where(diagonal, wide, 0.0), axis=1, keepdims=True)
+
+    targets = upright(targets_ref[...])
+    upper = jnp.floor(targets / 256.0)
+    parts += [upright(ids_ref[...]), upper, targets - upper * 256.0]
+    parts.append(jnp.zeros((rows, PARAMS - INFO - 3), F32))
+    params = list(thirds(-jnp.exp(decay_ref[...]))) + list(thirds(skip_ref[...]))
+    place = lax.broadcasted_iota(jnp.int32, (rows, heads), 0)
+    table = jnp.zeros((rows, heads), F32)
+    for k, part in enumerate(params):
+        table = jnp.where(place == k, part, table)
+    parts += [table, jnp.zeros((rows, LANES - PARAMS - heads), F32)]
     misc = jnp.concatenate(parts, axis=1).astype(BF16)
-    edge = 2 * channels
     for k in range(count):
         out_ref[k, :, 0:channels] = ssm_ref[...]
         out_ref[k, :, channels:edge] = gate_ref[...]
@@ -56,32 +74,38 @@
         out_ref[k, :, edge + 2 * state :] = misc
 
 
-def pack(count, ssm, gate, b, c, raw, ids, targets):
+def pack(count, ssm, gate, b, c, raw, bias, decay, skip, ids, targets):
     rows, channels = ssm.shape
+    heads = bias.shape[0]
     width = 2 * channels + 2 * b.shape[1] + LANES
     return pl.pallas_call(
         pack_kernel,
         out_shape=jax.ShapeDtypeStruct((count, rows, width), BF16),
         name="pack",
-    )(ssm, gate, b, c, raw, ids.reshape(1, rows), targets.reshape(1, rows))
+    )(
+        ssm, gate, b, c, raw, bias.reshape(1, heads), decay.reshape(1, heads),
+        skip.reshape(1, heads), ids.reshape(1, rows), targets.reshape(1, rows),
+    )
 
 
 def mixer_kernel(
-    seq_rows, x_ref, bias_ref, decay_ref, skip_ref, gain_ref, weight_ref, residual_ref,
+    seq_rows, heads, x_ref, gain_ref, weight_ref, residual_ref,
     mine_ref, theirs_ref, kept_ref, unit_ref,
 ):
     mine = lax.axis_index("vocab") + turn(lax.axis_index("seq"))
     rows = x_ref.shape[0]
-    heads = bias_ref.shape[1]
     channels = gain_ref.shape[1]
     state = (x_ref.shape[1] - LANES - 2 * channels) // 2
     edge = 2 * channels
     half = rows // 2
     size = channels // heads
-    misc = x_ref[:, edge + 2 * state :].astype(F32)
-    raw = misc[:, 0:heads] + misc[:, heads : 2 * heads] + misc[:, 2 * heads : 3 * heads]
-    step = jax.nn.softplus(raw + bias_ref[...])
-    rate = step * -jnp.exp(decay_ref[...])
+    packed = x_ref[:, edge + 2 * state :]
+    misc = packed.astype(F32)
+    step = misc[:, 0:heads] + misc[:, heads : 2 * heads] + misc[:, 2 * heads : 3 * heads]
+    params = pltpu.roll(misc[0:8], LANES - PARAMS, 1)
+    decay = params[0:1] + params[1:2] + params[2:3]
+    gains = params[3:4] + params[4:5] + params[5:6]
+    rate = step * decay[:, 0:heads]
     r64 = lax.broadcasted_iota(jnp.int32, (rows, rows), 0)
     c64 = lax.broadcasted_iota(jnp.int32, (rows, rows), 1)
     tri = (c64 <= r64).astype(F32)
@@ -94,7 +118,7 @@
     b = x_ref[:, edge : edge + state]
     c = x_ref[:, edge + state : edge + 2 * state]
     twice = jnp.concatenate([b, b], axis=0)
-    corr = lax.dot_general(c, twice, (((1,), (1,)), ((), ())), preferred_element_type=F32)
+    corr = times_transposed(c, twice)
     lane = lax.broadcasted_iota(jnp.int32, (rows, LANES), 1)
     row = lax.broadcasted_iota(jnp.int32, (rows, LANES), 0)
     first = lane < size
@@ -123,24 +147,21 @@
         stacked = jnp.concatenate([jnp.where(first, v, none), jnp.where(first, none, v)], axis=0)
         y = jnp.dot(high, stacked, preferred_element_type=F32)
         y = y + jnp.dot(low, stacked, preferred_element_type=F32)
-        skip = jnp.where(first_row, skip_ref[0, left], skip_ref[0, right])
+        skip = jnp.where(
+            first_row, gains[:, left : left + 1], gains[:, right : right + 1]
+        )
         mixed = y + skip * v.astype(F32)
         gate = x_ref[:, channels + j * LANES : channels + (j + 1) * LANES].astype(F32)
         gated = (mixed * (gate / (1.0 + jnp.exp(-gate)))).astype(BF16)
         moved = jnp.dot(order, gated, preferred_element_type=F32)
         squares = squares + moved * moved
         unit_ref[:, span] = (moved * gain_ref[:, span]).astype(BF16)
-    partial = jnp.dot(unit_ref[...], weight_ref[...], preferred_element_type=F32)
+    partial = times_transposed(unit_ref[...], weight_ref[...])
     kept_ref[...] = jnp.dot(order[0:half], residual_ref[...], preferred_element_type=F32)
 
-    at_row = row % seq_rows
-    info = jnp.zeros((rows, LANES), F32)
-    for k in range(3):
-        column = jnp.sum(
-            jnp.where(lane == IDS + k * seq_rows + at_row, misc, 0.0), axis=1, keepdims=True
-        )
-        info = jnp.where(lane == k + 1, column, info)
-    info = jnp.dot(order, info.astype(BF16), preferred_element_type=F32)
+    info = pltpu.roll(
+        jnp.dot(order, packed, preferred_element_type=F32), LANES + 1 - INFO, 1
+    )
     total = jnp.sum(squares, axis=1, keepdims=True)
     info = jnp.where(lane == 0, total, info)
     width = partial.shape[1]
@@ -151,10 +172,9 @@
     theirs_ref[:, start:] = info[half:]
 
 
-def mixer(x, seq_rows, bias, decay, skip, gain, weight, residual):
+def mixer(x, seq_rows, heads, gain, weight, residual):
     rows = x.shape[0]
-    heads = bias.shape[0]
-    channels = gain.shape[0]
+    channels = gain.shape[1]
     width = weight.shape[1]
     total = (width + LANES - 1) // LANES * LANES + LANES
     half = rows // 2
@@ -162,19 +182,16 @@
     whole = pl.BlockSpec(memory_space=VMEM)
 
     def kernel(*refs):
-        mixer_kernel(seq_rows, *refs)
+        mixer_kernel(seq_rows, heads, *refs)
 
     return pl.pallas_call(
         kernel,
         out_shape=(sums, sums, jax.ShapeDtypeStruct((half, width), F32)),
-        in_specs=[whole, whole, whole, pl.BlockSpec(memory_space=pltpu.SMEM), whole, whole, whole],
+        in_specs=[whole] * 4,
         scratch_shapes=[VMEM((rows, channels), BF16)],
         compiler_params=grant(8),
         name="mixer",
-    )(
-        x, bias.reshape(1, heads), decay.reshape(1, heads), skip.reshape(1, heads),
-        gain.reshape(1, channels), weight, residual,
-    )
+    )(x, gain, weight.T, residual)
 
 
 def hidden_kernel(features, mine_ref, theirs_ref, kept_ref, out_ref):
@@ -203,7 +220,8 @@
 
 
 def head_kernel(
-    h_ref, gain_ref, own_ref, other_ref, own_mask_ref, other_mask_ref, info_ref, out_ref
+    h_ref, gain_ref, own_ref, o0_ref, o1_ref, o2_ref, o3_ref, own_mask_ref, other_mask_ref,
+    info_ref, out_ref,
 ):
     core = lax.axis_index("vocab")
     block = lax.axis_index("seq") * 2
@@ -218,13 +236,16 @@
         parts.append(part)
         squares = squares + part * part
     scale = lax.rsqrt(jnp.sum(squares, axis=1, keepdims=True) / features + EPS)
-    entries = own_ref.shape[1]
-    logits = [jnp.zeros((rows, entries), F32), jnp.zeros((rows, entries), F32)]
-    for k in range(count):
-        final = (parts[k] * scale * gain_ref[k : k + 1, :]).astype(BF16)
-        span = slice(k * width, (k + 1) * width)
-        for i, ref in enumerate((own_ref, other_ref)):
-            logits[i] = logits[i] + jnp.dot(final, ref[span, :], preferred_element_type=F32)
+    entries = own_ref.shape[0]
+    parts = [parts[k] * scale * gain_ref[k : k + 1, :] for k in range(count)]
+    final = jnp.concatenate(parts, axis=1).astype(BF16)
+    logits = [times_transposed(final, own_ref[...])]
+    depth = features // 4
+    pieces = [
+        times_transposed(final[:, k * depth : (k + 1) * depth], ref[...])
+        for k, ref in enumerate((o0_ref, o1_ref, o2_ref, o3_ref))
+    ]
+    logits.append((pieces[0] + pieces[1]) + (pieces[2] + pieces[3]))
     states = own_mask_ref.shape[0]
     start = info_ref.shape[1] - LANES
     ids = info_ref[:, start + 1 : start + 2].astype(jnp.int32)
@@ -261,10 +282,10 @@
     return pl.pallas_call(
         head_kernel,
         out_shape=jax.ShapeDtypeStruct((count, 2 * half // count, LANES), F32),
-        in_specs=[whole] * 7,
+        in_specs=[whole] * 10,
         compiler_params=grant(12),
         name="head",
-    )(h, gain.reshape(count, width // 2), own, other, own_mask, other_mask, info)
+    )(h, gain, own.T, *(o.T for o in other), own_mask, other_mask, info)
 
 
 def combine_kernel(stats_ref, out_ref):
@@ -295,30 +316,37 @@
     return out.reshape(own)
 
 
-def wide_pack(count, ssm, gate, b, c, raw, ids, targets):
+def wide_pack(count, ssm, gate, b, c, raw, bias, decay, skip, ids, targets):
     rows = ssm.shape[0]
     heads = raw.shape[1]
-    high = lax.reduce_precision(raw, 8, 7)
-    middle = lax.reduce_precision(raw - high, 8, 7)
-    low = raw - high - middle
-    parts = [high, middle, low, jnp.zeros((rows, IDS - 3 * heads), F32)]
+
+    def split(a):
+        high = lax.reduce_precision(a, 8, 7)
+        middle = lax.reduce_precision(a - high, 8, 7)
+        return [high, middle, a - high - middle]
+
+    parts = split(jax.nn.softplus(raw + bias[None, :]))
     parts += [a.astype(F32)[:, None] for a in (ids, targets // 256, targets % 256)]
-    parts.append(jnp.zeros((rows, LANES - IDS - 3), F32))
+    parts.append(jnp.zeros((rows, PARAMS - INFO - 3), F32))
+    params = jnp.stack(split(-jnp.exp(decay)) + split(skip))
+    parts.append(jnp.pad(params, ((0, rows - 6), (0, LANES - PARAMS - heads))))
     misc = jnp.concatenate(parts, axis=1).astype(BF16)
     row = jnp.concatenate([ssm, gate, b, c, misc], axis=1)
     return jnp.broadcast_to(row[None], (count,) + row.shape)
 
 
-def wide_mixer(x, seq_rows, bias, decay, skip, gain, weight, residual):
+def wide_mixer(x, seq_rows, heads, gain, weight, residual):
     rows = x.shape[0]
-    heads, channels = bias.shape[0], gain.shape[0]
+    channels = gain.shape[1]
     state = (x.shape[1] - LANES - 2 * channels) // 2
     edge = 2 * channels
     core = lax.axis_index("vocab")
     misc = x[:, edge + 2 * state :].astype(F32)
-    raw = misc[:, 0:heads] + misc[:, heads : 2 * heads] + misc[:, 2 * heads : 3 * heads]
-    step = jax.nn.softplus(raw + bias[None, :])
-    log_cum = jnp.cumsum(step * -jnp.exp(decay)[None, :], axis=0)
+    step = misc[:, 0:heads] + misc[:, heads : 2 * heads] + misc[:, 2 * heads : 3 * heads]
+    params = misc[0:8, PARAMS : PARAMS + heads]
+    decay = params[0] + params[1] + params[2]
+    skip = params[3] + params[4] + params[5]
+    log_cum = jnp.cumsum(step * decay[None, :], axis=0)
     corr = jnp.dot(
         x[:, edge + state : edge + 2 * state],
         x[:, edge : edge + state].T,
@@ -337,11 +365,11 @@
     gated = (mixed * jax.nn.silu(x[:, channels:edge].astype(F32))).astype(BF16)
     wide = gated.astype(F32)
     squares = jnp.sum(wide * wide, axis=1, keepdims=True)
-    unit = (wide * gain[None, :]).astype(BF16)
+    unit = (wide * gain).astype(BF16)
     partial = jnp.dot(unit, weight, preferred_element_type=F32)
     width = weight.shape[1]
     start = (width + LANES - 1) // LANES * LANES
-    info = jnp.concatenate([squares, misc[:, IDS : IDS + 3]], axis=1)
+    info = jnp.concatenate([squares, misc[:, INFO : INFO + 3]], axis=1)
     sums = jnp.concatenate(
         [
             partial,
@@ -390,15 +418,28 @@
             return lax.all_to_all(a, both, 0, 0, tiled=True, axis_index_groups=groups)
         return lax.all_to_all(a, "seq", 0, 0, tiled=True)
 
-    other_weight = lax.ppermute(head_weight, "vocab", swap)
+    packed = (pack if small else wide_pack)(
+        count, ssm_input, gate_input, b_proj, readout_matrix, step_raw, step_bias, decay_log,
+        head_skip_gain, state_ids, targets,
+    )
+    if small:
+        depth = features // 4
+        other_weight = tuple(
+            lax.ppermute(head_weight[k * depth : (k + 1) * depth], "vocab", swap) for k in range(4)
+        )
+    else:
+        other_weight = lax.ppermute(head_weight, "vocab", swap)
     other_mask = lax.ppermute(mask_table, "vocab", swap)
-    packed = (pack if small else wide_pack)(
-        count, ssm_input, gate_input, b_proj, readout_matrix, step_raw, state_ids, targets
-    )
     gathered = lax.all_to_all(packed, "seq", 0, 0, tiled=True)
+    final_gain = final_gain.reshape(count, features // count)
+    norm_gain = norm_gain.reshape(1, channels)
+    if small:
+        gathered, other_weight, other_mask, final_gain = lax.optimization_barrier(
+            (gathered, other_weight, other_mask, final_gain)
+        )
     x = gathered.reshape(count * rows, packed.shape[2])
     mine, theirs, kept = (mixer if small else wide_mixer)(
-        x, rows, step_bias, decay_log, head_skip_gain, norm_gain, out_weight, residual
+        x, rows, step_bias.shape[0], norm_gain, out_weight, residual
     )
     arrived = lax.ppermute(theirs, "vocab", swap)
     if small:
@@ -427,7 +468,7 @@
     block = lax.axis_index("seq") * 2
     wide = full.transpose(1, 0, 2).reshape(rows, count * width).astype(F32)
     scale = lax.rsqrt(jnp.mean(wide * wide, axis=1, keepdims=True) + EPS)
-    final = (wide * scale * gain[None, :]).astype(BF16)
+    final = (wide * scale * gain.reshape(1, -1)).astype(BF16)
     start = info.shape[1] - LANES
     ids, upper, under = (info[:, start + k].astype(jnp.int32) for k in (1, 2, 3))
     target = upper * 256 + under

time: 47.7 us -> 46.2 us (0.969)
  blocking collectives: 8.96 us -> 19.8 us
  waiting for transfers between devices: 16.2 us -> 10.4 us
  starting transfers between devices: 11.4 us -> 8.35 us
  local copies, waits for them, and re-layouts: 3.56 us -> 1.12 us
  Pallas kernels: 6.95 us -> 6.12 us
    all_to_all x1 -> x2, blocking collectives: 8.96 us -> 19.8 us  [exchange(): return lax.all_to_all(a, both, 0, 0, tiled=True, axis_index_groups=groups)]
    all_to_all x1 -> x0, waiting for transfers between devices: 4.95 us -> none  [exchange(): return lax.all_to_all(a, both, 0, 0, tiled=True, axis_index_groups=groups)]
    all_to_all x1 -> x0, starting transfers between devices: 3.51 us -> none  [exchange(): return lax.all_to_all(a, both, 0, 0, tiled=True, axis_index_groups=groups)]
    all_to_all x1, waiting for transfers between devices: 9.97 us -> 7.3 us  [shards(): gathered = lax.all_to_all(packed, 'seq', 0, 0, tiled=True)]
    ppermute x1 -> x0, local copies, waits for them, and re-layouts: 1.54 us -> none  [shards(): other_weight = lax.ppermute(head_weight, 'vocab', swap)]
    ppermute x1, waiting for transfers between devices: 0.01 us -> 1.42 us  [shards(): other_mask = lax.ppermute(mask_table, 'vocab', swap)]
    unnamed x18 -> x12, local copies, waits for them, and re-layouts: 1.24 us -> 0.03 us
    ppermute x1 -> x4, starting transfers between devices: 0.01 us -> 1.02 us  [shards(): lax.ppermute(head_weight[k * depth:(k + 1) * depth], 'vocab', swap)]
  transfers between devices with their start and end apart: 5 -> 7, of which waited for: 3 -> 4; matrix products, arithmetic and copies ran while one was open for 7% -> 2% of each run, Pallas kernels for 8% -> 0%
where the time goes in v4:
time: 46.2 us; the launch traced here: 45.8 us
  blocking collectives  19.8 us (43%)
  waiting for transfers between devices  10.4 us (23%)
  starting transfers between devices  8.35 us (18%)
  Pallas kernels  6.12 us (13%)
  local copies, waits for them, and re-layouts  1.12 us (2%)
    all_to_all x2, blocking collectives, exchange(): return lax.all_to_all(a, both, 0, 0, tiled=True, axis_index_groups=groups)  19.8 us
    all_to_all x1, waiting for transfers between devices, shards(): gathered = lax.all_to_all(packed, 'seq', 0, 0, tiled=True)  7.3 us
    all_to_all x1, starting transfers between devices, shards(): gathered = lax.all_to_all(packed, 'seq', 0, 0, tiled=True)  7.25 us
    pallas_call x1, Pallas kernels, mixer(): pl.pallas_call(kernel, out_shape=(sums, sums, jax.ShapeDtypeStruct((half,...  2.38 us
    pallas_call x1, Pallas kernels, pack(): pl.pallas_call(pack_kernel, out_shape=jax.ShapeDtypeStruct((count, rows,...  1.73 us
    ppermute x1, waiting for transfers between devices, shards(): other_mask = lax.ppermute(mask_table, 'vocab', swap)  1.42 us
    ppermute x1, waiting for transfers between devices, shards(): arrived = lax.ppermute(theirs, 'vocab', swap)  1.24 us
    pallas_call x1, Pallas kernels, head(): pl.pallas_call(head_kernel, out_shape=jax.ShapeDtypeStruct((count, 2 * ha...  1.17 us
  transfers between devices with their start and end apart: 7, of which 4 were waited for; matrix products, arithmetic and copies ran while one was open for 2% of the time, Pallas kernels for 0%

profile of v4, /device:TPU:0, one launch (start us, length us, event | category | flops | bytes accessed | tf_op | source)
XLA Modules:
  0.0 45.8 jit_solution(16039261666953404521)
XLA Ops:
  0.0 1.7 %pack.1 = bf16[8,8,2944]{2,1,0:T(8,128)(2,1)} custom-call(bf16[8,1280]{1,0:T(8,128)(2,1)} %ssm_ref.1, bf16[8,1280]{1,0:T(8,128)(2,1)} %gate_ref.1, bf16[8,128]{1,0:T(8,128)(2,1)} %b_ref.1, bf16[8,128]{1,0:T(8,128)(2,1)} %c_ref.1, f32[8,20]{1,0:T(8,128)} %raw_ref.1, f32[1,20]{1,0:T(1,128)} %bitcast.20, f32[1,20]{1,0:T(1,128)} %bitcast.21, f32[1,20]{1,0:T(1,128)} %bitcast.22, ...), custom_call_target="tpu_custom_call" | custom-call | tf_op jit(solution)/shard_map/pack/pallas_call | solution.py:81
  1.7 7.3 %all-to-all-start = ((bf16[8,8,2944]{2,1,0:T(8,128)(2,1)}), bf16[8,8,2944]{2,1,0:T(8,128)(2,1)S(1)}, u32[]{:S(2)}, u32[]{:S(2)}) async-start(bf16[8,8,2944]{2,1,0:T(8,128)(2,1)} %pack.1), calls=%async_computation | async-start | bytes 753664 | tf_op jit(solution)/shard_map/all_to_all | solution.py:433
  9.0 0.0 copy-done
  9.0 0.0 copy-start.2
  9.0 0.0 copy-start.4
  9.0 0.0 copy-start.5
  9.0 0.0 copy-start.1
  9.0 1.0 %fusion = (bf16[640,196]{0,1:T(8,128)(2,1)}, bf16[640,196]{0,1:T(8,128)(2,1)}, bf16[640,196]{0,1:T(8,128)(2,1)}, bf16[640,196]{0,1:T(8,128)(2,1)}) fusion(bf16[2560,196]{0,1:T(8,128)(2,1)S(1)} %copy-done), kind=kLoop, calls=%fused_computation | loop fusion | bytes 2007040 | tf_op jit(solution)/shard_map/slice | solution.py:428
  10.1 0.0 collective-permute-start
  10.1 0.5 %collective-permute-start.1 = (bf16[640,196]{0,1:T(8,128)(2,1)}, bf16[640,196]{0,1:T(8,128)(2,1)S(1)}, u32[]{:S(2)}, u32[]{:S(2)}) collective-permute-start(bf16[640,196]{0,1:T(8,128)(2,1)} %get-tuple-element.27), channel_id=1, source_target_pairs={{0,1},{1,0},{2,3},{3,2},{4,5},{5,4},{6,7},{7,6},{8,9},{9,8},{10,11... | collective-permute-start | bytes 752648 | tf_op jit(solution)/shard_map/ppermute | solution.py:428
  10.6 0.0 collective-permute-start.2
  10.6 0.5 %collective-permute-start.3 = (bf16[640,196]{0,1:T(8,128)(2,1)}, bf16[640,196]{0,1:T(8,128)(2,1)S(1)}, u32[]{:S(2)}, u32[]{:S(2)}) collective-permute-start(bf16[640,196]{0,1:T(8,128)(2,1)} %get-tuple-element.25), channel_id=1, source_target_pairs={{0,1},{1,0},{2,3},{3,2},{4,5},{5,4},{6,7},{7,6},{8,9},{9,8},{10,11... | collective-permute-start | bytes 752648 | tf_op jit(solution)/shard_map/ppermute | solution.py:428
  11.1 0.0 copy-done.2
  11.1 0.0 collective-permute-start.4
  11.1 0.0 copy-done.4
  11.1 0.1 reshape.32.gain_ref
  11.2 0.0 copy-done.5
  11.2 1.4 %collective-permute-done.4.other_mask_ref = s32[96,196]{1,0:T(8,128)S(1)} collective-permute-done((s32[96,196]{1,0:T(8,128)S(1)}, s32[96,196]{1,0:T(8,128)S(1)}, u32[]{:S(2)}, u32[]{:S(2)}) %collective-permute-start.4) | collective-permute-done | bytes 75296 | tf_op jit(solution)/shard_map/ppermute | solution.py:432
  12.6 0.0 collective-permute-done
  12.6 0.0 collective-permute-done.1
  12.6 0.0 collective-permute-done.2
  12.6 0.4 collective-permute-done.3
  13.0 7.3 %all-to-all-done = bf16[8,8,2944]{2,1,0:T(8,128)(2,1)S(1)} async-done(((bf16[8,8,2944]{2,1,0:T(8,128)(2,1)}), bf16[8,8,2944]{2,1,0:T(8,128)(2,1)S(1)}, u32[]{:S(2)}, u32[]{:S(2)}) %all-to-all-start) | async-done | bytes 376864 | tf_op jit(solution)/shard_map/all_to_all | solution.py:433
  20.3 0.0 copy-done.1
  20.3 2.4 %mixer.1 = (f32[32,512]{1,0:T(8,128)S(1)}, f32[32,512]{1,0:T(8,128)S(1)}, f32[32,320]{1,0:T(8,128)S(1)}) custom-call(bf16[64,2944]{1,0:T(8,128)(2,1)S(1)} %bitcast.14, f32[1,1280]{1,0:T(1,128)S(1)} %reshape.34.refs_1_, bf16[320,1280]{1,0:T(8,128)(2,1)S(1)} %bitcast.15, bf16[64,320]{1,0:T(8,128)(2,1)S(1)} %copy-done.3), custom_call_target="tpu_custom_call" | custom-call | tf_op jit(solution)/shard_map/mixer/pallas_call | solution.py:187
  22.7 0.1 collective-permute-start.5
  22.8 1.2 %collective-permute-done.5.refs_1_ = f32[32,512]{1,0:T(8,128)S(1)} collective-permute-done((f32[32,512]{1,0:T(8,128)S(1)}, f32[32,512]{1,0:T(8,128)S(1)}, u32[]{:S(2)}, u32[]{:S(2)}) %collective-permute-start.5) | collective-permute-done | bytes 65568 | tf_op jit(solution)/shard_map/ppermute | solution.py:444
  24.0 0.2 hidden.1
  24.2 10.8 %all_to_all.15.h_ref = bf16[8,16,640]{2,1,0:T(8,128)(2,1)S(1)} all-to-all(bf16[8,16,640]{2,1,0:T(8,128)(2,1)S(1)} %hidden.1), channel_id=1, replica_groups={{0,2,5,7,8,10,13,15},{1,3,4,6,9,11,12,14},{16,18,21,23,24,26,29,31},{17..., dimensions={0} | all-to-all | bytes 327680 | tf_op jit(solution)/shard_map/all_to_all | solution.py:418
  35.0 1.2 %head.1 = f32[8,4,128]{2,1,0:T(4,128)S(1)} custom-call(bf16[8,16,640]{2,1,0:T(8,128)(2,1)S(1)} %all_to_all.15.h_ref, f32[8,320]{1,0:T(8,128)S(1)} %reshape.32.gain_ref, bf16[196,2560]{1,0:T(8,128)(2,1)S(1)} %bitcast.13, bf16[196,640]{1,0:T(8,128)(2,1)S(1)} %bitcast.16, bf16[196,640]{1,0:T(8,128)(2,1)S(1)} %bitcast.17, bf16[196,640]{1,0:T(8,128)(2,1)S(1)} %bitcast.18, ...), custom_call_target="tpu_custom_call" | custom-call | tf_op jit(solution)/shard_map/head/pallas_call | solution.py:282
  36.2 9.0 %all_to_all.16.stats_ref = f32[8,4,128]{2,1,0:T(4,128)S(1)} all-to-all(f32[8,4,128]{2,1,0:T(4,128)S(1)} %head.1), channel_id=1, replica_groups={{0,2,5,7,8,10,13,15},{1,3,4,6,9,11,12,14},{16,18,21,23,24,26,29,31},{17..., dimensions={0} | all-to-all | bytes 32768 | tf_op jit(solution)/shard_map/all_to_all | solution.py:418
  45.1 0.7 %combine.1 = f32[1,4]{1,0:T(1,128)} custom-call(f32[8,4,128]{2,1,0:T(4,128)S(1)} %all_to_all.16.stats_ref), custom_call_target="tpu_custom_call" | custom-call | tf_op jit(solution)/shard_map/combine/pallas_call | solution.py:310
  (4 shorter events, 0.0 us)
Async XLA Ops:
  0.0 9.0 %copy-start = (bf16[2560,196]{0,1:T(8,128)(2,1)S(1)}, bf16[2560,196]{0,1:T(8,128)(2,1)}, u32[]{:S(2)}) copy-start(bf16[2560,196]{0,1:T(8,128)(2,1)} %param.28) | copy-start | bytes 3010564
  1.7 18.6 %all-to-all-start = ((bf16[8,8,2944]{2,1,0:T(8,128)(2,1)}), bf16[8,8,2944]{2,1,0:T(8,128)(2,1)S(1)}, u32[]{:S(2)}, u32[]{:S(2)}) async-start(bf16[8,8,2944]{2,1,0:T(8,128)(2,1)} %pack.1), calls=%async_computation | async-start | bytes 753664 | tf_op jit(solution)/shard_map/all_to_all | solution.py:433
  9.0 2.1 %copy-start.2 = (s32[96,196]{1,0:T(8,128)S(1)}, s32[96,196]{1,0:T(8,128)}, u32[]{:S(2)}) copy-start(s32[96,196]{1,0:T(8,128)} %own_mask_ref.1) | copy-start | bytes 225796
  9.0 2.1 %copy-start.4 = (f32[2560]{0:T(1024)S(1)}, f32[2560]{0:T(1024)}, u32[]{:S(2)}) copy-start(f32[2560]{0:T(1024)} %param.27) | copy-start | bytes 30724
  9.0 2.1 %copy-start.5 = (f32[1280]{0:T(1024)S(1)}, f32[1280]{0:T(1024)}, u32[]{:S(2)}) copy-start(f32[1280]{0:T(1024)} %param.24) | copy-start | bytes 15364
  9.0 11.3 %copy-start.1 = (bf16[1280,320]{0,1:T(8,128)(2,1)S(1)}, bf16[1280,320]{0,1:T(8,128)(2,1)}, u32[]{:S(2)}) copy-start(bf16[1280,320]{0,1:T(8,128)(2,1)} %param.25) | copy-start | bytes 2457604
  10.1 10.3 %copy-start.3 = (bf16[64,320]{1,0:T(8,128)(2,1)S(1)}, bf16[64,320]{1,0:T(8,128)(2,1)}, u32[]{:S(2)}) copy-start(bf16[64,320]{1,0:T(8,128)(2,1)} %refs_3_.1) | copy-start | bytes 122884
  10.1 2.5 %collective-permute-start = (bf16[640,196]{0,1:T(8,128)(2,1)}, bf16[640,196]{0,1:T(8,128)(2,1)S(1)}, u32[]{:S(2)}, u32[]{:S(2)}) collective-permute-start(bf16[640,196]{0,1:T(8,128)(2,1)} %get-tuple-element.28), channel_id=1, source_target_pairs={{0,1},{1,0},{2,3},{3,2},{4,5},{5,4},{6,7},{7,6},{8,9},{9,8},{10,11... | collective-permute-start | bytes 752648 | tf_op jit(solution)/shard_map/ppermute | solution.py:428
  10.1 2.5 %collective-permute-start.1 = (bf16[640,196]{0,1:T(8,128)(2,1)}, bf16[640,196]{0,1:T(8,128)(2,1)S(1)}, u32[]{:S(2)}, u32[]{:S(2)}) collective-permute-start(bf16[640,196]{0,1:T(8,128)(2,1)} %get-tuple-element.27), channel_id=1, source_target_pairs={{0,1},{1,0},{2,3},{3,2},{4,5},{5,4},{6,7},{7,6},{8,9},{9,8},{10,11... | collective-permute-start | bytes 752648 | tf_op jit(solution)/shard_map/ppermute | solution.py:428
  10.6 2.0 %collective-permute-start.2 = (bf16[640,196]{0,1:T(8,128)(2,1)}, bf16[640,196]{0,1:T(8,128)(2,1)S(1)}, u32[]{:S(2)}, u32[]{:S(2)}) collective-permute-start(bf16[640,196]{0,1:T(8,128)(2,1)} %get-tuple-element.26), channel_id=1, source_target_pairs={{0,1},{1,0},{2,3},{3,2},{4,5},{5,4},{6,7},{7,6},{8,9},{9,8},{10,11... | collective-permute-start | bytes 752648 | tf_op jit(solution)/shard_map/ppermute | solution.py:428
  10.6 2.5 %collective-permute-start.3 = (bf16[640,196]{0,1:T(8,128)(2,1)}, bf16[640,196]{0,1:T(8,128)(2,1)S(1)}, u32[]{:S(2)}, u32[]{:S(2)}) collective-permute-start(bf16[640,196]{0,1:T(8,128)(2,1)} %get-tuple-element.25), channel_id=1, source_target_pairs={{0,1},{1,0},{2,3},{3,2},{4,5},{5,4},{6,7},{7,6},{8,9},{9,8},{10,11... | collective-permute-start | bytes 752648 | tf_op jit(solution)/shard_map/ppermute | solution.py:428
  11.1 1.5 %collective-permute-start.4 = (s32[96,196]{1,0:T(8,128)S(1)}, s32[96,196]{1,0:T(8,128)S(1)}, u32[]{:S(2)}, u32[]{:S(2)}) collective-permute-start(s32[96,196]{1,0:T(8,128)S(1)} %copy-done.2), channel_id=1, source_target_pairs={{0,1},{1,0},{2,3},{3,2},{4,5},{5,4},{6,7},{7,6},{8,9},{9,8},{10,11... | collective-permute-start | bytes 225800 | tf_op jit(solution)/shard_map/ppermute | solution.py:432
  22.7 1.3 %collective-permute-start.5 = (f32[32,512]{1,0:T(8,128)S(1)}, f32[32,512]{1,0:T(8,128)S(1)}, u32[]{:S(2)}, u32[]{:S(2)}) collective-permute-start(f32[32,512]{1,0:T(8,128)S(1)} %get-tuple-element.17), channel_id=1, source_target_pairs={{0,1},{1,0},{2,3},{3,2},{4,5},{5,4},{6,7},{7,6},{8,9},{9,8},{10,11... | collective-permute-start | bytes 196616 | tf_op jit(solution)/shard_map/ppermute | solution.py:444

commit v5 on v4

--- a/solution.py
+++ b/solution.py
@@ -90,7 +90,7 @@
 
 def mixer_kernel(
     seq_rows, heads, x_ref, gain_ref, weight_ref, residual_ref,
-    mine_ref, theirs_ref, kept_ref, unit_ref,
+    mine_ref, theirs_ref, kept_ref,
 ):
     mine = lax.axis_index("vocab") + turn(lax.axis_index("seq"))
     rows = x_ref.shape[0]
@@ -99,70 +99,59 @@
     edge = 2 * channels
     half = rows // 2
     size = channels // heads
-    packed = x_ref[:, edge + 2 * state :]
-    misc = packed.astype(F32)
+    r64 = lax.broadcasted_iota(jnp.int32, (rows, rows), 0)
+    c64 = lax.broadcasted_iota(jnp.int32, (rows, rows), 1)
+    own = seq_rows // 2
+    side = (r64 >= half).astype(jnp.int32)
+    place = r64 - side * half
+    seq = lax.shift_right_logical(place, own.bit_length() - 1)
+    which = (mine + side + lax.shift_right_logical(seq, 1)) & 1
+    source = place + seq * own + which * own
+    order = (c64 == source).astype(BF16)
+    causal = c64 <= source
+    moved = jnp.dot(order, x_ref[...], preferred_element_type=F32)
+
+    misc = x_ref[:, edge + 2 * state :].astype(F32)
     step = misc[:, 0:heads] + misc[:, heads : 2 * heads] + misc[:, 2 * heads : 3 * heads]
     params = pltpu.roll(misc[0:8], LANES - PARAMS, 1)
     decay = params[0:1] + params[1:2] + params[2:3]
     gains = params[3:4] + params[4:5] + params[5:6]
-    rate = step * decay[:, 0:heads]
-    r64 = lax.broadcasted_iota(jnp.int32, (rows, rows), 0)
-    c64 = lax.broadcasted_iota(jnp.int32, (rows, rows), 1)
-    tri = (c64 <= r64).astype(F32)
-    log_cum = jnp.dot(tri, rate, precision=HIGHEST, preferred_element_type=F32)
-    fill = jnp.zeros((rows, LANES - heads), F32)
-    wide_cum = jnp.concatenate([log_cum, fill], axis=1)
-    wide_step = jnp.concatenate([step, fill], axis=1)
-    cum_rows = jnp.concatenate([wide_cum, wide_cum], axis=0).T
-    step_rows = jnp.concatenate([wide_step, wide_step], axis=0).T
-    b = x_ref[:, edge : edge + state]
-    c = x_ref[:, edge + state : edge + 2 * state]
-    twice = jnp.concatenate([b, b], axis=0)
-    corr = times_transposed(c, twice)
+    rates = jnp.concatenate(thirds(step * decay[:, 0:heads]), axis=1).astype(BF16)
+    sums = jnp.concatenate([(c64 <= r64).astype(BF16), causal.astype(BF16)], axis=0)
+    cums = jnp.dot(sums, rates, preferred_element_type=F32)
+    cums = cums[:, 0:heads] + cums[:, heads : 2 * heads] + cums[:, 2 * heads :]
+    middle = cums[half - 1 : half]
+    ahead = jnp.exp(cums[rows:] - middle)
+    back = jnp.exp(middle - cums[0:rows]) * step
+    skips = jnp.broadcast_to(gains[:, 0:heads], (8, heads))
+    factors = jnp.concatenate([ahead, back, skips], axis=0)
+    factors = jnp.concatenate(thirds(factors), axis=1).astype(BF16)
+    head_row = lax.broadcasted_iota(jnp.int32, (3 * heads, channels), 0)
+    for _ in range(2):
+        head_row = jnp.where(head_row >= heads, head_row - heads, head_row)
+    from_head = lax.broadcasted_iota(jnp.int32, (3 * heads, channels), 1) - head_row * size
+    spread = ((from_head >= 0) & (from_head < size)).astype(BF16)
+    wide = jnp.dot(factors, spread, preferred_element_type=F32)
+
+    c = moved[:, edge + state : edge + 2 * state].astype(BF16)
+    corr = times_transposed(c, x_ref[:, edge : edge + state])
+    corr = jnp.where(causal, corr, 0.0)
+    high = corr.astype(BF16).astype(F32)
+    corr = jnp.concatenate([high, corr - high, high], axis=1).astype(BF16)
+    scaled = wide[rows : 2 * rows] * x_ref[:, 0:channels].astype(F32)
+    high = scaled.astype(BF16)
+    low = (scaled - high.astype(F32)).astype(BF16)
+    y = jnp.dot(corr, jnp.concatenate([high, high, low], axis=0), preferred_element_type=F32)
+    mixed = wide[0:rows] * y + wide[2 * rows : 2 * rows + 1] * moved[:, 0:channels]
+    gate = moved[:, channels:edge]
+    gated = (mixed * (gate / (1.0 + jnp.exp(-gate)))).astype(BF16).astype(F32)
+    unit = (gated * gain_ref[...]).astype(BF16)
+    partial = times_transposed(unit, weight_ref[...])
+    total = jnp.sum(gated * gated, axis=1, keepdims=True)
+    kept_ref[...] = jnp.dot(order[0:half], residual_ref[...], preferred_element_type=F32)
+
     lane = lax.broadcasted_iota(jnp.int32, (rows, LANES), 1)
-    row = lax.broadcasted_iota(jnp.int32, (rows, LANES), 0)
-    first = lane < size
-    causal = jnp.where(first, lane, lane - size) <= row
-    first_row = lax.broadcasted_iota(jnp.int32, (1, LANES), 1) < size
-
-    own = seq_rows // 2
-    side = r64 // half
-    place = r64 - side * half
-    which = (mine + side + turn(place // own)) % 2
-    source = (place // own) * seq_rows + which * own + place % own
-    order = (c64 == source).astype(BF16)
-
-    squares = jnp.zeros((rows, LANES), F32)
-    for j in range(heads // 2):
-        left, right = 2 * j, 2 * j + 1
-        span = slice(j * LANES, (j + 1) * LANES)
-        at = jnp.where(first, log_cum[:, left : left + 1], log_cum[:, right : right + 1])
-        back = jnp.where(first_row, cum_rows[left : left + 1], cum_rows[right : right + 1])
-        sizes = jnp.where(first_row, step_rows[left : left + 1], step_rows[right : right + 1])
-        weights = jnp.exp(jnp.where(causal, at - back, NEG)) * (corr * sizes)
-        high = weights.astype(BF16)
-        low = (weights - high.astype(F32)).astype(BF16)
-        v = x_ref[:, span]
-        none = jnp.zeros_like(v)
-        stacked = jnp.concatenate([jnp.where(first, v, none), jnp.where(first, none, v)], axis=0)
-        y = jnp.dot(high, stacked, preferred_element_type=F32)
-        y = y + jnp.dot(low, stacked, preferred_element_type=F32)
-        skip = jnp.where(
-            first_row, gains[:, left : left + 1], gains[:, right : right + 1]
-        )
-        mixed = y + skip * v.astype(F32)
-        gate = x_ref[:, channels + j * LANES : channels + (j + 1) * LANES].astype(F32)
-        gated = (mixed * (gate / (1.0 + jnp.exp(-gate)))).astype(BF16)
-        moved = jnp.dot(order, gated, preferred_element_type=F32)
-        squares = squares + moved * moved
-        unit_ref[:, span] = (moved * gain_ref[:, span]).astype(BF16)
-    partial = times_transposed(unit_ref[...], weight_ref[...])
-    kept_ref[...] = jnp.dot(order[0:half], residual_ref[...], preferred_element_type=F32)
-
-    info = pltpu.roll(
-        jnp.dot(order, packed, preferred_element_type=F32), LANES + 1 - INFO, 1
-    )
-    total = jnp.sum(squares, axis=1, keepdims=True)
+    info = pltpu.roll(moved[:, edge + 2 * state :], LANES + 1 - INFO, 1)
     info = jnp.where(lane == 0, total, info)
     width = partial.shape[1]
     start = mine_ref.shape[1] - LANES
@@ -188,7 +177,6 @@
         kernel,
         out_shape=(sums, sums, jax.ShapeDtypeStruct((half, width), F32)),
         in_specs=[whole] * 4,
-        scratch_shapes=[VMEM((rows, channels), BF16)],
         compiler_params=grant(8),
         name="mixer",
     )(x, gain, weight.T, residual)

time: 46.2 us -> 45.1 us (0.976)
  Pallas kernels: 6.12 us -> 5.04 us
    pallas_call x1, Pallas kernels: 2.38 us -> 1.29 us  [mixer(): pl.pallas_call(kernel, out_shape=(sums, sums, jax.ShapeDtypeStruct((half,...]
where the time goes in v5:
time: 45.1 us; the launch traced here: 44.7 us
  blocking collectives  19.8 us (44%)
  waiting for transfers between devices  10.4 us (23%)
  starting transfers between devices  8.35 us (19%)
  Pallas kernels  5.04 us (11%)
  local copies, waits for them, and re-layouts  1.12 us (2%)
    all_to_all x2, blocking collectives, exchange(): return lax.all_to_all(a, both, 0, 0, tiled=True, axis_index_groups=groups)  19.8 us
    all_to_all x1, waiting for transfers between devices, shards(): gathered = lax.all_to_all(packed, 'seq', 0, 0, tiled=True)  7.3 us
    all_to_all x1, starting transfers between devices, shards(): gathered = lax.all_to_all(packed, 'seq', 0, 0, tiled=True)  7.25 us
    pallas_call x1, Pallas kernels, pack(): pl.pallas_call(pack_kernel, out_shape=jax.ShapeDtypeStruct((count, rows,...  1.73 us
    ppermute x1, waiting for transfers between devices, shards(): other_mask = lax.ppermute(mask_table, 'vocab', swap)  1.42 us
    pallas_call x1, Pallas kernels, mixer(): pl.pallas_call(kernel, out_shape=(sums, sums, jax.ShapeDtypeStruct((half,...  1.29 us
    ppermute x1, waiting for transfers between devices, shards(): arrived = lax.ppermute(theirs, 'vocab', swap)  1.24 us
    pallas_call x1, Pallas kernels, head(): pl.pallas_call(head_kernel, out_shape=jax.ShapeDtypeStruct((count, 2 * ha...  1.17 us
  transfers between devices with their start and end apart: 7, of which 4 were waited for; matrix products, arithmetic and copies ran while one was open for 2% of the time, Pallas kernels for 0%

profile of v5, /device:TPU:0, one launch (start us, length us, event | category | flops | bytes accessed | tf_op | source)
XLA Modules:
  0.0 44.7 jit_solution(13048801109800300279)
XLA Ops:
  0.0 1.7 %pack.1 = bf16[8,8,2944]{2,1,0:T(8,128)(2,1)} custom-call(bf16[8,1280]{1,0:T(8,128)(2,1)} %ssm_ref.1, bf16[8,1280]{1,0:T(8,128)(2,1)} %gate_ref.1, bf16[8,128]{1,0:T(8,128)(2,1)} %b_ref.1, bf16[8,128]{1,0:T(8,128)(2,1)} %c_ref.1, f32[8,20]{1,0:T(8,128)} %raw_ref.1, f32[1,20]{1,0:T(1,128)} %bitcast.20, f32[1,20]{1,0:T(1,128)} %bitcast.21, f32[1,20]{1,0:T(1,128)} %bitcast.22, ...), custom_call_target="tpu_custom_call" | custom-call | tf_op jit(solution)/shard_map/pack/pallas_call | solution.py:81
  1.7 7.3 %all-to-all-start = ((bf16[8,8,2944]{2,1,0:T(8,128)(2,1)}), bf16[8,8,2944]{2,1,0:T(8,128)(2,1)S(1)}, u32[]{:S(2)}, u32[]{:S(2)}) async-start(bf16[8,8,2944]{2,1,0:T(8,128)(2,1)} %pack.1), calls=%async_computation | async-start | bytes 753664 | tf_op jit(solution)/shard_map/all_to_all | solution.py:421
  9.0 0.0 copy-done
  9.0 0.0 copy-start.2
  9.0 0.0 copy-start.4
  9.0 0.0 copy-start.5
  9.0 0.0 copy-start.1
  9.0 1.0 %fusion = (bf16[640,196]{0,1:T(8,128)(2,1)}, bf16[640,196]{0,1:T(8,128)(2,1)}, bf16[640,196]{0,1:T(8,128)(2,1)}, bf16[640,196]{0,1:T(8,128)(2,1)}) fusion(bf16[2560,196]{0,1:T(8,128)(2,1)S(1)} %copy-done), kind=kLoop, calls=%fused_computation | loop fusion | bytes 2007040 | tf_op jit(solution)/shard_map/slice | solution.py:416
  10.1 0.0 collective-permute-start
  10.1 0.5 %collective-permute-start.1 = (bf16[640,196]{0,1:T(8,128)(2,1)}, bf16[640,196]{0,1:T(8,128)(2,1)S(1)}, u32[]{:S(2)}, u32[]{:S(2)}) collective-permute-start(bf16[640,196]{0,1:T(8,128)(2,1)} %get-tuple-element.27), channel_id=1, source_target_pairs={{0,1},{1,0},{2,3},{3,2},{4,5},{5,4},{6,7},{7,6},{8,9},{9,8},{10,11... | collective-permute-start | bytes 752648 | tf_op jit(solution)/shard_map/ppermute | solution.py:416
  10.6 0.0 collective-permute-start.2
  10.6 0.5 %collective-permute-start.3 = (bf16[640,196]{0,1:T(8,128)(2,1)}, bf16[640,196]{0,1:T(8,128)(2,1)S(1)}, u32[]{:S(2)}, u32[]{:S(2)}) collective-permute-start(bf16[640,196]{0,1:T(8,128)(2,1)} %get-tuple-element.25), channel_id=1, source_target_pairs={{0,1},{1,0},{2,3},{3,2},{4,5},{5,4},{6,7},{7,6},{8,9},{9,8},{10,11... | collective-permute-start | bytes 752648 | tf_op jit(solution)/shard_map/ppermute | solution.py:416
  11.1 0.0 copy-done.2
  11.1 0.0 collective-permute-start.4
  11.1 0.0 copy-done.4
  11.1 0.1 reshape.32.gain_ref
  11.2 0.0 copy-done.5
  11.2 1.4 %collective-permute-done.4.other_mask_ref = s32[96,196]{1,0:T(8,128)S(1)} collective-permute-done((s32[96,196]{1,0:T(8,128)S(1)}, s32[96,196]{1,0:T(8,128)S(1)}, u32[]{:S(2)}, u32[]{:S(2)}) %collective-permute-start.4) | collective-permute-done | bytes 75296 | tf_op jit(solution)/shard_map/ppermute | solution.py:420
  12.6 0.0 collective-permute-done
  12.6 0.0 collective-permute-done.1
  12.6 0.0 collective-permute-done.2
  12.6 0.4 collective-permute-done.3
  13.0 7.3 %all-to-all-done = bf16[8,8,2944]{2,1,0:T(8,128)(2,1)S(1)} async-done(((bf16[8,8,2944]{2,1,0:T(8,128)(2,1)}), bf16[8,8,2944]{2,1,0:T(8,128)(2,1)S(1)}, u32[]{:S(2)}, u32[]{:S(2)}) %all-to-all-start) | async-done | bytes 376864 | tf_op jit(solution)/shard_map/all_to_all | solution.py:421
  20.3 0.0 copy-done.1
  20.3 1.3 %mixer.1 = (f32[32,512]{1,0:T(8,128)S(1)}, f32[32,512]{1,0:T(8,128)S(1)}, f32[32,320]{1,0:T(8,128)S(1)}) custom-call(bf16[64,2944]{1,0:T(8,128)(2,1)S(1)} %bitcast.14, f32[1,1280]{1,0:T(1,128)S(1)} %reshape.34.refs_1_, bf16[320,1280]{1,0:T(8,128)(2,1)S(1)} %bitcast.15, bf16[64,320]{1,0:T(8,128)(2,1)S(1)} %copy-done.3), custom_call_target="tpu_custom_call" | custom-call | tf_op jit(solution)/shard_map/mixer/pallas_call | solution.py:176
  21.6 0.1 collective-permute-start.5
  21.7 1.2 %collective-permute-done.5.refs_1_ = f32[32,512]{1,0:T(8,128)S(1)} collective-permute-done((f32[32,512]{1,0:T(8,128)S(1)}, f32[32,512]{1,0:T(8,128)S(1)}, u32[]{:S(2)}, u32[]{:S(2)}) %collective-permute-start.5) | collective-permute-done | bytes 65568 | tf_op jit(solution)/shard_map/ppermute | solution.py:432
  23.0 0.2 hidden.1
  23.1 10.8 %all_to_all.15.h_ref = bf16[8,16,640]{2,1,0:T(8,128)(2,1)S(1)} all-to-all(bf16[8,16,640]{2,1,0:T(8,128)(2,1)S(1)} %hidden.1), channel_id=1, replica_groups={{0,2,5,7,8,10,13,15},{1,3,4,6,9,11,12,14},{16,18,21,23,24,26,29,31},{17..., dimensions={0} | all-to-all | bytes 327680 | tf_op jit(solution)/shard_map/all_to_all | solution.py:406
  33.9 1.2 %head.1 = f32[8,4,128]{2,1,0:T(4,128)S(1)} custom-call(bf16[8,16,640]{2,1,0:T(8,128)(2,1)S(1)} %all_to_all.15.h_ref, f32[8,320]{1,0:T(8,128)S(1)} %reshape.32.gain_ref, bf16[196,2560]{1,0:T(8,128)(2,1)S(1)} %bitcast.13, bf16[196,640]{1,0:T(8,128)(2,1)S(1)} %bitcast.16, bf16[196,640]{1,0:T(8,128)(2,1)S(1)} %bitcast.17, bf16[196,640]{1,0:T(8,128)(2,1)S(1)} %bitcast.18, ...), custom_call_target="tpu_custom_call" | custom-call | tf_op jit(solution)/shard_map/head/pallas_call | solution.py:270
  35.1 9.0 %all_to_all.16.stats_ref = f32[8,4,128]{2,1,0:T(4,128)S(1)} all-to-all(f32[8,4,128]{2,1,0:T(4,128)S(1)} %head.1), channel_id=1, replica_groups={{0,2,5,7,8,10,13,15},{1,3,4,6,9,11,12,14},{16,18,21,23,24,26,29,31},{17..., dimensions={0} | all-to-all | bytes 32768 | tf_op jit(solution)/shard_map/all_to_all | solution.py:406
  44.1 0.7 %combine.1 = f32[1,4]{1,0:T(1,128)} custom-call(f32[8,4,128]{2,1,0:T(4,128)S(1)} %all_to_all.16.stats_ref), custom_call_target="tpu_custom_call" | custom-call | tf_op jit(solution)/shard_map/combine/pallas_call | solution.py:298
  (4 shorter events, 0.0 us)
Async XLA Ops:
  0.0 9.0 %copy-start = (bf16[2560,196]{0,1:T(8,128)(2,1)S(1)}, bf16[2560,196]{0,1:T(8,128)(2,1)}, u32[]{:S(2)}) copy-start(bf16[2560,196]{0,1:T(8,128)(2,1)} %param.28) | copy-start | bytes 3010564
  1.7 18.6 %all-to-all-start = ((bf16[8,8,2944]{2,1,0:T(8,128)(2,1)}), bf16[8,8,2944]{2,1,0:T(8,128)(2,1)S(1)}, u32[]{:S(2)}, u32[]{:S(2)}) async-start(bf16[8,8,2944]{2,1,0:T(8,128)(2,1)} %pack.1), calls=%async_computation | async-start | bytes 753664 | tf_op jit(solution)/shard_map/all_to_all | solution.py:421
  9.0 2.1 %copy-start.2 = (s32[96,196]{1,0:T(8,128)S(1)}, s32[96,196]{1,0:T(8,128)}, u32[]{:S(2)}) copy-start(s32[96,196]{1,0:T(8,128)} %own_mask_ref.1) | copy-start | bytes 225796
  9.0 2.1 %copy-start.4 = (f32[2560]{0:T(1024)S(1)}, f32[2560]{0:T(1024)}, u32[]{:S(2)}) copy-start(f32[2560]{0:T(1024)} %param.27) | copy-start | bytes 30724
  9.0 2.1 %copy-start.5 = (f32[1280]{0:T(1024)S(1)}, f32[1280]{0:T(1024)}, u32[]{:S(2)}) copy-start(f32[1280]{0:T(1024)} %param.24) | copy-start | bytes 15364
  9.0 11.3 %copy-start.1 = (bf16[1280,320]{0,1:T(8,128)(2,1)S(1)}, bf16[1280,320]{0,1:T(8,128)(2,1)}, u32[]{:S(2)}) copy-start(bf16[1280,320]{0,1:T(8,128)(2,1)} %param.25) | copy-start | bytes 2457604
  10.1 10.3 %copy-start.3 = (bf16[64,320]{1,0:T(8,128)(2,1)S(1)}, bf16[64,320]{1,0:T(8,128)(2,1)}, u32[]{:S(2)}) copy-start(bf16[64,320]{1,0:T(8,128)(2,1)} %refs_3_.1) | copy-start | bytes 122884
  10.1 2.5 %collective-permute-start = (bf16[640,196]{0,1:T(8,128)(2,1)}, bf16[640,196]{0,1:T(8,128)(2,1)S(1)}, u32[]{:S(2)}, u32[]{:S(2)}) collective-permute-start(bf16[640,196]{0,1:T(8,128)(2,1)} %get-tuple-element.28), channel_id=1, source_target_pairs={{0,1},{1,0},{2,3},{3,2},{4,5},{5,4},{6,7},{7,6},{8,9},{9,8},{10,11... | collective-permute-start | bytes 752648 | tf_op jit(solution)/shard_map/ppermute | solution.py:416
  10.1 2.5 %collective-permute-start.1 = (bf16[640,196]{0,1:T(8,128)(2,1)}, bf16[640,196]{0,1:T(8,128)(2,1)S(1)}, u32[]{:S(2)}, u32[]{:S(2)}) collective-permute-start(bf16[640,196]{0,1:T(8,128)(2,1)} %get-tuple-element.27), channel_id=1, source_target_pairs={{0,1},{1,0},{2,3},{3,2},{4,5},{5,4},{6,7},{7,6},{8,9},{9,8},{10,11... | collective-permute-start | bytes 752648 | tf_op jit(solution)/shard_map/ppermute | solution.py:416
  10.6 2.0 %collective-permute-start.2 = (bf16[640,196]{0,1:T(8,128)(2,1)}, bf16[640,196]{0,1:T(8,128)(2,1)S(1)}, u32[]{:S(2)}, u32[]{:S(2)}) collective-permute-start(bf16[640,196]{0,1:T(8,128)(2,1)} %get-tuple-element.26), channel_id=1, source_target_pairs={{0,1},{1,0},{2,3},{3,2},{4,5},{5,4},{6,7},{7,6},{8,9},{9,8},{10,11... | collective-permute-start | bytes 752648 | tf_op jit(solution)/shard_map/ppermute | solution.py:416
  10.6 2.5 %collective-permute-start.3 = (bf16[640,196]{0,1:T(8,128)(2,1)}, bf16[640,196]{0,1:T(8,128)(2,1)S(1)}, u32[]{:S(2)}, u32[]{:S(2)}) collective-permute-start(bf16[640,196]{0,1:T(8,128)(2,1)} %get-tuple-element.25), channel_id=1, source_target_pairs={{0,1},{1,0},{2,3},{3,2},{4,5},{5,4},{6,7},{7,6},{8,9},{9,8},{10,11... | collective-permute-start | bytes 752648 | tf_op jit(solution)/shard_map/ppermute | solution.py:416
  11.1 1.5 %collective-permute-start.4 = (s32[96,196]{1,0:T(8,128)S(1)}, s32[96,196]{1,0:T(8,128)S(1)}, u32[]{:S(2)}, u32[]{:S(2)}) collective-permute-start(s32[96,196]{1,0:T(8,128)S(1)} %copy-done.2), channel_id=1, source_target_pairs={{0,1},{1,0},{2,3},{3,2},{4,5},{5,4},{6,7},{7,6},{8,9},{9,8},{10,11... | collective-permute-start | bytes 225800 | tf_op jit(solution)/shard_map/ppermute | solution.py:420
  21.6 1.3 %collective-permute-start.5 = (f32[32,512]{1,0:T(8,128)S(1)}, f32[32,512]{1,0:T(8,128)S(1)}, u32[]{:S(2)}, u32[]{:S(2)}) collective-permute-start(f32[32,512]{1,0:T(8,128)S(1)} %get-tuple-element.17), channel_id=1, source_target_pairs={{0,1},{1,0},{2,3},{3,2},{4,5},{5,4},{6,7},{7,6},{8,9},{9,8},{10,11... | collective-permute-start | bytes 196616 | tf_op jit(solution)/shard_map/ppermute | solution.py:432

commit v6 on v5

--- a/solution.py
+++ b/solution.py
@@ -12,6 +12,7 @@
 LANES = 128
 NEG = -1e30
 INFO = 60
+GAP = 32
 PARAMS = 64
 VMEM = pltpu.VMEM
 
@@ -25,7 +26,7 @@
 
 
 def turn(seq):
-    return (seq // 2) % 2
+    return seq % 2
 
 
 def circles(count):
@@ -105,7 +106,7 @@
     side = (r64 >= half).astype(jnp.int32)
     place = r64 - side * half
     seq = lax.shift_right_logical(place, own.bit_length() - 1)
-    which = (mine + side + lax.shift_right_logical(seq, 1)) & 1
+    which = (mine + side + seq) & 1
     source = place + seq * own + which * own
     order = (c64 == source).astype(BF16)
     causal = c64 <= source
@@ -208,8 +209,7 @@
 
 
 def head_kernel(
-    h_ref, gain_ref, own_ref, o0_ref, o1_ref, o2_ref, o3_ref, own_mask_ref, other_mask_ref,
-    info_ref, out_ref,
+    h_ref, gain_ref, own_ref, upper_ref, lower_ref, own_mask_ref, other_mask_ref, info_ref, out_ref
 ):
     core = lax.axis_index("vocab")
     block = lax.axis_index("seq") * 2
@@ -228,12 +228,11 @@
     parts = [parts[k] * scale * gain_ref[k : k + 1, :] for k in range(count)]
     final = jnp.concatenate(parts, axis=1).astype(BF16)
     logits = [times_transposed(final, own_ref[...])]
-    depth = features // 4
-    pieces = [
-        times_transposed(final[:, k * depth : (k + 1) * depth], ref[...])
-        for k, ref in enumerate((o0_ref, o1_ref, o2_ref, o3_ref))
-    ]
-    logits.append((pieces[0] + pieces[1]) + (pieces[2] + pieces[3]))
+    depth = features // 2
+    logits.append(
+        times_transposed(final[:, :depth], upper_ref[...])
+        + times_transposed(final[:, depth:], lower_ref[...])
+    )
     states = own_mask_ref.shape[0]
     start = info_ref.shape[1] - LANES
     ids = info_ref[:, start + 1 : start + 2].astype(jnp.int32)
@@ -257,11 +256,14 @@
     for a, w, x in zip(allowed, wanted, logits):
         total = total + jnp.sum(jnp.where(a, jnp.exp(x - top), 0.0), axis=1, keepdims=True)
         picked = picked + jnp.sum(jnp.where(w, x, 0.0), axis=1, keepdims=True)
+    own = rows // count
     lane = lax.broadcasted_iota(jnp.int32, (rows, LANES), 1)
-    stats = jnp.where(lane == 0, top, jnp.where(lane == 1, total, picked))
-    own = out_ref.shape[1]
+    place = lane - (lax.broadcasted_iota(jnp.int32, (rows, LANES), 0) & (own - 1))
+    stats = jnp.where(
+        place == 0, top, jnp.where(place == GAP, total, jnp.where(place == 2 * GAP, picked, 0.0))
+    )
     for k in range(count):
-        out_ref[k] = stats[k * own : (k + 1) * own]
+        out_ref[k] = jnp.sum(stats[k * own : (k + 1) * own], axis=0, keepdims=True)
 
 
 def head(h, gain, own, other, own_mask, other_mask, info):
@@ -269,32 +271,24 @@
     whole = pl.BlockSpec(memory_space=VMEM)
     return pl.pallas_call(
         head_kernel,
-        out_shape=jax.ShapeDtypeStruct((count, 2 * half // count, LANES), F32),
-        in_specs=[whole] * 10,
+        out_shape=jax.ShapeDtypeStruct((count, 1, LANES), F32),
+        in_specs=[whole] * 8,
         compiler_params=grant(12),
         name="head",
     )(h, gain, own.T, *(o.T for o in other), own_mask, other_mask, info)
 
 
 def combine_kernel(stats_ref, out_ref):
-    count = stats_ref.shape[0]
-    top = stats_ref[0, :, 0:1]
-    for k in range(1, count):
-        top = jnp.maximum(top, stats_ref[k, :, 0:1])
-    total = jnp.zeros_like(top)
-    picked = jnp.zeros_like(top)
-    for k in range(count):
-        total = total + stats_ref[k, :, 1:2] * jnp.exp(stats_ref[k, :, 0:1] - top)
-        picked = picked + stats_ref[k, :, 2:3]
-    losses = jnp.broadcast_to(jnp.log(total) + top - picked, (top.shape[0], LANES))
-    row = lax.broadcasted_iota(jnp.int32, losses.shape, 0)
-    lane = lax.broadcasted_iota(jnp.int32, losses.shape, 1)
-    flat = jnp.sum(jnp.where(row == lane, losses, 0.0), axis=0, keepdims=True)
-    out_ref[...] = flat[:, 0 : out_ref.shape[1]]
-
-
-def combine(stats):
-    own = stats.shape[1]
+    tops = stats_ref[:, 0, :]
+    totals = pltpu.roll(tops, LANES - GAP, 1)
+    picked = pltpu.roll(tops, LANES - 2 * GAP, 1)
+    top = jnp.max(tops, axis=0, keepdims=True)
+    total = jnp.sum(totals * jnp.exp(tops - top), axis=0, keepdims=True)
+    losses = jnp.log(total) + top - jnp.sum(picked, axis=0, keepdims=True)
+    out_ref[...] = losses[:, 0 : out_ref.shape[1]]
+
+
+def combine(own, stats):
     out = pl.pallas_call(
         combine_kernel,
         out_shape=jax.ShapeDtypeStruct((1, own), F32),
@@ -411,9 +405,9 @@
         head_skip_gain, state_ids, targets,
     )
     if small:
-        depth = features // 4
+        depth = features // 2
         other_weight = tuple(
-            lax.ppermute(head_weight[k * depth : (k + 1) * depth], "vocab", swap) for k in range(4)
+            lax.ppermute(head_weight[k * depth : (k + 1) * depth], "vocab", swap) for k in range(2)
         )
     else:
         other_weight = lax.ppermute(head_weight, "vocab", swap)
@@ -447,7 +441,7 @@
             full, final_gain, head_weight, other_weight, mask_table, other_mask, mine
         )
     placed = exchange(stats)
-    return combine(placed) if small else wide_combine(placed)
+    return combine(rows // 2, placed) if small else wide_combine(placed)
 
 
 def wide_head(full, gain, own, other, own_mask, other_mask, info):

time: 45.1 us -> 44.9 us (level)
    ppermute x4 -> x2, starting transfers between devices: 1.02 us -> 0.51 us  [shards(): lax.ppermute(head_weight[k * depth:(k + 1) * depth], 'vocab', swap)]
  transfers between devices with their start and end apart: 7 -> 5, of which waited for: 4 -> 4; matrix products, arithmetic and copies ran while one was open for 2% -> 3% of each run, Pallas kernels for 0% -> 0%
where the time goes in v6:
time: 44.9 us; the launch traced here: 44.5 us
  blocking collectives  19.7 us (44%)
  waiting for transfers between devices  10.8 us (24%)
  starting transfers between devices  7.9 us (18%)
  Pallas kernels  4.84 us (11%)
  local copies, waits for them, and re-layouts  1.2 us (3%)
    all_to_all x2, blocking collectives, exchange(): return lax.all_to_all(a, both, 0, 0, tiled=True, axis_index_groups=groups)  19.7 us
    all_to_all x1, waiting for transfers between devices, shards(): gathered = lax.all_to_all(packed, 'seq', 0, 0, tiled=True)  7.27 us
    all_to_all x1, starting transfers between devices, shards(): gathered = lax.all_to_all(packed, 'seq', 0, 0, tiled=True)  7.25 us
    pallas_call x1, Pallas kernels, pack(): pl.pallas_call(pack_kernel, out_shape=jax.ShapeDtypeStruct((count, rows,...  1.73 us
    ppermute x1, waiting for transfers between devices, shards(): other_mask = lax.ppermute(mask_table, 'vocab', swap)  1.47 us
    pallas_call x1, Pallas kernels, mixer(): pl.pallas_call(kernel, out_shape=(sums, sums, jax.ShapeDtypeStruct((half,...  1.29 us
    ppermute x1, waiting for transfers between devices, shards(): arrived = lax.ppermute(theirs, 'vocab', swap)  1.24 us
    pallas_call x1, Pallas kernels, head(): pl.pallas_call(head_kernel, out_shape=jax.ShapeDtypeStruct((count, 1, LAN...  1.06 us
  transfers between devices with their start and end apart: 5, of which 4 were waited for; matrix products, arithmetic and copies ran while one was open for 3% of the time, Pallas kernels for 0%

profile of v6, /device:TPU:0, one launch (start us, length us, event | category | flops | bytes accessed | tf_op | source)
XLA Modules:
  0.0 44.5 jit_solution(14545309093330840021)
XLA Ops:
  0.0 0.0 copy-start
  0.0 1.7 %pack.1 = bf16[8,8,2944]{2,1,0:T(8,128)(2,1)} custom-call(bf16[8,1280]{1,0:T(8,128)(2,1)} %ssm_ref.1, bf16[8,1280]{1,0:T(8,128)(2,1)} %gate_ref.1, bf16[8,128]{1,0:T(8,128)(2,1)} %b_ref.1, bf16[8,128]{1,0:T(8,128)(2,1)} %c_ref.1, f32[8,20]{1,0:T(8,128)} %raw_ref.1, f32[1,20]{1,0:T(1,128)} %bitcast.16, f32[1,20]{1,0:T(1,128)} %bitcast.17, f32[1,20]{1,0:T(1,128)} %bitcast.18, ...), custom_call_target="tpu_custom_call" | custom-call | tf_op jit(solution)/shard_map/pack/pallas_call | solution.py:82
  1.7 7.3 %all-to-all-start = ((bf16[8,8,2944]{2,1,0:T(8,128)(2,1)}), bf16[8,8,2944]{2,1,0:T(8,128)(2,1)S(1)}, u32[]{:S(2)}, u32[]{:S(2)}) async-start(bf16[8,8,2944]{2,1,0:T(8,128)(2,1)} %pack.1), calls=%async_computation | async-start | bytes 753664 | tf_op jit(solution)/shard_map/all_to_all | solution.py:415
  9.0 0.0 copy-done
  9.0 0.0 copy-start.2
  9.0 0.0 copy-start.4
  9.0 0.0 copy-start.1
  9.0 0.0 copy-start.3
  9.0 1.0 %fusion = (bf16[1280,196]{0,1:T(8,128)(2,1)}, bf16[1280,196]{0,1:T(8,128)(2,1)}) fusion(bf16[2560,196]{0,1:T(8,128)(2,1)S(1)} %copy-done), kind=kLoop, calls=%fused_computation | loop fusion | bytes 2007040 | tf_op jit(solution)/shard_map/slice | solution.py:410
  10.1 0.0 collective-permute-start
  10.1 0.0 copy-start.5
  10.1 0.5 %collective-permute-start.1 = (bf16[1280,196]{0,1:T(8,128)(2,1)}, bf16[1280,196]{0,1:T(8,128)(2,1)S(1)}, u32[]{:S(2)}, u32[]{:S(2)}) collective-permute-start(bf16[1280,196]{0,1:T(8,128)(2,1)} %get-tuple-element.21), channel_id=1, source_target_pairs={{0,1},{1,0},{2,3},{3,2},{4,5},{5,4},{6,7},{7,6},{8,9},{9,8},{10,11... | collective-permute-start | bytes 1505288 | tf_op jit(solution)/shard_map/ppermute | solution.py:410
  10.6 0.0 copy-done.2
  10.6 0.1 collective-permute-start.2
  10.7 0.0 copy-done.4
  10.7 0.1 reshape.32.gain_ref
  10.7 0.0 copy-done.5
  10.8 1.5 %collective-permute-done.2.other_mask_ref = s32[96,196]{1,0:T(8,128)S(1)} collective-permute-done((s32[96,196]{1,0:T(8,128)S(1)}, s32[96,196]{1,0:T(8,128)S(1)}, u32[]{:S(2)}, u32[]{:S(2)}) %collective-permute-start.2) | collective-permute-done | bytes 75296 | tf_op jit(solution)/shard_map/ppermute | solution.py:414
  12.3 0.0 collective-permute-done
  12.3 0.8 %collective-permute-done.1 = bf16[1280,196]{0,1:T(8,128)(2,1)S(1)} collective-permute-done((bf16[1280,196]{0,1:T(8,128)(2,1)}, bf16[1280,196]{0,1:T(8,128)(2,1)S(1)}, u32[]{:S(2)}, u32[]{:S(2)}) %collective-permute-start.1) | collective-permute-done | bytes 501792 | tf_op jit(solution)/shard_map/ppermute | solution.py:410
  13.1 7.3 %all-to-all-done = bf16[8,8,2944]{2,1,0:T(8,128)(2,1)S(1)} async-done(((bf16[8,8,2944]{2,1,0:T(8,128)(2,1)}), bf16[8,8,2944]{2,1,0:T(8,128)(2,1)S(1)}, u32[]{:S(2)}, u32[]{:S(2)}) %all-to-all-start) | async-done | bytes 376864 | tf_op jit(solution)/shard_map/all_to_all | solution.py:415
  20.3 0.0 copy-done.1
  20.3 0.0 copy-done.3
  20.3 1.3 %mixer.1 = (f32[32,512]{1,0:T(8,128)S(1)}, f32[32,512]{1,0:T(8,128)S(1)}, f32[32,320]{1,0:T(8,128)S(1)}) custom-call(bf16[64,2944]{1,0:T(8,128)(2,1)S(1)} %bitcast.12, f32[1,1280]{1,0:T(1,128)S(1)} %reshape.34.refs_1_, bf16[320,1280]{1,0:T(8,128)(2,1)S(1)} %bitcast.13, bf16[64,320]{1,0:T(8,128)(2,1)S(1)} %copy-done.3), custom_call_target="tpu_custom_call" | custom-call | tf_op jit(solution)/shard_map/mixer/pallas_call | solution.py:177
  21.6 0.1 collective-permute-start.3
  21.7 1.2 %collective-permute-done.3.refs_1_ = f32[32,512]{1,0:T(8,128)S(1)} collective-permute-done((f32[32,512]{1,0:T(8,128)S(1)}, f32[32,512]{1,0:T(8,128)S(1)}, u32[]{:S(2)}, u32[]{:S(2)}) %collective-permute-start.3) | collective-permute-done | bytes 65568 | tf_op jit(solution)/shard_map/ppermute | solution.py:426
  23.0 0.2 hidden.1
  23.1 10.8 %all_to_all.15.h_ref = bf16[8,16,640]{2,1,0:T(8,128)(2,1)S(1)} all-to-all(bf16[8,16,640]{2,1,0:T(8,128)(2,1)S(1)} %hidden.1), channel_id=1, replica_groups={{0,3,4,7,8,11,12,15},{1,2,5,6,9,10,13,14},{16,19,20,23,24,27,28,31},{17..., dimensions={0} | all-to-all | bytes 327680 | tf_op jit(solution)/shard_map/all_to_all | solution.py:400
  33.9 1.1 %head.1 = f32[8,1,128]{2,1,0:T(1,128)S(1)} custom-call(bf16[8,16,640]{2,1,0:T(8,128)(2,1)S(1)} %all_to_all.15.h_ref, f32[8,320]{1,0:T(8,128)S(1)} %reshape.32.gain_ref, bf16[196,2560]{1,0:T(8,128)(2,1)S(1)} %bitcast.11, bf16[196,1280]{1,0:T(8,128)(2,1)S(1)} %bitcast.14, bf16[196,1280]{1,0:T(8,128)(2,1)S(1)} %bitcast.15, s32[96,196]{1,0:T(8,128)S(1)} %copy-done.2, ...), custom_call_target="tpu_custom_call" | custom-call | tf_op jit(solution)/shard_map/head/pallas_call | solution.py:272
  35.0 8.9 %all_to_all.16.stats_ref = f32[8,1,128]{2,1,0:T(1,128)S(1)} all-to-all(f32[8,1,128]{2,1,0:T(1,128)S(1)} %head.1), channel_id=1, replica_groups={{0,3,4,7,8,11,12,15},{1,2,5,6,9,10,13,14},{16,19,20,23,24,27,28,31},{17..., dimensions={0} | all-to-all | bytes 8192 | tf_op jit(solution)/shard_map/all_to_all | solution.py:400
  43.9 0.6 %combine.1 = f32[1,4]{1,0:T(1,128)} custom-call(f32[8,1,128]{2,1,0:T(1,128)S(1)} %all_to_all.16.stats_ref), custom_call_target="tpu_custom_call" | custom-call | tf_op jit(solution)/shard_map/combine/pallas_call | solution.py:292
  (1 shorter events, 0.0 us)
Async XLA Ops:
  0.0 9.0 %copy-start = (bf16[2560,196]{0,1:T(8,128)(2,1)S(1)}, bf16[2560,196]{0,1:T(8,128)(2,1)}, u32[]{:S(2)}) copy-start(bf16[2560,196]{0,1:T(8,128)(2,1)} %param.28) | copy-start | bytes 3010564
  1.7 18.6 %all-to-all-start = ((bf16[8,8,2944]{2,1,0:T(8,128)(2,1)}), bf16[8,8,2944]{2,1,0:T(8,128)(2,1)S(1)}, u32[]{:S(2)}, u32[]{:S(2)}) async-start(bf16[8,8,2944]{2,1,0:T(8,128)(2,1)} %pack.1), calls=%async_computation | async-start | bytes 753664 | tf_op jit(solution)/shard_map/all_to_all | solution.py:415
  9.0 1.6 %copy-start.2 = (s32[96,196]{1,0:T(8,128)S(1)}, s32[96,196]{1,0:T(8,128)}, u32[]{:S(2)}) copy-start(s32[96,196]{1,0:T(8,128)} %own_mask_ref.1) | copy-start | bytes 225796
  9.0 1.7 %copy-start.4 = (f32[2560]{0:T(1024)S(1)}, f32[2560]{0:T(1024)}, u32[]{:S(2)}) copy-start(f32[2560]{0:T(1024)} %param.27) | copy-start | bytes 30724
  9.0 11.3 %copy-start.1 = (bf16[1280,320]{0,1:T(8,128)(2,1)S(1)}, bf16[1280,320]{0,1:T(8,128)(2,1)}, u32[]{:S(2)}) copy-start(bf16[1280,320]{0,1:T(8,128)(2,1)} %param.25) | copy-start | bytes 2457604
  9.0 11.3 %copy-start.3 = (bf16[64,320]{1,0:T(8,128)(2,1)S(1)}, bf16[64,320]{1,0:T(8,128)(2,1)}, u32[]{:S(2)}) copy-start(bf16[64,320]{1,0:T(8,128)(2,1)} %refs_3_.1) | copy-start | bytes 122884
  10.1 2.2 %collective-permute-start = (bf16[1280,196]{0,1:T(8,128)(2,1)}, bf16[1280,196]{0,1:T(8,128)(2,1)S(1)}, u32[]{:S(2)}, u32[]{:S(2)}) collective-permute-start(bf16[1280,196]{0,1:T(8,128)(2,1)} %get-tuple-element.22), channel_id=1, source_target_pairs={{0,1},{1,0},{2,3},{3,2},{4,5},{5,4},{6,7},{7,6},{8,9},{9,8},{10,11... | collective-permute-start | bytes 1505288 | tf_op jit(solution)/shard_map/ppermute | solution.py:410
  10.1 0.7 %copy-start.5 = (f32[1280]{0:T(1024)S(1)}, f32[1280]{0:T(1024)}, u32[]{:S(2)}) copy-start(f32[1280]{0:T(1024)} %param.24) | copy-start | bytes 15364
  10.1 3.0 %collective-permute-start.1 = (bf16[1280,196]{0,1:T(8,128)(2,1)}, bf16[1280,196]{0,1:T(8,128)(2,1)S(1)}, u32[]{:S(2)}, u32[]{:S(2)}) collective-permute-start(bf16[1280,196]{0,1:T(8,128)(2,1)} %get-tuple-element.21), channel_id=1, source_target_pairs={{0,1},{1,0},{2,3},{3,2},{4,5},{5,4},{6,7},{7,6},{8,9},{9,8},{10,11... | collective-permute-start | bytes 1505288 | tf_op jit(solution)/shard_map/ppermute | solution.py:410
  10.6 1.7 %collective-permute-start.2 = (s32[96,196]{1,0:T(8,128)S(1)}, s32[96,196]{1,0:T(8,128)S(1)}, u32[]{:S(2)}, u32[]{:S(2)}) collective-permute-start(s32[96,196]{1,0:T(8,128)S(1)} %copy-done.2), channel_id=1, source_target_pairs={{0,1},{1,0},{2,3},{3,2},{4,5},{5,4},{6,7},{7,6},{8,9},{9,8},{10,11... | collective-permute-start | bytes 225800 | tf_op jit(solution)/shard_map/ppermute | solution.py:414
  21.6 1.3 %collective-permute-start.3 = (f32[32,512]{1,0:T(8,128)S(1)}, f32[32,512]{1,0:T(8,128)S(1)}, u32[]{:S(2)}, u32[]{:S(2)}) collective-permute-start(f32[32,512]{1,0:T(8,128)S(1)} %get-tuple-element.15), channel_id=1, source_target_pairs={{0,1},{1,0},{2,3},{3,2},{4,5},{5,4},{6,7},{7,6},{8,9},{9,8},{10,11... | collective-permute-start | bytes 196616 | tf_op jit(solution)/shard_map/ppermute | solution.py:426

commit v7 on v6

--- a/solution.py
+++ b/solution.py
@@ -146,8 +146,11 @@
     mixed = wide[0:rows] * y + wide[2 * rows : 2 * rows + 1] * moved[:, 0:channels]
     gate = moved[:, channels:edge]
     gated = (mixed * (gate / (1.0 + jnp.exp(-gate)))).astype(BF16).astype(F32)
-    unit = (gated * gain_ref[...]).astype(BF16)
-    partial = times_transposed(unit, weight_ref[...])
+    unit = gated * gain_ref[...]
+    high = unit.astype(BF16)
+    low = (unit - high.astype(F32)).astype(BF16)
+    partial = times_transposed(jnp.concatenate([high, low], axis=0), weight_ref[...])
+    partial = partial[0:rows] + partial[rows:]
     total = jnp.sum(gated * gated, axis=1, keepdims=True)
     kept_ref[...] = jnp.dot(order[0:half], residual_ref[...], preferred_element_type=F32)
 
@@ -347,8 +350,11 @@
     gated = (mixed * jax.nn.silu(x[:, channels:edge].astype(F32))).astype(BF16)
     wide = gated.astype(F32)
     squares = jnp.sum(wide * wide, axis=1, keepdims=True)
-    unit = (wide * gain).astype(BF16)
-    partial = jnp.dot(unit, weight, preferred_element_type=F32)
+    unit = wide * gain
+    high = lax.reduce_precision(unit, 8, 7)
+    partial = jnp.dot(high.astype(BF16), weight, preferred_element_type=F32)
+    low = (unit - high).astype(BF16)
+    partial = partial + jnp.dot(low, weight, preferred_element_type=F32)
     width = weight.shape[1]
     start = (width + LANES - 1) // LANES * LANES
     info = jnp.concatenate([squares, misc[:, INFO : INFO + 3]], axis=1)

time: 44.9 us -> 44.9 us (level)
  no operation moved by 1% of the time
where the time goes in v7:
time: 44.9 us; the launch traced here: 44.5 us
  blocking collectives  19.7 us (44%)
  waiting for transfers between devices  10.8 us (24%)
  starting transfers between devices  7.9 us (18%)
  Pallas kernels  4.82 us (11%)
  local copies, waits for them, and re-layouts  1.2 us (3%)
    all_to_all x2, blocking collectives, exchange(): return lax.all_to_all(a, both, 0, 0, tiled=True, axis_index_groups=groups)  19.7 us
    all_to_all x1, waiting for transfers between devices, shards(): gathered = lax.all_to_all(packed, 'seq', 0, 0, tiled=True)  7.27 us
    all_to_all x1, starting transfers between devices, shards(): gathered = lax.all_to_all(packed, 'seq', 0, 0, tiled=True)  7.25 us
    pallas_call x1, Pallas kernels, pack(): pl.pallas_call(pack_kernel, out_shape=jax.ShapeDtypeStruct((count, rows,...  1.73 us
    ppermute x1, waiting for transfers between devices, shards(): other_mask = lax.ppermute(mask_table, 'vocab', swap)  1.47 us
    pallas_call x1, Pallas kernels, mixer(): pl.pallas_call(kernel, out_shape=(sums, sums, jax.ShapeDtypeStruct((half,...  1.27 us
    ppermute x1, waiting for transfers between devices, shards(): arrived = lax.ppermute(theirs, 'vocab', swap)  1.24 us
    pallas_call x1, Pallas kernels, head(): pl.pallas_call(head_kernel, out_shape=jax.ShapeDtypeStruct((count, 1, LAN...  1.06 us
  transfers between devices with their start and end apart: 5, of which 4 were waited for; matrix products, arithmetic and copies ran while one was open for 3% of the time, Pallas kernels for 0%

profile of v7, /device:TPU:0, one launch (start us, length us, event | category | flops | bytes accessed | tf_op | source)
XLA Modules:
  0.0 44.5 jit_solution(15261603512604702423)
XLA Ops:
  0.0 0.0 copy-start
  0.0 1.7 %pack.1 = bf16[8,8,2944]{2,1,0:T(8,128)(2,1)} custom-call(bf16[8,1280]{1,0:T(8,128)(2,1)} %ssm_ref.1, bf16[8,1280]{1,0:T(8,128)(2,1)} %gate_ref.1, bf16[8,128]{1,0:T(8,128)(2,1)} %b_ref.1, bf16[8,128]{1,0:T(8,128)(2,1)} %c_ref.1, f32[8,20]{1,0:T(8,128)} %raw_ref.1, f32[1,20]{1,0:T(1,128)} %bitcast.16, f32[1,20]{1,0:T(1,128)} %bitcast.17, f32[1,20]{1,0:T(1,128)} %bitcast.18, ...), custom_call_target="tpu_custom_call" | custom-call | tf_op jit(solution)/shard_map/pack/pallas_call | solution.py:82
  1.7 7.3 %all-to-all-start = ((bf16[8,8,2944]{2,1,0:T(8,128)(2,1)}), bf16[8,8,2944]{2,1,0:T(8,128)(2,1)S(1)}, u32[]{:S(2)}, u32[]{:S(2)}) async-start(bf16[8,8,2944]{2,1,0:T(8,128)(2,1)} %pack.1), calls=%async_computation | async-start | bytes 753664 | tf_op jit(solution)/shard_map/all_to_all | solution.py:421
  9.0 0.0 copy-done
  9.0 0.0 copy-start.2
  9.0 0.0 copy-start.4
  9.0 0.0 copy-start.1
  9.0 0.0 copy-start.3
  9.0 1.0 %fusion = (bf16[1280,196]{0,1:T(8,128)(2,1)}, bf16[1280,196]{0,1:T(8,128)(2,1)}) fusion(bf16[2560,196]{0,1:T(8,128)(2,1)S(1)} %copy-done), kind=kLoop, calls=%fused_computation | loop fusion | bytes 2007040 | tf_op jit(solution)/shard_map/slice | solution.py:416
  10.1 0.0 collective-permute-start
  10.1 0.0 copy-start.5
  10.1 0.5 %collective-permute-start.1 = (bf16[1280,196]{0,1:T(8,128)(2,1)}, bf16[1280,196]{0,1:T(8,128)(2,1)S(1)}, u32[]{:S(2)}, u32[]{:S(2)}) collective-permute-start(bf16[1280,196]{0,1:T(8,128)(2,1)} %get-tuple-element.21), channel_id=1, source_target_pairs={{0,1},{1,0},{2,3},{3,2},{4,5},{5,4},{6,7},{7,6},{8,9},{9,8},{10,11... | collective-permute-start | bytes 1505288 | tf_op jit(solution)/shard_map/ppermute | solution.py:416
  10.6 0.0 copy-done.2
  10.6 0.1 collective-permute-start.2
  10.7 0.0 copy-done.4
  10.7 0.1 reshape.32.gain_ref
  10.7 0.0 copy-done.5
  10.8 1.5 %collective-permute-done.2.other_mask_ref = s32[96,196]{1,0:T(8,128)S(1)} collective-permute-done((s32[96,196]{1,0:T(8,128)S(1)}, s32[96,196]{1,0:T(8,128)S(1)}, u32[]{:S(2)}, u32[]{:S(2)}) %collective-permute-start.2) | collective-permute-done | bytes 75296 | tf_op jit(solution)/shard_map/ppermute | solution.py:420
  12.3 0.0 collective-permute-done
  12.3 0.8 %collective-permute-done.1 = bf16[1280,196]{0,1:T(8,128)(2,1)S(1)} collective-permute-done((bf16[1280,196]{0,1:T(8,128)(2,1)}, bf16[1280,196]{0,1:T(8,128)(2,1)S(1)}, u32[]{:S(2)}, u32[]{:S(2)}) %collective-permute-start.1) | collective-permute-done | bytes 501792 | tf_op jit(solution)/shard_map/ppermute | solution.py:416
  13.1 7.3 %all-to-all-done = bf16[8,8,2944]{2,1,0:T(8,128)(2,1)S(1)} async-done(((bf16[8,8,2944]{2,1,0:T(8,128)(2,1)}), bf16[8,8,2944]{2,1,0:T(8,128)(2,1)S(1)}, u32[]{:S(2)}, u32[]{:S(2)}) %all-to-all-start) | async-done | bytes 376864 | tf_op jit(solution)/shard_map/all_to_all | solution.py:421
  20.3 0.0 copy-done.1
  20.3 0.0 copy-done.3
  20.3 1.3 %mixer.1 = (f32[32,512]{1,0:T(8,128)S(1)}, f32[32,512]{1,0:T(8,128)S(1)}, f32[32,320]{1,0:T(8,128)S(1)}) custom-call(bf16[64,2944]{1,0:T(8,128)(2,1)S(1)} %bitcast.12, f32[1,1280]{1,0:T(1,128)S(1)} %reshape.34.refs_1_, bf16[320,1280]{1,0:T(8,128)(2,1)S(1)} %bitcast.13, bf16[64,320]{1,0:T(8,128)(2,1)S(1)} %copy-done.3), custom_call_target="tpu_custom_call" | custom-call | tf_op jit(solution)/shard_map/mixer/pallas_call | solution.py:180
  21.6 0.1 collective-permute-start.3
  21.7 1.2 %collective-permute-done.3.refs_1_ = f32[32,512]{1,0:T(8,128)S(1)} collective-permute-done((f32[32,512]{1,0:T(8,128)S(1)}, f32[32,512]{1,0:T(8,128)S(1)}, u32[]{:S(2)}, u32[]{:S(2)}) %collective-permute-start.3) | collective-permute-done | bytes 65568 | tf_op jit(solution)/shard_map/ppermute | solution.py:432
  22.9 0.2 hidden.1
  23.1 10.8 %all_to_all.15.h_ref = bf16[8,16,640]{2,1,0:T(8,128)(2,1)S(1)} all-to-all(bf16[8,16,640]{2,1,0:T(8,128)(2,1)S(1)} %hidden.1), channel_id=1, replica_groups={{0,3,4,7,8,11,12,15},{1,2,5,6,9,10,13,14},{16,19,20,23,24,27,28,31},{17..., dimensions={0} | all-to-all | bytes 327680 | tf_op jit(solution)/shard_map/all_to_all | solution.py:406
  33.9 1.1 %head.1 = f32[8,1,128]{2,1,0:T(1,128)S(1)} custom-call(bf16[8,16,640]{2,1,0:T(8,128)(2,1)S(1)} %all_to_all.15.h_ref, f32[8,320]{1,0:T(8,128)S(1)} %reshape.32.gain_ref, bf16[196,2560]{1,0:T(8,128)(2,1)S(1)} %bitcast.11, bf16[196,1280]{1,0:T(8,128)(2,1)S(1)} %bitcast.14, bf16[196,1280]{1,0:T(8,128)(2,1)S(1)} %bitcast.15, s32[96,196]{1,0:T(8,128)S(1)} %copy-done.2, ...), custom_call_target="tpu_custom_call" | custom-call | tf_op jit(solution)/shard_map/head/pallas_call | solution.py:275
  35.0 8.9 %all_to_all.16.stats_ref = f32[8,1,128]{2,1,0:T(1,128)S(1)} all-to-all(f32[8,1,128]{2,1,0:T(1,128)S(1)} %head.1), channel_id=1, replica_groups={{0,3,4,7,8,11,12,15},{1,2,5,6,9,10,13,14},{16,19,20,23,24,27,28,31},{17..., dimensions={0} | all-to-all | bytes 8192 | tf_op jit(solution)/shard_map/all_to_all | solution.py:406
  43.9 0.6 %combine.1 = f32[1,4]{1,0:T(1,128)} custom-call(f32[8,1,128]{2,1,0:T(1,128)S(1)} %all_to_all.16.stats_ref), custom_call_target="tpu_custom_call" | custom-call | tf_op jit(solution)/shard_map/combine/pallas_call | solution.py:295
  (1 shorter events, 0.0 us)
Async XLA Ops:
  0.0 9.0 %copy-start = (bf16[2560,196]{0,1:T(8,128)(2,1)S(1)}, bf16[2560,196]{0,1:T(8,128)(2,1)}, u32[]{:S(2)}) copy-start(bf16[2560,196]{0,1:T(8,128)(2,1)} %param.28) | copy-start | bytes 3010564
  1.7 18.6 %all-to-all-start = ((bf16[8,8,2944]{2,1,0:T(8,128)(2,1)}), bf16[8,8,2944]{2,1,0:T(8,128)(2,1)S(1)}, u32[]{:S(2)}, u32[]{:S(2)}) async-start(bf16[8,8,2944]{2,1,0:T(8,128)(2,1)} %pack.1), calls=%async_computation | async-start | bytes 753664 | tf_op jit(solution)/shard_map/all_to_all | solution.py:421
  9.0 1.6 %copy-start.2 = (s32[96,196]{1,0:T(8,128)S(1)}, s32[96,196]{1,0:T(8,128)}, u32[]{:S(2)}) copy-start(s32[96,196]{1,0:T(8,128)} %own_mask_ref.1) | copy-start | bytes 225796
  9.0 1.7 %copy-start.4 = (f32[2560]{0:T(1024)S(1)}, f32[2560]{0:T(1024)}, u32[]{:S(2)}) copy-start(f32[2560]{0:T(1024)} %param.27) | copy-start | bytes 30724
  9.0 11.3 %copy-start.1 = (bf16[1280,320]{0,1:T(8,128)(2,1)S(1)}, bf16[1280,320]{0,1:T(8,128)(2,1)}, u32[]{:S(2)}) copy-start(bf16[1280,320]{0,1:T(8,128)(2,1)} %param.25) | copy-start | bytes 2457604
  9.0 11.3 %copy-start.3 = (bf16[64,320]{1,0:T(8,128)(2,1)S(1)}, bf16[64,320]{1,0:T(8,128)(2,1)}, u32[]{:S(2)}) copy-start(bf16[64,320]{1,0:T(8,128)(2,1)} %refs_3_.1) | copy-start | bytes 122884
  10.1 2.2 %collective-permute-start = (bf16[1280,196]{0,1:T(8,128)(2,1)}, bf16[1280,196]{0,1:T(8,128)(2,1)S(1)}, u32[]{:S(2)}, u32[]{:S(2)}) collective-permute-start(bf16[1280,196]{0,1:T(8,128)(2,1)} %get-tuple-element.22), channel_id=1, source_target_pairs={{0,1},{1,0},{2,3},{3,2},{4,5},{5,4},{6,7},{7,6},{8,9},{9,8},{10,11... | collective-permute-start | bytes 1505288 | tf_op jit(solution)/shard_map/ppermute | solution.py:416
  10.1 0.7 %copy-start.5 = (f32[1280]{0:T(1024)S(1)}, f32[1280]{0:T(1024)}, u32[]{:S(2)}) copy-start(f32[1280]{0:T(1024)} %param.24) | copy-start | bytes 15364
  10.1 3.0 %collective-permute-start.1 = (bf16[1280,196]{0,1:T(8,128)(2,1)}, bf16[1280,196]{0,1:T(8,128)(2,1)S(1)}, u32[]{:S(2)}, u32[]{:S(2)}) collective-permute-start(bf16[1280,196]{0,1:T(8,128)(2,1)} %get-tuple-element.21), channel_id=1, source_target_pairs={{0,1},{1,0},{2,3},{3,2},{4,5},{5,4},{6,7},{7,6},{8,9},{9,8},{10,11... | collective-permute-start | bytes 1505288 | tf_op jit(solution)/shard_map/ppermute | solution.py:416
  10.6 1.7 %collective-permute-start.2 = (s32[96,196]{1,0:T(8,128)S(1)}, s32[96,196]{1,0:T(8,128)S(1)}, u32[]{:S(2)}, u32[]{:S(2)}) collective-permute-start(s32[96,196]{1,0:T(8,128)S(1)} %copy-done.2), channel_id=1, source_target_pairs={{0,1},{1,0},{2,3},{3,2},{4,5},{5,4},{6,7},{7,6},{8,9},{9,8},{10,11... | collective-permute-start | bytes 225800 | tf_op jit(solution)/shard_map/ppermute | solution.py:420
  21.6 1.3 %collective-permute-start.3 = (f32[32,512]{1,0:T(8,128)S(1)}, f32[32,512]{1,0:T(8,128)S(1)}, u32[]{:S(2)}, u32[]{:S(2)}) collective-permute-start(f32[32,512]{1,0:T(8,128)S(1)} %get-tuple-element.15), channel_id=1, source_target_pairs={{0,1},{1,0},{2,3},{3,2},{4,5},{5,4},{6,7},{7,6},{8,9},{9,8},{10,11... | collective-permute-start | bytes 196616 | tf_op jit(solution)/shard_map/ppermute | solution.py:432

commit v8 on v7

--- a/solution.py
+++ b/solution.py
@@ -26,7 +26,7 @@
 
 
 def turn(seq):
-    return seq % 2
+    return seq // 4
 
 
 def circles(count):
@@ -106,7 +106,7 @@
     side = (r64 >= half).astype(jnp.int32)
     place = r64 - side * half
     seq = lax.shift_right_logical(place, own.bit_length() - 1)
-    which = (mine + side + seq) & 1
+    which = (mine + side + lax.shift_right_logical(seq, 2)) & 1
     source = place + seq * own + which * own
     order = (c64 == source).astype(BF16)
     causal = c64 <= source
@@ -126,11 +126,11 @@
     back = jnp.exp(middle - cums[0:rows]) * step
     skips = jnp.broadcast_to(gains[:, 0:heads], (8, heads))
     factors = jnp.concatenate([ahead, back, skips], axis=0)
-    factors = jnp.concatenate(thirds(factors), axis=1).astype(BF16)
-    head_row = lax.broadcasted_iota(jnp.int32, (3 * heads, channels), 0)
-    for _ in range(2):
-        head_row = jnp.where(head_row >= heads, head_row - heads, head_row)
-    from_head = lax.broadcasted_iota(jnp.int32, (3 * heads, channels), 1) - head_row * size
+    high = factors.astype(BF16).astype(F32)
+    factors = jnp.concatenate([high, factors - high], axis=1).astype(BF16)
+    head_row = lax.broadcasted_iota(jnp.int32, (2 * heads, channels), 0)
+    head_row = jnp.where(head_row >= heads, head_row - heads, head_row)
+    from_head = lax.broadcasted_iota(jnp.int32, (2 * heads, channels), 1) - head_row * size
     spread = ((from_head >= 0) & (from_head < size)).astype(BF16)
     wide = jnp.dot(factors, spread, preferred_element_type=F32)
 

time: 44.9 us -> 44.7 us (level)
  no operation moved by 1% of the time
where the time goes in v8:
time: 44.7 us; the launch traced here: 44.4 us
  blocking collectives  19.6 us (44%)
  waiting for transfers between devices  10.8 us (24%)
  starting transfers between devices  7.9 us (18%)
  Pallas kernels  4.82 us (11%)
  local copies, waits for them, and re-layouts  1.2 us (3%)
    all_to_all x2, blocking collectives, exchange(): return lax.all_to_all(a, both, 0, 0, tiled=True, axis_index_groups=groups)  19.6 us
    all_to_all x1, waiting for transfers between devices, shards(): gathered = lax.all_to_all(packed, 'seq', 0, 0, tiled=True)  7.27 us
    all_to_all x1, starting transfers between devices, shards(): gathered = lax.all_to_all(packed, 'seq', 0, 0, tiled=True)  7.25 us
    pallas_call x1, Pallas kernels, pack(): pl.pallas_call(pack_kernel, out_shape=jax.ShapeDtypeStruct((count, rows,...  1.73 us
    ppermute x1, waiting for transfers between devices, shards(): other_mask = lax.ppermute(mask_table, 'vocab', swap)  1.47 us
    pallas_call x1, Pallas kernels, mixer(): pl.pallas_call(kernel, out_shape=(sums, sums, jax.ShapeDtypeStruct((half,...  1.27 us
    ppermute x1, waiting for transfers between devices, shards(): arrived = lax.ppermute(theirs, 'vocab', swap)  1.24 us
    pallas_call x1, Pallas kernels, head(): pl.pallas_call(head_kernel, out_shape=jax.ShapeDtypeStruct((count, 1, LAN...  1.06 us
  transfers between devices with their start and end apart: 5, of which 4 were waited for; matrix products, arithmetic and copies ran while one was open for 3% of the time, Pallas kernels for 0%

profile of v8, /device:TPU:0, one launch (start us, length us, event | category | flops | bytes accessed | tf_op | source)
XLA Modules:
  0.0 44.4 jit_solution(2548725167914077148)
XLA Ops:
  0.0 0.0 copy-start
  0.0 1.7 %pack.1 = bf16[8,8,2944]{2,1,0:T(8,128)(2,1)} custom-call(bf16[8,1280]{1,0:T(8,128)(2,1)} %ssm_ref.1, bf16[8,1280]{1,0:T(8,128)(2,1)} %gate_ref.1, bf16[8,128]{1,0:T(8,128)(2,1)} %b_ref.1, bf16[8,128]{1,0:T(8,128)(2,1)} %c_ref.1, f32[8,20]{1,0:T(8,128)} %raw_ref.1, f32[1,20]{1,0:T(1,128)} %bitcast.16, f32[1,20]{1,0:T(1,128)} %bitcast.17, f32[1,20]{1,0:T(1,128)} %bitcast.18, ...), custom_call_target="tpu_custom_call" | custom-call | tf_op jit(solution)/shard_map/pack/pallas_call | solution.py:82
  1.7 7.3 %all-to-all-start = ((bf16[8,8,2944]{2,1,0:T(8,128)(2,1)}), bf16[8,8,2944]{2,1,0:T(8,128)(2,1)S(1)}, u32[]{:S(2)}, u32[]{:S(2)}) async-start(bf16[8,8,2944]{2,1,0:T(8,128)(2,1)} %pack.1), calls=%async_computation | async-start | bytes 753664 | tf_op jit(solution)/shard_map/all_to_all | solution.py:421
  9.0 0.0 copy-done
  9.0 0.0 copy-start.2
  9.0 0.0 copy-start.4
  9.0 0.0 copy-start.1
  9.0 0.0 copy-start.3
  9.0 1.0 %fusion = (bf16[1280,196]{0,1:T(8,128)(2,1)}, bf16[1280,196]{0,1:T(8,128)(2,1)}) fusion(bf16[2560,196]{0,1:T(8,128)(2,1)S(1)} %copy-done), kind=kLoop, calls=%fused_computation | loop fusion | bytes 2007040 | tf_op jit(solution)/shard_map/slice | solution.py:416
  10.1 0.0 collective-permute-start
  10.1 0.0 copy-start.5
  10.1 0.5 %collective-permute-start.1 = (bf16[1280,196]{0,1:T(8,128)(2,1)}, bf16[1280,196]{0,1:T(8,128)(2,1)S(1)}, u32[]{:S(2)}, u32[]{:S(2)}) collective-permute-start(bf16[1280,196]{0,1:T(8,128)(2,1)} %get-tuple-element.21), channel_id=1, source_target_pairs={{0,1},{1,0},{2,3},{3,2},{4,5},{5,4},{6,7},{7,6},{8,9},{9,8},{10,11... | collective-permute-start | bytes 1505288 | tf_op jit(solution)/shard_map/ppermute | solution.py:416
  10.6 0.0 copy-done.2
  10.6 0.1 collective-permute-start.2
  10.7 0.0 copy-done.4
  10.7 0.1 reshape.32.gain_ref
  10.7 0.0 copy-done.5
  10.8 1.5 %collective-permute-done.2.other_mask_ref = s32[96,196]{1,0:T(8,128)S(1)} collective-permute-done((s32[96,196]{1,0:T(8,128)S(1)}, s32[96,196]{1,0:T(8,128)S(1)}, u32[]{:S(2)}, u32[]{:S(2)}) %collective-permute-start.2) | collective-permute-done | bytes 75296 | tf_op jit(solution)/shard_map/ppermute | solution.py:420
  12.3 0.0 collective-permute-done
  12.3 0.8 %collective-permute-done.1 = bf16[1280,196]{0,1:T(8,128)(2,1)S(1)} collective-permute-done((bf16[1280,196]{0,1:T(8,128)(2,1)}, bf16[1280,196]{0,1:T(8,128)(2,1)S(1)}, u32[]{:S(2)}, u32[]{:S(2)}) %collective-permute-start.1) | collective-permute-done | bytes 501792 | tf_op jit(solution)/shard_map/ppermute | solution.py:416
  13.1 7.3 %all-to-all-done = bf16[8,8,2944]{2,1,0:T(8,128)(2,1)S(1)} async-done(((bf16[8,8,2944]{2,1,0:T(8,128)(2,1)}), bf16[8,8,2944]{2,1,0:T(8,128)(2,1)S(1)}, u32[]{:S(2)}, u32[]{:S(2)}) %all-to-all-start) | async-done | bytes 376864 | tf_op jit(solution)/shard_map/all_to_all | solution.py:421
  20.3 0.0 copy-done.1
  20.3 0.0 copy-done.3
  20.3 1.3 %mixer.1 = (f32[32,512]{1,0:T(8,128)S(1)}, f32[32,512]{1,0:T(8,128)S(1)}, f32[32,320]{1,0:T(8,128)S(1)}) custom-call(bf16[64,2944]{1,0:T(8,128)(2,1)S(1)} %bitcast.12, f32[1,1280]{1,0:T(1,128)S(1)} %reshape.34.refs_1_, bf16[320,1280]{1,0:T(8,128)(2,1)S(1)} %bitcast.13, bf16[64,320]{1,0:T(8,128)(2,1)S(1)} %copy-done.3), custom_call_target="tpu_custom_call" | custom-call | tf_op jit(solution)/shard_map/mixer/pallas_call | solution.py:180
  21.6 0.1 collective-permute-start.3
  21.7 1.2 %collective-permute-done.3.refs_1_ = f32[32,512]{1,0:T(8,128)S(1)} collective-permute-done((f32[32,512]{1,0:T(8,128)S(1)}, f32[32,512]{1,0:T(8,128)S(1)}, u32[]{:S(2)}, u32[]{:S(2)}) %collective-permute-start.3) | collective-permute-done | bytes 65568 | tf_op jit(solution)/shard_map/ppermute | solution.py:432
  22.9 0.2 hidden.1
  23.1 10.8 %all_to_all.15.h_ref = bf16[8,16,640]{2,1,0:T(8,128)(2,1)S(1)} all-to-all(bf16[8,16,640]{2,1,0:T(8,128)(2,1)S(1)} %hidden.1), channel_id=1, replica_groups={{0,2,4,6,9,11,13,15},{1,3,5,7,8,10,12,14},{16,18,20,22,25,27,29,31},{17..., dimensions={0} | all-to-all | bytes 327680 | tf_op jit(solution)/shard_map/all_to_all | solution.py:406
  33.9 1.1 %head.1 = f32[8,1,128]{2,1,0:T(1,128)S(1)} custom-call(bf16[8,16,640]{2,1,0:T(8,128)(2,1)S(1)} %all_to_all.15.h_ref, f32[8,320]{1,0:T(8,128)S(1)} %reshape.32.gain_ref, bf16[196,2560]{1,0:T(8,128)(2,1)S(1)} %bitcast.11, bf16[196,1280]{1,0:T(8,128)(2,1)S(1)} %bitcast.14, bf16[196,1280]{1,0:T(8,128)(2,1)S(1)} %bitcast.15, s32[96,196]{1,0:T(8,128)S(1)} %copy-done.2, ...), custom_call_target="tpu_custom_call" | custom-call | tf_op jit(solution)/shard_map/head/pallas_call | solution.py:275
  35.0 8.8 %all_to_all.16.stats_ref = f32[8,1,128]{2,1,0:T(1,128)S(1)} all-to-all(f32[8,1,128]{2,1,0:T(1,128)S(1)} %head.1), channel_id=1, replica_groups={{0,2,4,6,9,11,13,15},{1,3,5,7,8,10,12,14},{16,18,20,22,25,27,29,31},{17..., dimensions={0} | all-to-all | bytes 8192 | tf_op jit(solution)/shard_map/all_to_all | solution.py:406
  43.8 0.6 %combine.1 = f32[1,4]{1,0:T(1,128)} custom-call(f32[8,1,128]{2,1,0:T(1,128)S(1)} %all_to_all.16.stats_ref), custom_call_target="tpu_custom_call" | custom-call | tf_op jit(solution)/shard_map/combine/pallas_call | solution.py:295
  (1 shorter events, 0.0 us)
Async XLA Ops:
  0.0 9.0 %copy-start = (bf16[2560,196]{0,1:T(8,128)(2,1)S(1)}, bf16[2560,196]{0,1:T(8,128)(2,1)}, u32[]{:S(2)}) copy-start(bf16[2560,196]{0,1:T(8,128)(2,1)} %param.28) | copy-start | bytes 3010564
  1.7 18.6 %all-to-all-start = ((bf16[8,8,2944]{2,1,0:T(8,128)(2,1)}), bf16[8,8,2944]{2,1,0:T(8,128)(2,1)S(1)}, u32[]{:S(2)}, u32[]{:S(2)}) async-start(bf16[8,8,2944]{2,1,0:T(8,128)(2,1)} %pack.1), calls=%async_computation | async-start | bytes 753664 | tf_op jit(solution)/shard_map/all_to_all | solution.py:421
  9.0 1.6 %copy-start.2 = (s32[96,196]{1,0:T(8,128)S(1)}, s32[96,196]{1,0:T(8,128)}, u32[]{:S(2)}) copy-start(s32[96,196]{1,0:T(8,128)} %own_mask_ref.1) | copy-start | bytes 225796
  9.0 1.7 %copy-start.4 = (f32[2560]{0:T(1024)S(1)}, f32[2560]{0:T(1024)}, u32[]{:S(2)}) copy-start(f32[2560]{0:T(1024)} %param.27) | copy-start | bytes 30724
  9.0 11.3 %copy-start.1 = (bf16[1280,320]{0,1:T(8,128)(2,1)S(1)}, bf16[1280,320]{0,1:T(8,128)(2,1)}, u32[]{:S(2)}) copy-start(bf16[1280,320]{0,1:T(8,128)(2,1)} %param.25) | copy-start | bytes 2457604
  9.0 11.3 %copy-start.3 = (bf16[64,320]{1,0:T(8,128)(2,1)S(1)}, bf16[64,320]{1,0:T(8,128)(2,1)}, u32[]{:S(2)}) copy-start(bf16[64,320]{1,0:T(8,128)(2,1)} %refs_3_.1) | copy-start | bytes 122884
  10.1 2.2 %collective-permute-start = (bf16[1280,196]{0,1:T(8,128)(2,1)}, bf16[1280,196]{0,1:T(8,128)(2,1)S(1)}, u32[]{:S(2)}, u32[]{:S(2)}) collective-permute-start(bf16[1280,196]{0,1:T(8,128)(2,1)} %get-tuple-element.22), channel_id=1, source_target_pairs={{0,1},{1,0},{2,3},{3,2},{4,5},{5,4},{6,7},{7,6},{8,9},{9,8},{10,11... | collective-permute-start | bytes 1505288 | tf_op jit(solution)/shard_map/ppermute | solution.py:416
  10.1 0.7 %copy-start.5 = (f32[1280]{0:T(1024)S(1)}, f32[1280]{0:T(1024)}, u32[]{:S(2)}) copy-start(f32[1280]{0:T(1024)} %param.24) | copy-start | bytes 15364
  10.1 3.0 %collective-permute-start.1 = (bf16[1280,196]{0,1:T(8,128)(2,1)}, bf16[1280,196]{0,1:T(8,128)(2,1)S(1)}, u32[]{:S(2)}, u32[]{:S(2)}) collective-permute-start(bf16[1280,196]{0,1:T(8,128)(2,1)} %get-tuple-element.21), channel_id=1, source_target_pairs={{0,1},{1,0},{2,3},{3,2},{4,5},{5,4},{6,7},{7,6},{8,9},{9,8},{10,11... | collective-permute-start | bytes 1505288 | tf_op jit(solution)/shard_map/ppermute | solution.py:416
  10.6 1.7 %collective-permute-start.2 = (s32[96,196]{1,0:T(8,128)S(1)}, s32[96,196]{1,0:T(8,128)S(1)}, u32[]{:S(2)}, u32[]{:S(2)}) collective-permute-start(s32[96,196]{1,0:T(8,128)S(1)} %copy-done.2), channel_id=1, source_target_pairs={{0,1},{1,0},{2,3},{3,2},{4,5},{5,4},{6,7},{7,6},{8,9},{9,8},{10,11... | collective-permute-start | bytes 225800 | tf_op jit(solution)/shard_map/ppermute | solution.py:420
  21.6 1.3 %collective-permute-start.3 = (f32[32,512]{1,0:T(8,128)S(1)}, f32[32,512]{1,0:T(8,128)S(1)}, u32[]{:S(2)}, u32[]{:S(2)}) collective-permute-start(f32[32,512]{1,0:T(8,128)S(1)} %get-tuple-element.15), channel_id=1, source_target_pairs={{0,1},{1,0},{2,3},{3,2},{4,5},{5,4},{6,7},{7,6},{8,9},{9,8},{10,11... | collective-permute-start | bytes 196616 | tf_op jit(solution)/shard_map/ppermute | solution.py:432

commit v9 on v7

--- a/solution.py
+++ b/solution.py
@@ -26,7 +26,7 @@
 
 
 def turn(seq):
-    return seq % 2
+    return seq // 4
 
 
 def circles(count):
@@ -106,7 +106,7 @@
     side = (r64 >= half).astype(jnp.int32)
     place = r64 - side * half
     seq = lax.shift_right_logical(place, own.bit_length() - 1)
-    which = (mine + side + seq) & 1
+    which = (mine + side + lax.shift_right_logical(seq, 2)) & 1
     source = place + seq * own + which * own
     order = (c64 == source).astype(BF16)
     causal = c64 <= source
@@ -127,11 +127,13 @@
     skips = jnp.broadcast_to(gains[:, 0:heads], (8, heads))
     factors = jnp.concatenate([ahead, back, skips], axis=0)
     factors = jnp.concatenate(thirds(factors), axis=1).astype(BF16)
-    head_row = lax.broadcasted_iota(jnp.int32, (3 * heads, channels), 0)
+    head_row = lax.broadcasted_iota(jnp.int32, (3 * heads, 1), 0)
     for _ in range(2):
         head_row = jnp.where(head_row >= heads, head_row - heads, head_row)
-    from_head = lax.broadcasted_iota(jnp.int32, (3 * heads, channels), 1) - head_row * size
-    spread = ((from_head >= 0) & (from_head < size)).astype(BF16)
+    head_lane = lax.shift_right_logical(
+        lax.broadcasted_iota(jnp.int32, (1, channels), 1), size.bit_length() - 1
+    )
+    spread = (head_row == head_lane).astype(BF16)
     wide = jnp.dot(factors, spread, preferred_element_type=F32)
 
     c = moved[:, edge + state : edge + 2 * state].astype(BF16)
@@ -245,8 +247,7 @@
     column = lax.broadcasted_iota(jnp.int32, (rows, entries), 1)
     allowed, wanted = [], []
     for ref, which in ((own_mask_ref, core), (other_mask_ref, 1 - core)):
-        table = (ref[...] == 1).astype(F32).astype(BF16)
-        chosen = jnp.dot(pick_row, table, preferred_element_type=F32)
+        chosen = jnp.dot(pick_row, ref[...], preferred_element_type=F32)
         is_target = column + (block + which) * entries == target
         wanted.append(is_target)
         allowed.append((chosen > 0.5) | is_target)
@@ -417,13 +418,14 @@
         )
     else:
         other_weight = lax.ppermute(head_weight, "vocab", swap)
+    mask_table = (mask_table == 1).astype(BF16)
     other_mask = lax.ppermute(mask_table, "vocab", swap)
     gathered = lax.all_to_all(packed, "seq", 0, 0, tiled=True)
     final_gain = final_gain.reshape(count, features // count)
     norm_gain = norm_gain.reshape(1, channels)
     if small:
-        gathered, other_weight, other_mask, final_gain = lax.optimization_barrier(
-            (gathered, other_weight, other_mask, final_gain)
+        gathered, other_weight, mask_table, other_mask, final_gain = lax.optimization_barrier(
+            (gathered, other_weight, mask_table, other_mask, final_gain)
         )
     x = gathered.reshape(count * rows, packed.shape[2])
     mine, theirs, kept = (mixer if small else wide_mixer)(

time: 44.9 us -> 44.7 us (level)
  waiting for transfers between devices: 10.8 us -> 10.3 us
  local copies, waits for them, and re-layouts: 1.2 us -> 1.69 us
    ppermute x1, waiting for transfers between devices: 1.47 us -> 0.79 us  [shards(): other_mask = lax.ppermute(mask_table, 'vocab', swap)]
    unnamed x12, local copies, waits for them, and re-layouts: 0.08 us -> 0.56 us
  transfers between devices with their start and end apart: 5 -> 5, of which waited for: 4 -> 5; matrix products, arithmetic and copies ran while one was open for 3% -> 3% of each run, Pallas kernels for 0% -> 0%
where the time goes in v9:
time: 44.7 us; the launch traced here: 44.4 us
  blocking collectives  19.6 us (44%)
  waiting for transfers between devices  10.3 us (23%)
  starting transfers between devices  7.91 us (18%)
  Pallas kernels  4.82 us (11%)
  local copies, waits for them, and re-layouts  1.69 us (4%)
    all_to_all x2, blocking collectives, exchange(): return lax.all_to_all(a, both, 0, 0, tiled=True, axis_index_groups=groups)  19.6 us
    all_to_all x1, waiting for transfers between devices, shards(): gathered = lax.all_to_all(packed, 'seq', 0, 0, tiled=True)  7.37 us
    all_to_all x1, starting transfers between devices, shards(): gathered = lax.all_to_all(packed, 'seq', 0, 0, tiled=True)  7.25 us
    pallas_call x1, Pallas kernels, pack(): pl.pallas_call(pack_kernel, out_shape=jax.ShapeDtypeStruct((count, rows,...  1.73 us
    pallas_call x1, Pallas kernels, mixer(): pl.pallas_call(kernel, out_shape=(sums, sums, jax.ShapeDtypeStruct((half,...  1.27 us
    ppermute x1, waiting for transfers between devices, shards(): arrived = lax.ppermute(theirs, 'vocab', swap)  1.24 us
    pallas_call x1, Pallas kernels, head(): pl.pallas_call(head_kernel, out_shape=jax.ShapeDtypeStruct((count, 1, LAN...  1.06 us
    slice x1, local copies, waits for them, and re-layouts, shards(): head_weight[k * depth:(k + 1) * depth]  1.04 us
  transfers between devices with their start and end apart: 5, of which 5 were waited for; matrix products, arithmetic and copies ran while one was open for 3% of the time, Pallas kernels for 0%

profile of v9, /device:TPU:0, one launch (start us, length us, event | category | flops | bytes accessed | tf_op | source)
XLA Modules:
  0.0 44.4 jit_solution(16791252680781990409)
XLA Ops:
  0.0 0.0 copy-start
  0.0 1.7 %pack.1 = bf16[8,8,2944]{2,1,0:T(8,128)(2,1)} custom-call(bf16[8,1280]{1,0:T(8,128)(2,1)} %ssm_ref.1, bf16[8,1280]{1,0:T(8,128)(2,1)} %gate_ref.1, bf16[8,128]{1,0:T(8,128)(2,1)} %b_ref.1, bf16[8,128]{1,0:T(8,128)(2,1)} %c_ref.1, f32[8,20]{1,0:T(8,128)} %raw_ref.1, f32[1,20]{1,0:T(1,128)} %bitcast.16, f32[1,20]{1,0:T(1,128)} %bitcast.17, f32[1,20]{1,0:T(1,128)} %bitcast.18, ...), custom_call_target="tpu_custom_call" | custom-call | tf_op jit(solution)/shard_map/pack/pallas_call | solution.py:82
  1.7 7.3 %all-to-all-start = ((bf16[8,8,2944]{2,1,0:T(8,128)(2,1)}), bf16[8,8,2944]{2,1,0:T(8,128)(2,1)S(1)}, u32[]{:S(2)}, u32[]{:S(2)}) async-start(bf16[8,8,2944]{2,1,0:T(8,128)(2,1)} %pack.1), calls=%async_computation | async-start | bytes 753664 | tf_op jit(solution)/shard_map/all_to_all | solution.py:423
  9.0 0.0 copy-done
  9.0 0.0 copy-start.3
  9.0 0.0 copy-start.1
  9.0 1.0 %fusion = (bf16[1280,196]{0,1:T(8,128)(2,1)}, bf16[1280,196]{0,1:T(8,128)(2,1)}) fusion(bf16[2560,196]{0,1:T(8,128)(2,1)S(1)} %copy-done), kind=kLoop, calls=%fused_computation.1 | loop fusion | bytes 2007040 | tf_op jit(solution)/shard_map/slice | solution.py:417
  10.1 0.0 collective-permute-start
  10.1 0.0 copy-start.4
  10.1 0.5 %collective-permute-start.1 = (bf16[1280,196]{0,1:T(8,128)(2,1)}, bf16[1280,196]{0,1:T(8,128)(2,1)S(1)}, u32[]{:S(2)}, u32[]{:S(2)}) collective-permute-start(bf16[1280,196]{0,1:T(8,128)(2,1)} %get-tuple-element.23), channel_id=1, source_target_pairs={{0,1},{1,0},{2,3},{3,2},{4,5},{5,4},{6,7},{7,6},{8,9},{9,8},{10,11... | collective-permute-start | bytes 1505288 | tf_op jit(solution)/shard_map/ppermute | solution.py:417
  10.6 0.0 copy-done.3
  10.6 0.0 copy-start.2
  10.6 0.0 copy-start.5
  10.6 0.1 collective-permute-start.2
  10.7 0.1 copy-done.4
  10.8 0.1 reshape.32.gain_ref
  10.8 0.5 %copy-done.5 = f32[1280]{0:T(1024)S(1)} copy-done((f32[1280]{0:T(1024)S(1)}, f32[1280]{0:T(1024)}, u32[]{:S(2)}) %copy-start.5) | copy-done | bytes 5144
  11.3 0.8 %collective-permute-done.2.other_mask_ref = bf16[96,196]{1,0:T(8,128)(2,1)S(1)} collective-permute-done((bf16[96,196]{1,0:T(8,128)(2,1)S(1)}, bf16[96,196]{1,0:T(8,128)(2,1)S(1)}, u32[]{:S(2)}, u32[]{:S(2)}) %collective-permute-start.2) | collective-permute-done | bytes 37664 | tf_op jit(solution)/shard_map/ppermute | solution.py:422
  12.1 0.1 collective-permute-done
  12.2 0.8 %collective-permute-done.1 = bf16[1280,196]{0,1:T(8,128)(2,1)S(1)} collective-permute-done((bf16[1280,196]{0,1:T(8,128)(2,1)}, bf16[1280,196]{0,1:T(8,128)(2,1)S(1)}, u32[]{:S(2)}, u32[]{:S(2)}) %collective-permute-start.1) | collective-permute-done | bytes 501792 | tf_op jit(solution)/shard_map/ppermute | solution.py:417
  13.0 7.4 %all-to-all-done = bf16[8,8,2944]{2,1,0:T(8,128)(2,1)S(1)} async-done(((bf16[8,8,2944]{2,1,0:T(8,128)(2,1)}), bf16[8,8,2944]{2,1,0:T(8,128)(2,1)S(1)}, u32[]{:S(2)}, u32[]{:S(2)}) %all-to-all-start) | async-done | bytes 376864 | tf_op jit(solution)/shard_map/all_to_all | solution.py:423
  20.3 0.0 copy-done.1
  20.3 0.0 copy-done.2
  20.3 1.3 %mixer.1 = (f32[32,512]{1,0:T(8,128)S(1)}, f32[32,512]{1,0:T(8,128)S(1)}, f32[32,320]{1,0:T(8,128)S(1)}) custom-call(bf16[64,2944]{1,0:T(8,128)(2,1)S(1)} %bitcast.12, f32[1,1280]{1,0:T(1,128)S(1)} %reshape.34.refs_1_, bf16[320,1280]{1,0:T(8,128)(2,1)S(1)} %bitcast.13, bf16[64,320]{1,0:T(8,128)(2,1)S(1)} %copy-done.2), custom_call_target="tpu_custom_call" | custom-call | tf_op jit(solution)/shard_map/mixer/pallas_call | solution.py:182
  21.6 0.1 collective-permute-start.3
  21.7 1.2 %collective-permute-done.3.refs_1_ = f32[32,512]{1,0:T(8,128)S(1)} collective-permute-done((f32[32,512]{1,0:T(8,128)S(1)}, f32[32,512]{1,0:T(8,128)S(1)}, u32[]{:S(2)}, u32[]{:S(2)}) %collective-permute-start.3) | collective-permute-done | bytes 65568 | tf_op jit(solution)/shard_map/ppermute | solution.py:434
  22.9 0.2 hidden.1
  23.1 10.8 %all_to_all.15.h_ref = bf16[8,16,640]{2,1,0:T(8,128)(2,1)S(1)} all-to-all(bf16[8,16,640]{2,1,0:T(8,128)(2,1)S(1)} %hidden.1), channel_id=1, replica_groups={{0,2,4,6,9,11,13,15},{1,3,5,7,8,10,12,14},{16,18,20,22,25,27,29,31},{17..., dimensions={0} | all-to-all | bytes 327680 | tf_op jit(solution)/shard_map/all_to_all | solution.py:407
  33.9 1.1 %head.1 = f32[8,1,128]{2,1,0:T(1,128)S(1)} custom-call(bf16[8,16,640]{2,1,0:T(8,128)(2,1)S(1)} %all_to_all.15.h_ref, f32[8,320]{1,0:T(8,128)S(1)} %reshape.32.gain_ref, bf16[196,2560]{1,0:T(8,128)(2,1)S(1)} %bitcast.11, bf16[196,1280]{1,0:T(8,128)(2,1)S(1)} %bitcast.14, bf16[196,1280]{1,0:T(8,128)(2,1)S(1)} %bitcast.15, ...), custom_call_target="tpu_custom_call" | custom-call | tf_op jit(solution)/shard_map/head/pallas_call | solution.py:276
  35.0 8.8 %all_to_all.16.stats_ref = f32[8,1,128]{2,1,0:T(1,128)S(1)} all-to-all(f32[8,1,128]{2,1,0:T(1,128)S(1)} %head.1), channel_id=1, replica_groups={{0,2,4,6,9,11,13,15},{1,3,5,7,8,10,12,14},{16,18,20,22,25,27,29,31},{17..., dimensions={0} | all-to-all | bytes 8192 | tf_op jit(solution)/shard_map/all_to_all | solution.py:407
  43.8 0.6 %combine.1 = f32[1,4]{1,0:T(1,128)} custom-call(f32[8,1,128]{2,1,0:T(1,128)S(1)} %all_to_all.16.stats_ref), custom_call_target="tpu_custom_call" | custom-call | tf_op jit(solution)/shard_map/combine/pallas_call | solution.py:296
  (2 shorter events, 0.0 us)
Async XLA Ops:
  0.0 9.0 %copy-start = (bf16[2560,196]{0,1:T(8,128)(2,1)S(1)}, bf16[2560,196]{0,1:T(8,128)(2,1)}, u32[]{:S(2)}) copy-start(bf16[2560,196]{0,1:T(8,128)(2,1)} %param.28) | copy-start | bytes 3010564
  1.7 18.6 %all-to-all-start = ((bf16[8,8,2944]{2,1,0:T(8,128)(2,1)}), bf16[8,8,2944]{2,1,0:T(8,128)(2,1)S(1)}, u32[]{:S(2)}, u32[]{:S(2)}) async-start(bf16[8,8,2944]{2,1,0:T(8,128)(2,1)} %pack.1), calls=%async_computation | async-start | bytes 753664 | tf_op jit(solution)/shard_map/all_to_all | solution.py:423
  9.0 1.6 %copy-start.3 = (s32[96,196]{1,0:T(8,128)S(1)}, s32[96,196]{1,0:T(8,128)}, u32[]{:S(2)}) copy-start(s32[96,196]{1,0:T(8,128)} %param.29) | copy-start | bytes 225796
  9.0 11.3 %copy-start.1 = (bf16[1280,320]{0,1:T(8,128)(2,1)S(1)}, bf16[1280,320]{0,1:T(8,128)(2,1)}, u32[]{:S(2)}) copy-start(bf16[1280,320]{0,1:T(8,128)(2,1)} %param.25) | copy-start | bytes 2457604
  10.1 2.1 %collective-permute-start = (bf16[1280,196]{0,1:T(8,128)(2,1)}, bf16[1280,196]{0,1:T(8,128)(2,1)S(1)}, u32[]{:S(2)}, u32[]{:S(2)}) collective-permute-start(bf16[1280,196]{0,1:T(8,128)(2,1)} %get-tuple-element.24), channel_id=1, source_target_pairs={{0,1},{1,0},{2,3},{3,2},{4,5},{5,4},{6,7},{7,6},{8,9},{9,8},{10,11... | collective-permute-start | bytes 1505288 | tf_op jit(solution)/shard_map/ppermute | solution.py:417
  10.1 0.7 %copy-start.4 = (f32[2560]{0:T(1024)S(1)}, f32[2560]{0:T(1024)}, u32[]{:S(2)}) copy-start(f32[2560]{0:T(1024)} %param.27) | copy-start | bytes 30724
  10.1 2.9 %collective-permute-start.1 = (bf16[1280,196]{0,1:T(8,128)(2,1)}, bf16[1280,196]{0,1:T(8,128)(2,1)S(1)}, u32[]{:S(2)}, u32[]{:S(2)}) collective-permute-start(bf16[1280,196]{0,1:T(8,128)(2,1)} %get-tuple-element.23), channel_id=1, source_target_pairs={{0,1},{1,0},{2,3},{3,2},{4,5},{5,4},{6,7},{7,6},{8,9},{9,8},{10,11... | collective-permute-start | bytes 1505288 | tf_op jit(solution)/shard_map/ppermute | solution.py:417
  10.6 9.8 %copy-start.2 = (bf16[64,320]{1,0:T(8,128)(2,1)S(1)}, bf16[64,320]{1,0:T(8,128)(2,1)}, u32[]{:S(2)}) copy-start(bf16[64,320]{1,0:T(8,128)(2,1)} %refs_3_.1) | copy-start | bytes 122884
  10.6 0.7 %copy-start.5 = (f32[1280]{0:T(1024)S(1)}, f32[1280]{0:T(1024)}, u32[]{:S(2)}) copy-start(f32[1280]{0:T(1024)} %param.24) | copy-start | bytes 15364
  10.6 1.5 %collective-permute-start.2 = (bf16[96,196]{1,0:T(8,128)(2,1)S(1)}, bf16[96,196]{1,0:T(8,128)(2,1)S(1)}, u32[]{:S(2)}, u32[]{:S(2)}) collective-permute-start(bf16[96,196]{1,0:T(8,128)(2,1)S(1)} %compare_convert_fusion.own_mask_ref), channel_id=1, source_target_pairs={{0,1},{1,0},{2,3},{3,2},{4,5},{5,4},{6,7},{7,6},{8,9},{9,8},{10,11... | collective-permute-start | bytes 112904 | tf_op jit(solution)/shard_map/ppermute | solution.py:422
  21.6 1.3 %collective-permute-start.3 = (f32[32,512]{1,0:T(8,128)S(1)}, f32[32,512]{1,0:T(8,128)S(1)}, u32[]{:S(2)}, u32[]{:S(2)}) collective-permute-start(f32[32,512]{1,0:T(8,128)S(1)} %get-tuple-element.16), channel_id=1, source_target_pairs={{0,1},{1,0},{2,3},{3,2},{4,5},{5,4},{6,7},{7,6},{8,9},{9,8},{10,11... | collective-permute-start | bytes 196616 | tf_op jit(solution)/shard_map/ppermute | solution.py:434

commit v10 on v9

--- a/solution.py
+++ b/solution.py
@@ -89,9 +89,42 @@
     )
 
 
+def row_order(rows, seq_rows, half, mine):
+    r64 = lax.broadcasted_iota(jnp.int32, (rows, rows), 0)
+    c64 = lax.broadcasted_iota(jnp.int32, (rows, rows), 1)
+    own = seq_rows // 2
+    side = (r64 >= half).astype(jnp.int32)
+    place = r64 - side * half
+    seq = lax.shift_right_logical(place, own.bit_length() - 1)
+    which = (mine + side + lax.shift_right_logical(seq, 2)) & 1
+    source = place + seq * own + which * own
+    return r64, c64, source
+
+
+def keep_kernel(seq_rows, residual_ref, kept_ref):
+    mine = lax.axis_index("vocab") + turn(lax.axis_index("seq"))
+    rows, half = residual_ref.shape[0], kept_ref.shape[0]
+    _, c64, source = row_order(rows, seq_rows, half, mine)
+    order = (c64 == source).astype(BF16)
+    kept_ref[...] = jnp.dot(order[0:half], residual_ref[...], preferred_element_type=F32)
+
+
+def keep(seq_rows, residual):
+    rows, width = residual.shape
+
+    def kernel(*refs):
+        keep_kernel(seq_rows, *refs)
+
+    return pl.pallas_call(
+        kernel,
+        out_shape=jax.ShapeDtypeStruct((rows // 2, width), F32),
+        compiler_params=grant(2),
+        name="keep",
+    )(residual)
+
+
 def mixer_kernel(
-    seq_rows, heads, x_ref, gain_ref, weight_ref, residual_ref,
-    mine_ref, theirs_ref, kept_ref,
+    seq_rows, heads, x_ref, gain_ref, weight_ref, mine_ref, theirs_ref,
 ):
     mine = lax.axis_index("vocab") + turn(lax.axis_index("seq"))
     rows = x_ref.shape[0]
@@ -100,14 +133,7 @@
     edge = 2 * channels
     half = rows // 2
     size = channels // heads
-    r64 = lax.broadcasted_iota(jnp.int32, (rows, rows), 0)
-    c64 = lax.broadcasted_iota(jnp.int32, (rows, rows), 1)
-    own = seq_rows // 2
-    side = (r64 >= half).astype(jnp.int32)
-    place = r64 - side * half
-    seq = lax.shift_right_logical(place, own.bit_length() - 1)
-    which = (mine + side + lax.shift_right_logical(seq, 2)) & 1
-    source = place + seq * own + which * own
+    r64, c64, source = row_order(rows, seq_rows, half, mine)
     order = (c64 == source).astype(BF16)
     causal = c64 <= source
     moved = jnp.dot(order, x_ref[...], preferred_element_type=F32)
@@ -154,8 +180,6 @@
     partial = times_transposed(jnp.concatenate([high, low], axis=0), weight_ref[...])
     partial = partial[0:rows] + partial[rows:]
     total = jnp.sum(gated * gated, axis=1, keepdims=True)
-    kept_ref[...] = jnp.dot(order[0:half], residual_ref[...], preferred_element_type=F32)
-
     lane = lax.broadcasted_iota(jnp.int32, (rows, LANES), 1)
     info = pltpu.roll(moved[:, edge + 2 * state :], LANES + 1 - INFO, 1)
     info = jnp.where(lane == 0, total, info)
@@ -167,7 +191,7 @@
     theirs_ref[:, start:] = info[half:]
 
 
-def mixer(x, seq_rows, heads, gain, weight, residual):
+def mixer(x, seq_rows, heads, gain, weight):
     rows = x.shape[0]
     channels = gain.shape[1]
     width = weight.shape[1]
@@ -181,11 +205,11 @@
 
     return pl.pallas_call(
         kernel,
-        out_shape=(sums, sums, jax.ShapeDtypeStruct((half, width), F32)),
-        in_specs=[whole] * 4,
+        out_shape=(sums, sums),
+        in_specs=[whole] * 3,
         compiler_params=grant(8),
         name="mixer",
-    )(x, gain, weight.T, residual)
+    )(x, gain, weight.T)
 
 
 def hidden_kernel(features, mine_ref, theirs_ref, kept_ref, out_ref):
@@ -424,13 +448,16 @@
     final_gain = final_gain.reshape(count, features // count)
     norm_gain = norm_gain.reshape(1, channels)
     if small:
-        gathered, other_weight, mask_table, other_mask, final_gain = lax.optimization_barrier(
-            (gathered, other_weight, mask_table, other_mask, final_gain)
+        kept = keep(rows, residual)
+        gathered, other_weight, mask_table, other_mask, final_gain, kept = lax.optimization_barrier(
+            (gathered, other_weight, mask_table, other_mask, final_gain, kept)
         )
     x = gathered.reshape(count * rows, packed.shape[2])
-    mine, theirs, kept = (mixer if small else wide_mixer)(
-        x, rows, step_bias.shape[0], norm_gain, out_weight, residual
-    )
+    heads = step_bias.shape[0]
+    if small:
+        mine, theirs = mixer(x, rows, heads, norm_gain, out_weight)
+    else:
+        mine, theirs, kept = wide_mixer(x, rows, heads, norm_gain, out_weight, residual)
     arrived = lax.ppermute(theirs, "vocab", swap)
     if small:
         spread = hidden_rows(count, features, mine, arrived, kept)

time: 44.7 us -> 44.8 us (level)
  waiting for transfers between devices: 10.3 us -> 9.56 us
  local copies, waits for them, and re-layouts: 1.69 us -> 2.26 us
    ppermute x1, waiting for transfers between devices: 0.79 us -> 0.08 us  [shards(): other_mask = lax.ppermute(mask_table, 'vocab', swap)]
    unnamed x12, local copies, waits for them, and re-layouts: 0.56 us -> 1.13 us
    pallas_call x1 -> x2, Pallas kernels: 1.27 us -> 1.41 us  [the longest x1 1.27 us: mixer(): pl.pallas_call(kernel, out_shape=(sums, sums), in_specs=[whole] * 3, comp...]
where the time goes in v10:
time: 44.8 us; the launch traced here: 44.4 us
  blocking collectives  19.6 us (44%)
  waiting for transfers between devices  9.56 us (21%)
  starting transfers between devices  7.9 us (18%)
  Pallas kernels  4.95 us (11%)
  local copies, waits for them, and re-layouts  2.26 us (5%)
    all_to_all x2, blocking collectives, exchange(): return lax.all_to_all(a, both, 0, 0, tiled=True, axis_index_groups=groups)  19.6 us
    all_to_all x1, waiting for transfers between devices, shards(): gathered = lax.all_to_all(packed, 'seq', 0, 0, tiled=True)  7.37 us
    all_to_all x1, starting transfers between devices, shards(): gathered = lax.all_to_all(packed, 'seq', 0, 0, tiled=True)  7.25 us
    pallas_call x1, Pallas kernels, pack(): pl.pallas_call(pack_kernel, out_shape=jax.ShapeDtypeStruct((count, rows,...  1.73 us
    pallas_call x1, Pallas kernels, mixer(): pl.pallas_call(kernel, out_shape=(sums, sums), in_specs=[whole] * 3, comp...  1.27 us
    ppermute x1, waiting for transfers between devices, shards(): arrived = lax.ppermute(theirs, 'vocab', swap)  1.24 us
    unnamed x12, local copies, waits for them, and re-layouts  1.13 us
    pallas_call x1, Pallas kernels, head(): pl.pallas_call(head_kernel, out_shape=jax.ShapeDtypeStruct((count, 1, LAN...  1.06 us
  transfers between devices with their start and end apart: 5, of which 5 were waited for; matrix products, arithmetic and copies ran while one was open for 3% of the time, Pallas kernels for 0%

profile of v10, /device:TPU:0, one launch (start us, length us, event | category | flops | bytes accessed | tf_op | source)
XLA Modules:
  0.0 44.4 jit_solution(6475067871826758623)
XLA Ops:
  0.0 0.0 copy-start
  0.0 1.7 %pack.1 = bf16[8,8,2944]{2,1,0:T(8,128)(2,1)} custom-call(bf16[8,1280]{1,0:T(8,128)(2,1)} %ssm_ref.1, bf16[8,1280]{1,0:T(8,128)(2,1)} %gate_ref.1, bf16[8,128]{1,0:T(8,128)(2,1)} %b_ref.1, bf16[8,128]{1,0:T(8,128)(2,1)} %c_ref.1, f32[8,20]{1,0:T(8,128)} %raw_ref.1, f32[1,20]{1,0:T(1,128)} %bitcast.16, f32[1,20]{1,0:T(1,128)} %bitcast.17, f32[1,20]{1,0:T(1,128)} %bitcast.18, ...), custom_call_target="tpu_custom_call" | custom-call | tf_op jit(solution)/shard_map/pack/pallas_call | solution.py:82
  1.7 7.3 %all-to-all-start = ((bf16[8,8,2944]{2,1,0:T(8,128)(2,1)}), bf16[8,8,2944]{2,1,0:T(8,128)(2,1)S(1)}, u32[]{:S(2)}, u32[]{:S(2)}) async-start(bf16[8,8,2944]{2,1,0:T(8,128)(2,1)} %pack.1), calls=%async_computation | async-start | bytes 753664 | tf_op jit(solution)/shard_map/all_to_all | solution.py:447
  9.0 0.0 copy-done
  9.0 0.0 copy-start.3
  9.0 0.0 copy-start.1
  9.0 1.0 %fusion = (bf16[1280,196]{0,1:T(8,128)(2,1)}, bf16[1280,196]{0,1:T(8,128)(2,1)}) fusion(bf16[2560,196]{0,1:T(8,128)(2,1)S(1)} %copy-done), kind=kLoop, calls=%fused_computation.1 | loop fusion | bytes 2007040 | tf_op jit(solution)/shard_map/slice | solution.py:441
  10.1 0.0 collective-permute-start
  10.1 0.0 copy-start.2
  10.1 0.5 %collective-permute-start.1 = (bf16[1280,196]{0,1:T(8,128)(2,1)}, bf16[1280,196]{0,1:T(8,128)(2,1)S(1)}, u32[]{:S(2)}, u32[]{:S(2)}) collective-permute-start(bf16[1280,196]{0,1:T(8,128)(2,1)} %get-tuple-element.23), channel_id=1, source_target_pairs={{0,1},{1,0},{2,3},{3,2},{4,5},{5,4},{6,7},{7,6},{8,9},{9,8},{10,11... | collective-permute-start | bytes 1505288 | tf_op jit(solution)/shard_map/ppermute | solution.py:441
  10.6 0.0 copy-done.3
  10.6 0.0 copy-start.4
  10.6 0.1 collective-permute-start.2
  10.7 0.2 copy-done.2
  10.9 0.1 keep.1.refs_2_
  11.0 0.3 copy-done.4
  11.3 0.0 copy-start.5
  11.3 0.1 reshape.32.gain_ref
  11.4 0.6 %copy-done.5 = f32[1280]{0:T(1024)S(1)} copy-done((f32[1280]{0:T(1024)S(1)}, f32[1280]{0:T(1024)}, u32[]{:S(2)}) %copy-start.5) | copy-done | bytes 5144
  12.0 0.1 collective-permute-done.2.other_mask_ref
  12.1 0.1 collective-permute-done
  12.2 0.8 %collective-permute-done.1 = bf16[1280,196]{0,1:T(8,128)(2,1)S(1)} collective-permute-done((bf16[1280,196]{0,1:T(8,128)(2,1)}, bf16[1280,196]{0,1:T(8,128)(2,1)S(1)}, u32[]{:S(2)}, u32[]{:S(2)}) %collective-permute-start.1) | collective-permute-done | bytes 501792 | tf_op jit(solution)/shard_map/ppermute | solution.py:441
  13.0 7.4 %all-to-all-done = bf16[8,8,2944]{2,1,0:T(8,128)(2,1)S(1)} async-done(((bf16[8,8,2944]{2,1,0:T(8,128)(2,1)}), bf16[8,8,2944]{2,1,0:T(8,128)(2,1)S(1)}, u32[]{:S(2)}, u32[]{:S(2)}) %all-to-all-start) | async-done | bytes 376864 | tf_op jit(solution)/shard_map/all_to_all | solution.py:447
  20.3 0.0 copy-done.1
  20.3 1.3 %mixer.1 = (f32[32,512]{1,0:T(8,128)S(1)}, f32[32,512]{1,0:T(8,128)S(1)}) custom-call(bf16[64,2944]{1,0:T(8,128)(2,1)S(1)} %bitcast.12, f32[1,1280]{1,0:T(1,128)S(1)} %reshape.34.refs_1_, bf16[320,1280]{1,0:T(8,128)(2,1)S(1)} %bitcast.13), custom_call_target="tpu_custom_call" | custom-call | tf_op jit(solution)/shard_map/mixer/pallas_call | solution.py:206
  21.6 0.1 collective-permute-start.3
  21.7 1.2 %collective-permute-done.3.refs_1_ = f32[32,512]{1,0:T(8,128)S(1)} collective-permute-done((f32[32,512]{1,0:T(8,128)S(1)}, f32[32,512]{1,0:T(8,128)S(1)}, u32[]{:S(2)}, u32[]{:S(2)}) %collective-permute-start.3) | collective-permute-done | bytes 65568 | tf_op jit(solution)/shard_map/ppermute | solution.py:461
  22.9 0.2 hidden.1
  23.1 10.8 %all_to_all.15.h_ref = bf16[8,16,640]{2,1,0:T(8,128)(2,1)S(1)} all-to-all(bf16[8,16,640]{2,1,0:T(8,128)(2,1)S(1)} %hidden.1), channel_id=1, replica_groups={{0,2,4,6,9,11,13,15},{1,3,5,7,8,10,12,14},{16,18,20,22,25,27,29,31},{17..., dimensions={0} | all-to-all | bytes 327680 | tf_op jit(solution)/shard_map/all_to_all | solution.py:431
  33.9 1.1 %head.1 = f32[8,1,128]{2,1,0:T(1,128)S(1)} custom-call(bf16[8,16,640]{2,1,0:T(8,128)(2,1)S(1)} %all_to_all.15.h_ref, f32[8,320]{1,0:T(8,128)S(1)} %reshape.32.gain_ref, bf16[196,2560]{1,0:T(8,128)(2,1)S(1)} %bitcast.11, bf16[196,1280]{1,0:T(8,128)(2,1)S(1)} %bitcast.14, bf16[196,1280]{1,0:T(8,128)(2,1)S(1)} %bitcast.15, ...), custom_call_target="tpu_custom_call" | custom-call | tf_op jit(solution)/shard_map/head/pallas_call | solution.py:300
  35.0 8.8 %all_to_all.16.stats_ref = f32[8,1,128]{2,1,0:T(1,128)S(1)} all-to-all(f32[8,1,128]{2,1,0:T(1,128)S(1)} %head.1), channel_id=1, replica_groups={{0,2,4,6,9,11,13,15},{1,3,5,7,8,10,12,14},{16,18,20,22,25,27,29,31},{17..., dimensions={0} | all-to-all | bytes 8192 | tf_op jit(solution)/shard_map/all_to_all | solution.py:431
  43.8 0.6 %combine.1 = f32[1,4]{1,0:T(1,128)} custom-call(f32[8,1,128]{2,1,0:T(1,128)S(1)} %all_to_all.16.stats_ref), custom_call_target="tpu_custom_call" | custom-call | tf_op jit(solution)/shard_map/combine/pallas_call | solution.py:320
  (2 shorter events, 0.0 us)
Async XLA Ops:
  0.0 9.0 %copy-start = (bf16[2560,196]{0,1:T(8,128)(2,1)S(1)}, bf16[2560,196]{0,1:T(8,128)(2,1)}, u32[]{:S(2)}) copy-start(bf16[2560,196]{0,1:T(8,128)(2,1)} %param.28) | copy-start | bytes 3010564
  1.7 18.6 %all-to-all-start = ((bf16[8,8,2944]{2,1,0:T(8,128)(2,1)}), bf16[8,8,2944]{2,1,0:T(8,128)(2,1)S(1)}, u32[]{:S(2)}, u32[]{:S(2)}) async-start(bf16[8,8,2944]{2,1,0:T(8,128)(2,1)} %pack.1), calls=%async_computation | async-start | bytes 753664 | tf_op jit(solution)/shard_map/all_to_all | solution.py:447
  9.0 1.6 %copy-start.3 = (s32[96,196]{1,0:T(8,128)S(1)}, s32[96,196]{1,0:T(8,128)}, u32[]{:S(2)}) copy-start(s32[96,196]{1,0:T(8,128)} %param.29) | copy-start | bytes 225796
  9.0 11.3 %copy-start.1 = (bf16[1280,320]{0,1:T(8,128)(2,1)S(1)}, bf16[1280,320]{0,1:T(8,128)(2,1)}, u32[]{:S(2)}) copy-start(bf16[1280,320]{0,1:T(8,128)(2,1)} %param.25) | copy-start | bytes 2457604
  10.1 2.1 %collective-permute-start = (bf16[1280,196]{0,1:T(8,128)(2,1)}, bf16[1280,196]{0,1:T(8,128)(2,1)S(1)}, u32[]{:S(2)}, u32[]{:S(2)}) collective-permute-start(bf16[1280,196]{0,1:T(8,128)(2,1)} %get-tuple-element.24), channel_id=1, source_target_pairs={{0,1},{1,0},{2,3},{3,2},{4,5},{5,4},{6,7},{7,6},{8,9},{9,8},{10,11... | collective-permute-start | bytes 1505288 | tf_op jit(solution)/shard_map/ppermute | solution.py:441
  10.1 0.8 %copy-start.2 = (bf16[64,320]{1,0:T(8,128)(2,1)S(1)}, bf16[64,320]{1,0:T(8,128)(2,1)}, u32[]{:S(2)}) copy-start(bf16[64,320]{1,0:T(8,128)(2,1)} %refs_0_.1) | copy-start | bytes 122884
  10.1 2.9 %collective-permute-start.1 = (bf16[1280,196]{0,1:T(8,128)(2,1)}, bf16[1280,196]{0,1:T(8,128)(2,1)S(1)}, u32[]{:S(2)}, u32[]{:S(2)}) collective-permute-start(bf16[1280,196]{0,1:T(8,128)(2,1)} %get-tuple-element.23), channel_id=1, source_target_pairs={{0,1},{1,0},{2,3},{3,2},{4,5},{5,4},{6,7},{7,6},{8,9},{9,8},{10,11... | collective-permute-start | bytes 1505288 | tf_op jit(solution)/shard_map/ppermute | solution.py:441
  10.6 0.7 %copy-start.4 = (f32[2560]{0:T(1024)S(1)}, f32[2560]{0:T(1024)}, u32[]{:S(2)}) copy-start(f32[2560]{0:T(1024)} %param.27) | copy-start | bytes 30724
  10.6 1.5 %collective-permute-start.2 = (bf16[96,196]{1,0:T(8,128)(2,1)S(1)}, bf16[96,196]{1,0:T(8,128)(2,1)S(1)}, u32[]{:S(2)}, u32[]{:S(2)}) collective-permute-start(bf16[96,196]{1,0:T(8,128)(2,1)S(1)} %compare_convert_fusion.own_mask_ref), channel_id=1, source_target_pairs={{0,1},{1,0},{2,3},{3,2},{4,5},{5,4},{6,7},{7,6},{8,9},{9,8},{10,11... | collective-permute-start | bytes 112904 | tf_op jit(solution)/shard_map/ppermute | solution.py:446
  11.3 0.7 %copy-start.5 = (f32[1280]{0:T(1024)S(1)}, f32[1280]{0:T(1024)}, u32[]{:S(2)}) copy-start(f32[1280]{0:T(1024)} %param.24) | copy-start | bytes 15364
  21.6 1.3 %collective-permute-start.3 = (f32[32,512]{1,0:T(8,128)S(1)}, f32[32,512]{1,0:T(8,128)S(1)}, u32[]{:S(2)}, u32[]{:S(2)}) collective-permute-start(f32[32,512]{1,0:T(8,128)S(1)} %get-tuple-element.16), channel_id=1, source_target_pairs={{0,1},{1,0},{2,3},{3,2},{4,5},{5,4},{6,7},{7,6},{8,9},{9,8},{10,11... | collective-permute-start | bytes 196616 | tf_op jit(solution)/shard_map/ppermute | solution.py:461

commit v11 on v10

--- a/solution.py
+++ b/solution.py
@@ -26,7 +26,7 @@
 
 
 def turn(seq):
-    return seq // 4
+    return seq % 2
 
 
 def circles(count):
@@ -96,7 +96,7 @@
     side = (r64 >= half).astype(jnp.int32)
     place = r64 - side * half
     seq = lax.shift_right_logical(place, own.bit_length() - 1)
-    which = (mine + side + lax.shift_right_logical(seq, 2)) & 1
+    which = (mine + side + seq) & 1
     source = place + seq * own + which * own
     return r64, c64, source
 

time: 44.8 us -> 44.9 us (level)
  no operation moved by 1% of the time
where the time goes in v11:
time: 44.9 us; the launch traced here: 44.5 us
  blocking collectives  19.7 us (44%)
  waiting for transfers between devices  9.56 us (21%)
  starting transfers between devices  7.9 us (18%)
  Pallas kernels  4.95 us (11%)
  local copies, waits for them, and re-layouts  2.26 us (5%)
    all_to_all x2, blocking collectives, exchange(): return lax.all_to_all(a, both, 0, 0, tiled=True, axis_index_groups=groups)  19.7 us
    all_to_all x1, waiting for transfers between devices, shards(): gathered = lax.all_to_all(packed, 'seq', 0, 0, tiled=True)  7.37 us
    all_to_all x1, starting transfers between devices, shards(): gathered = lax.all_to_all(packed, 'seq', 0, 0, tiled=True)  7.25 us
    pallas_call x1, Pallas kernels, pack(): pl.pallas_call(pack_kernel, out_shape=jax.ShapeDtypeStruct((count, rows,...  1.73 us
    pallas_call x1, Pallas kernels, mixer(): pl.pallas_call(kernel, out_shape=(sums, sums), in_specs=[whole] * 3, comp...  1.27 us
    ppermute x1, waiting for transfers between devices, shards(): arrived = lax.ppermute(theirs, 'vocab', swap)  1.24 us
    unnamed x12, local copies, waits for them, and re-layouts  1.14 us
    pallas_call x1, Pallas kernels, head(): pl.pallas_call(head_kernel, out_shape=jax.ShapeDtypeStruct((count, 1, LAN...  1.06 us
  transfers between devices with their start and end apart: 5, of which 5 were waited for; matrix products, arithmetic and copies ran while one was open for 3% of the time, Pallas kernels for 0%

profile of v11, /device:TPU:0, one launch (start us, length us, event | category | flops | bytes accessed | tf_op | source)
XLA Modules:
  0.0 44.5 jit_solution(132268225642006698)
XLA Ops:
  0.0 0.0 copy-start
  0.0 1.7 %pack.1 = bf16[8,8,2944]{2,1,0:T(8,128)(2,1)} custom-call(bf16[8,1280]{1,0:T(8,128)(2,1)} %ssm_ref.1, bf16[8,1280]{1,0:T(8,128)(2,1)} %gate_ref.1, bf16[8,128]{1,0:T(8,128)(2,1)} %b_ref.1, bf16[8,128]{1,0:T(8,128)(2,1)} %c_ref.1, f32[8,20]{1,0:T(8,128)} %raw_ref.1, f32[1,20]{1,0:T(1,128)} %bitcast.16, f32[1,20]{1,0:T(1,128)} %bitcast.17, f32[1,20]{1,0:T(1,128)} %bitcast.18, ...), custom_call_target="tpu_custom_call" | custom-call | tf_op jit(solution)/shard_map/pack/pallas_call | solution.py:82
  1.7 7.3 %all-to-all-start = ((bf16[8,8,2944]{2,1,0:T(8,128)(2,1)}), bf16[8,8,2944]{2,1,0:T(8,128)(2,1)S(1)}, u32[]{:S(2)}, u32[]{:S(2)}) async-start(bf16[8,8,2944]{2,1,0:T(8,128)(2,1)} %pack.1), calls=%async_computation | async-start | bytes 753664 | tf_op jit(solution)/shard_map/all_to_all | solution.py:447
  9.0 0.0 copy-done
  9.0 0.0 copy-start.3
  9.0 0.0 copy-start.1
  9.0 1.0 %fusion = (bf16[1280,196]{0,1:T(8,128)(2,1)}, bf16[1280,196]{0,1:T(8,128)(2,1)}) fusion(bf16[2560,196]{0,1:T(8,128)(2,1)S(1)} %copy-done), kind=kLoop, calls=%fused_computation.1 | loop fusion | bytes 2007040 | tf_op jit(solution)/shard_map/slice | solution.py:441
  10.1 0.0 collective-permute-start
  10.1 0.0 copy-start.2
  10.1 0.5 %collective-permute-start.1 = (bf16[1280,196]{0,1:T(8,128)(2,1)}, bf16[1280,196]{0,1:T(8,128)(2,1)S(1)}, u32[]{:S(2)}, u32[]{:S(2)}) collective-permute-start(bf16[1280,196]{0,1:T(8,128)(2,1)} %get-tuple-element.23), channel_id=1, source_target_pairs={{0,1},{1,0},{2,3},{3,2},{4,5},{5,4},{6,7},{7,6},{8,9},{9,8},{10,11... | collective-permute-start | bytes 1505288 | tf_op jit(solution)/shard_map/ppermute | solution.py:441
  10.6 0.0 copy-done.3
  10.6 0.0 copy-start.4
  10.6 0.1 collective-permute-start.2
  10.7 0.2 copy-done.2
  10.9 0.1 keep.1.refs_2_
  11.0 0.3 copy-done.4
  11.3 0.0 copy-start.5
  11.3 0.1 reshape.32.gain_ref
  11.4 0.6 %copy-done.5 = f32[1280]{0:T(1024)S(1)} copy-done((f32[1280]{0:T(1024)S(1)}, f32[1280]{0:T(1024)}, u32[]{:S(2)}) %copy-start.5) | copy-done | bytes 5144
  12.0 0.1 collective-permute-done.2.other_mask_ref
  12.1 0.1 collective-permute-done
  12.2 0.8 %collective-permute-done.1 = bf16[1280,196]{0,1:T(8,128)(2,1)S(1)} collective-permute-done((bf16[1280,196]{0,1:T(8,128)(2,1)}, bf16[1280,196]{0,1:T(8,128)(2,1)S(1)}, u32[]{:S(2)}, u32[]{:S(2)}) %collective-permute-start.1) | collective-permute-done | bytes 501792 | tf_op jit(solution)/shard_map/ppermute | solution.py:441
  13.0 7.4 %all-to-all-done = bf16[8,8,2944]{2,1,0:T(8,128)(2,1)S(1)} async-done(((bf16[8,8,2944]{2,1,0:T(8,128)(2,1)}), bf16[8,8,2944]{2,1,0:T(8,128)(2,1)S(1)}, u32[]{:S(2)}, u32[]{:S(2)}) %all-to-all-start) | async-done | bytes 376864 | tf_op jit(solution)/shard_map/all_to_all | solution.py:447
  20.3 0.0 copy-done.1
  20.3 1.3 %mixer.1 = (f32[32,512]{1,0:T(8,128)S(1)}, f32[32,512]{1,0:T(8,128)S(1)}) custom-call(bf16[64,2944]{1,0:T(8,128)(2,1)S(1)} %bitcast.12, f32[1,1280]{1,0:T(1,128)S(1)} %reshape.34.refs_1_, bf16[320,1280]{1,0:T(8,128)(2,1)S(1)} %bitcast.13), custom_call_target="tpu_custom_call" | custom-call | tf_op jit(solution)/shard_map/mixer/pallas_call | solution.py:206
  21.6 0.1 collective-permute-start.3
  21.7 1.2 %collective-permute-done.3.refs_1_ = f32[32,512]{1,0:T(8,128)S(1)} collective-permute-done((f32[32,512]{1,0:T(8,128)S(1)}, f32[32,512]{1,0:T(8,128)S(1)}, u32[]{:S(2)}, u32[]{:S(2)}) %collective-permute-start.3) | collective-permute-done | bytes 65568 | tf_op jit(solution)/shard_map/ppermute | solution.py:461
  22.9 0.2 hidden.1
  23.1 10.8 %all_to_all.15.h_ref = bf16[8,16,640]{2,1,0:T(8,128)(2,1)S(1)} all-to-all(bf16[8,16,640]{2,1,0:T(8,128)(2,1)S(1)} %hidden.1), channel_id=1, replica_groups={{0,3,4,7,8,11,12,15},{1,2,5,6,9,10,13,14},{16,19,20,23,24,27,28,31},{17..., dimensions={0} | all-to-all | bytes 327680 | tf_op jit(solution)/shard_map/all_to_all | solution.py:431
  33.9 1.1 %head.1 = f32[8,1,128]{2,1,0:T(1,128)S(1)} custom-call(bf16[8,16,640]{2,1,0:T(8,128)(2,1)S(1)} %all_to_all.15.h_ref, f32[8,320]{1,0:T(8,128)S(1)} %reshape.32.gain_ref, bf16[196,2560]{1,0:T(8,128)(2,1)S(1)} %bitcast.11, bf16[196,1280]{1,0:T(8,128)(2,1)S(1)} %bitcast.14, bf16[196,1280]{1,0:T(8,128)(2,1)S(1)} %bitcast.15, ...), custom_call_target="tpu_custom_call" | custom-call | tf_op jit(solution)/shard_map/head/pallas_call | solution.py:300
  35.0 8.9 %all_to_all.16.stats_ref = f32[8,1,128]{2,1,0:T(1,128)S(1)} all-to-all(f32[8,1,128]{2,1,0:T(1,128)S(1)} %head.1), channel_id=1, replica_groups={{0,3,4,7,8,11,12,15},{1,2,5,6,9,10,13,14},{16,19,20,23,24,27,28,31},{17..., dimensions={0} | all-to-all | bytes 8192 | tf_op jit(solution)/shard_map/all_to_all | solution.py:431
  43.9 0.6 %combine.1 = f32[1,4]{1,0:T(1,128)} custom-call(f32[8,1,128]{2,1,0:T(1,128)S(1)} %all_to_all.16.stats_ref), custom_call_target="tpu_custom_call" | custom-call | tf_op jit(solution)/shard_map/combine/pallas_call | solution.py:320
  (2 shorter events, 0.0 us)
Async XLA Ops:
  0.0 9.0 %copy-start = (bf16[2560,196]{0,1:T(8,128)(2,1)S(1)}, bf16[2560,196]{0,1:T(8,128)(2,1)}, u32[]{:S(2)}) copy-start(bf16[2560,196]{0,1:T(8,128)(2,1)} %param.28) | copy-start | bytes 3010564
  1.7 18.6 %all-to-all-start = ((bf16[8,8,2944]{2,1,0:T(8,128)(2,1)}), bf16[8,8,2944]{2,1,0:T(8,128)(2,1)S(1)}, u32[]{:S(2)}, u32[]{:S(2)}) async-start(bf16[8,8,2944]{2,1,0:T(8,128)(2,1)} %pack.1), calls=%async_computation | async-start | bytes 753664 | tf_op jit(solution)/shard_map/all_to_all | solution.py:447
  9.0 1.6 %copy-start.3 = (s32[96,196]{1,0:T(8,128)S(1)}, s32[96,196]{1,0:T(8,128)}, u32[]{:S(2)}) copy-start(s32[96,196]{1,0:T(8,128)} %param.29) | copy-start | bytes 225796
  9.0 11.3 %copy-start.1 = (bf16[1280,320]{0,1:T(8,128)(2,1)S(1)}, bf16[1280,320]{0,1:T(8,128)(2,1)}, u32[]{:S(2)}) copy-start(bf16[1280,320]{0,1:T(8,128)(2,1)} %param.25) | copy-start | bytes 2457604
  10.1 2.1 %collective-permute-start = (bf16[1280,196]{0,1:T(8,128)(2,1)}, bf16[1280,196]{0,1:T(8,128)(2,1)S(1)}, u32[]{:S(2)}, u32[]{:S(2)}) collective-permute-start(bf16[1280,196]{0,1:T(8,128)(2,1)} %get-tuple-element.24), channel_id=1, source_target_pairs={{0,1},{1,0},{2,3},{3,2},{4,5},{5,4},{6,7},{7,6},{8,9},{9,8},{10,11... | collective-permute-start | bytes 1505288 | tf_op jit(solution)/shard_map/ppermute | solution.py:441
  10.1 0.8 %copy-start.2 = (bf16[64,320]{1,0:T(8,128)(2,1)S(1)}, bf16[64,320]{1,0:T(8,128)(2,1)}, u32[]{:S(2)}) copy-start(bf16[64,320]{1,0:T(8,128)(2,1)} %refs_0_.1) | copy-start | bytes 122884
  10.1 2.9 %collective-permute-start.1 = (bf16[1280,196]{0,1:T(8,128)(2,1)}, bf16[1280,196]{0,1:T(8,128)(2,1)S(1)}, u32[]{:S(2)}, u32[]{:S(2)}) collective-permute-start(bf16[1280,196]{0,1:T(8,128)(2,1)} %get-tuple-element.23), channel_id=1, source_target_pairs={{0,1},{1,0},{2,3},{3,2},{4,5},{5,4},{6,7},{7,6},{8,9},{9,8},{10,11... | collective-permute-start | bytes 1505288 | tf_op jit(solution)/shard_map/ppermute | solution.py:441
  10.6 0.7 %copy-start.4 = (f32[2560]{0:T(1024)S(1)}, f32[2560]{0:T(1024)}, u32[]{:S(2)}) copy-start(f32[2560]{0:T(1024)} %param.27) | copy-start | bytes 30724
  10.6 1.5 %collective-permute-start.2 = (bf16[96,196]{1,0:T(8,128)(2,1)S(1)}, bf16[96,196]{1,0:T(8,128)(2,1)S(1)}, u32[]{:S(2)}, u32[]{:S(2)}) collective-permute-start(bf16[96,196]{1,0:T(8,128)(2,1)S(1)} %compare_convert_fusion.own_mask_ref), channel_id=1, source_target_pairs={{0,1},{1,0},{2,3},{3,2},{4,5},{5,4},{6,7},{7,6},{8,9},{9,8},{10,11... | collective-permute-start | bytes 112904 | tf_op jit(solution)/shard_map/ppermute | solution.py:446
  11.3 0.7 %copy-start.5 = (f32[1280]{0:T(1024)S(1)}, f32[1280]{0:T(1024)}, u32[]{:S(2)}) copy-start(f32[1280]{0:T(1024)} %param.24) | copy-start | bytes 15364
  21.6 1.3 %collective-permute-start.3 = (f32[32,512]{1,0:T(8,128)S(1)}, f32[32,512]{1,0:T(8,128)S(1)}, u32[]{:S(2)}, u32[]{:S(2)}) collective-permute-start(f32[32,512]{1,0:T(8,128)S(1)} %get-tuple-element.16), channel_id=1, source_target_pairs={{0,1},{1,0},{2,3},{3,2},{4,5},{5,4},{6,7},{7,6},{8,9},{9,8},{10,11... | collective-permute-start | bytes 196616 | tf_op jit(solution)/shard_map/ppermute | solution.py:461
